TPU v7x, 32 devices: a whole 2x2x4 slice. The times are simulated.
32 devices in a mesh: dp: 8 (over z, x), tensor: 4 (over y, core).
Axes of the slice: x: 2, y: 2, z: 4, core: 2. Of those that a mesh axis runs over, the one named last changes fastest.
Arguments:
- inputs: float32 [32, 1024, 768], P(('dp', 'tensor')), may hold values from -6 to 6
- w_qkv: float32 [3, 768, 768], P(None, None, 'tensor'), may hold values from -0.21875 to 0.21875
- b_qv: float32 [2, 768], P(None, 'tensor'), may hold values from -3 to 3
- w_out: float32 [768, 768], P('tensor'), may hold values from -0.875 to 0.875
- w_in: float32 [768, 3072], P(None, 'tensor'), may hold values from -0.21875 to 0.21875
- b_in: float32 [3072], P('tensor'), may hold values from -3 to 3
- w_back: float32 [3072, 768], P('tensor'), may hold values from -0.109375 to 0.109375
- norm_gains: float32 [2, 768], replicated, may hold values from 0.5 to 1.5
- shifts: float32 [4, 768], replicated, may hold values from -2 to 2
- segment_ids: int32 [32, 1024], P('dp'), may hold values from 0 to 7, never falling along the last dimension, each value on 1 to 512 neighbouring positions
- valid_lengths: int32 [32], P('dp'), may hold values from 307 to 1024, as said below
- teacher: float32 [32, 1024, 768], P(('dp', 'tensor')), may hold values from -6 to 6
Outputs:
- output: float32 [32, 1024, 768], P(('dp', 'tensor'))
- loss: float32 [], replicated
- grad_inputs: float32 [32, 1024, 768], P(('dp', 'tensor'))
- grad_w_qkv: float32 [3, 768, 768], P(None, None, 'tensor')
- grad_b_qv: float32 [2, 768], P(None, 'tensor')
- grad_w_out: float32 [768, 768], P('tensor')
- grad_w_in: float32 [768, 3072], P(None, 'tensor')
- grad_b_in: float32 [3072], P('tensor')
- grad_w_back: float32 [3072, 768], P('tensor')
- grad_norm_gains: float32 [2, 768], replicated
- grad_shifts: float32 [4, 768], replicated
Inputs may be any that keep to these rules, and one draw needn't show every extreme that they name: `valid_lengths`: each sequence's slots at and after its valid length are padding; some sequence has all 1024 slots in use. `segment_ids`: along a sequence the document number never falls; a document holds 1 to 512 slots, one exactly that many.
All inputs are finite; a program needn't handle non-finite values.
Results may differ from a plain program's by a relative error of at most 0.0095.
The roundings to bfloat16 on the way count: a program that leaves them out, or rounds other values in their place, can miss the bound.
Values may be sent and summed in bfloat16 or wider, within the bound.
A program may use at most 320 MiB of HBM per device.

v0:
```python
import math

import jax
import jax.numpy as jnp
from jax import lax
from jax.sharding import PartitionSpec as P

HD = 64


LN_EPSILON = 1e-05
MASKED_SCORE = -1000000000.0


def layer_norm(values, gain, shift):
    centred = values - jnp.mean(values, axis=-1, keepdims=True)
    spread = jnp.mean(centred * centred, axis=-1, keepdims=True)
    return centred * lax.rsqrt(spread + LN_EPSILON) * gain + shift


def exact_gelu(values):
    return jax.nn.gelu(values, approximate=False)


def matmul_f32(left, right):
    return jnp.dot(left, right, preferred_element_type=jnp.float32)


def left_cross(left, right):
    return jnp.einsum("nd,ne->de", left, right, preferred_element_type=jnp.float32)


def right_cross(left, right):
    return jnp.einsum("ne,de->nd", left, right, preferred_element_type=jnp.float32)


def block_scores(queries, keys_all, segments, valid_len, block_start, block_size):
    positions = jnp.arange(segments.shape[0], dtype=jnp.int32)
    rows_here = positions[block_start : block_start + block_size]
    same_doc = segments[block_start : block_start + block_size, None] == segments[None, :]
    allowed = same_doc & (positions[None, :] < valid_len) | (
        rows_here[:, None] == positions[None, :]
    )
    scale = 1.0 / math.sqrt(queries.shape[-1])
    scores = (
        jnp.einsum(
            "qhd,khd->hqk",
            queries[block_start : block_start + block_size],
            keys_all,
            preferred_element_type=jnp.float32,
        )
        * scale
    )
    return jnp.where(allowed[None], scores, MASKED_SCORE)


def attend_forward(operands):
    queries, keys_all, values, segments, valid_len = operands
    seq_len = queries.shape[0]
    block_size = min(512, seq_len)
    contexts = []
    totals = []
    for block_start in range(0, seq_len, block_size):
        scores = block_scores(queries, keys_all, segments, valid_len, block_start, block_size)
        row_max = jnp.max(scores, axis=-1, keepdims=True)
        exp_scores = jnp.exp(scores - row_max)
        row_total = jnp.sum(exp_scores, axis=-1, keepdims=True)
        probs_low = (exp_scores / row_total).astype(jnp.bfloat16)
        contexts.append(
            jnp.einsum("hqk,khd->qhd", probs_low, values, preferred_element_type=jnp.float32)
        )
        totals.append((row_max + jnp.log(row_total))[:, :, 0])
    return (jnp.concatenate(contexts, axis=0), jnp.concatenate(totals, axis=1))


def attend_backward(operands):
    queries, keys_all, values, grad_ctx, log_total, segments, valid_len = operands
    seq_len = queries.shape[0]
    block_size = min(512, seq_len)
    scale = 1.0 / math.sqrt(queries.shape[-1])
    query_parts = []
    key_grad = jnp.zeros(keys_all.shape, jnp.float32)
    value_grad = jnp.zeros(values.shape, jnp.float32)
    for block_start in range(0, seq_len, block_size):
        scores = block_scores(queries, keys_all, segments, valid_len, block_start, block_size)
        probs = jnp.exp(scores - log_total[:, block_start : block_start + block_size, None])
        probs_low = probs.astype(jnp.bfloat16)
        grad_block = grad_ctx[block_start : block_start + block_size]
        query_block = queries[block_start : block_start + block_size]
        value_grad = value_grad + jnp.einsum(
            "hqk,qhd->khd", probs_low, grad_block, preferred_element_type=jnp.float32
        )
        prob_grad = jnp.einsum(
            "qhd,khd->hqk", grad_block, values, preferred_element_type=jnp.float32
        )
        delta = jnp.sum(probs * prob_grad, axis=-1, keepdims=True)
        score_grad = (probs * (prob_grad - delta)).astype(jnp.bfloat16)
        query_parts.append(
            jnp.einsum("hqk,khd->qhd", score_grad, keys_all, preferred_element_type=jnp.float32)
            * scale
        )
        key_grad = (
            key_grad
            + jnp.einsum(
                "hqk,qhd->khd", score_grad, query_block, preferred_element_type=jnp.float32
            )
            * scale
        )
    return (jnp.concatenate(query_parts, axis=0), key_grad, value_grad)


def per_device(
    inputs,
    w_qkv,
    b_qv,
    w_out,
    w_in,
    b_in,
    w_back,
    norm_gains,
    shifts,
    segment_ids,
    valid_lengths,
    teacher,
):
    own_seqs, seq_len, width = inputs.shape
    own_rows = own_seqs * seq_len
    total_slots = own_rows * lax.axis_size("tensor") * lax.axis_size("dp")
    x_rows = inputs.reshape(own_rows, width)
    own_valid = lax.dynamic_slice_in_dim(
        valid_lengths, lax.axis_index("tensor") * own_seqs, own_seqs
    )
    positions = jnp.arange(seq_len, dtype=jnp.int32)
    live_mask = (positions[None, :] < own_valid[:, None]).reshape(own_rows).astype(jnp.float32)
    own_count = jnp.sum(own_valid).astype(jnp.float32)
    weights_low, out_low, in_low, back_low = (
        lax.all_gather(w_qkv.astype(jnp.bfloat16), "tensor", axis=2, tiled=True),
        lax.all_gather(w_out.astype(jnp.bfloat16), "tensor", axis=0, tiled=True),
        lax.all_gather(w_in.astype(jnp.bfloat16), "tensor", axis=1, tiled=True),
        lax.all_gather(w_back.astype(jnp.bfloat16), "tensor", axis=0, tiled=True),
    )
    bias_qv, bias_in = (
        lax.all_gather(b_qv, "tensor", axis=1, tiled=True),
        lax.all_gather(b_in, "tensor", axis=0, tiled=True),
    )
    seg_here = lax.dynamic_slice_in_dim(
        segment_ids, lax.axis_index("tensor") * own_seqs, own_seqs, 0
    )
    x_group = x_rows.astype(jnp.bfloat16)
    heads_here = weights_low.shape[2] // HD
    seq_count = seg_here.shape[0]
    group_rows = seq_count * seq_len
    head_shape = (seq_count, seq_len, heads_here, HD)
    query_low = (
        (matmul_f32(x_group, weights_low[0]) + bias_qv[0]).astype(jnp.bfloat16).reshape(head_shape)
    )
    keys_low = matmul_f32(x_group, weights_low[1]).astype(jnp.bfloat16).reshape(head_shape)
    values_low = (
        (matmul_f32(x_group, weights_low[2]) + bias_qv[1]).astype(jnp.bfloat16).reshape(head_shape)
    )
    context, log_total = lax.map(
        attend_forward, (query_low, keys_low, values_low, seg_here, own_valid)
    )
    context_low = context.reshape(group_rows, heads_here * HD).astype(jnp.bfloat16)
    attn_rows = matmul_f32(context_low, out_low)
    mid_state, norm_one_back = jax.vjp(
        layer_norm, attn_rows + shifts[0] + x_rows, norm_gains[0], shifts[1]
    )
    mid_group = mid_state.astype(jnp.bfloat16)
    hidden, gelu_back = jax.vjp(exact_gelu, matmul_f32(mid_group, in_low) + bias_in)
    hidden_low = hidden.astype(jnp.bfloat16)
    ffn_rows = matmul_f32(hidden_low, back_low)
    output, norm_two_back = jax.vjp(
        layer_norm, ffn_rows + shifts[2] + mid_state, norm_gains[1], shifts[3]
    )
    distance = output - teacher.reshape(own_rows, width)
    squared_sum = jnp.sum(live_mask * jnp.sum(distance * distance, axis=-1))
    squared_total, token_count = lax.psum((squared_sum, own_count), ("dp", "tensor"))
    out_grad = total_slots / token_count * live_mask[:, None] * distance
    dh_two, gain_two, shift_two = norm_two_back(out_grad)
    out_grad_group = dh_two.astype(jnp.bfloat16)
    hidden_grad = right_cross(out_grad_group, back_low)
    grad_w_back = left_cross(hidden_low, out_grad_group)
    (pre_grad,) = gelu_back(hidden_grad)
    pre_grad_low = pre_grad.astype(jnp.bfloat16)
    grad_b_in = jnp.sum(pre_grad_low.astype(jnp.float32), axis=0)
    grad_w_in = left_cross(mid_group, pre_grad_low)
    grad_w_in, grad_b_in, grad_w_back = (
        lax.psum_scatter(
            grad_w_in.astype(jnp.bfloat16), "tensor", scatter_dimension=1, tiled=True
        ).astype(jnp.float32),
        lax.psum_scatter(
            grad_b_in.astype(jnp.bfloat16), "tensor", scatter_dimension=0, tiled=True
        ).astype(jnp.float32),
        lax.psum_scatter(
            grad_w_back.astype(jnp.bfloat16), "tensor", scatter_dimension=0, tiled=True
        ).astype(jnp.float32),
    )
    mid_grad = right_cross(pre_grad_low, in_low) + dh_two
    dh_one, gain_one, shift_one = norm_one_back(mid_grad)
    attn_grad_group = dh_one.astype(jnp.bfloat16)
    context_grad = right_cross(attn_grad_group, out_low).astype(jnp.bfloat16)
    grad_w_out = left_cross(context_low, attn_grad_group)
    grads_query, grads_key, grads_value = lax.map(
        attend_backward,
        (
            query_low,
            keys_low,
            values_low,
            context_grad.reshape(head_shape),
            log_total,
            seg_here,
            own_valid,
        ),
    )
    query_grad = grads_query.reshape(group_rows, heads_here * HD).astype(jnp.bfloat16)
    key_grad = grads_key.reshape(group_rows, heads_here * HD).astype(jnp.bfloat16)
    value_grad = grads_value.reshape(group_rows, heads_here * HD).astype(jnp.bfloat16)
    grad_b_qv = jnp.stack(
        [
            jnp.sum(query_grad.astype(jnp.float32), axis=0),
            jnp.sum(value_grad.astype(jnp.float32), axis=0),
        ]
    )
    grad_w_qkv = jnp.stack(
        [
            left_cross(x_group, query_grad),
            left_cross(x_group, key_grad),
            left_cross(x_group, value_grad),
        ]
    )
    part_query = lax.slice_in_dim(query_grad, 0, own_rows, axis=0)
    part_key = lax.slice_in_dim(key_grad, 0, own_rows, axis=0)
    part_value = lax.slice_in_dim(value_grad, 0, own_rows, axis=0)
    grad_inputs = (
        right_cross(part_query, weights_low[0])
        + right_cross(part_key, weights_low[1])
        + right_cross(part_value, weights_low[2])
        + dh_one
    )
    grad_w_qkv, grad_b_qv, grad_w_out = (
        lax.psum_scatter(
            grad_w_qkv.astype(jnp.bfloat16), "tensor", scatter_dimension=2, tiled=True
        ).astype(jnp.float32),
        lax.psum_scatter(
            grad_b_qv.astype(jnp.bfloat16), "tensor", scatter_dimension=1, tiled=True
        ).astype(jnp.float32),
        lax.psum_scatter(
            grad_w_out.astype(jnp.bfloat16), "tensor", scatter_dimension=0, tiled=True
        ).astype(jnp.float32),
    )
    grad_w_qkv, grad_b_qv, grad_w_out, grad_w_in, grad_b_in, grad_w_back = lax.psum(
        (grad_w_qkv, grad_b_qv, grad_w_out, grad_w_in, grad_b_in, grad_w_back), "dp"
    )
    gain_grads = jnp.stack([gain_one, gain_two])
    shift_grads = jnp.stack(
        [jnp.sum(dh_one, axis=0), shift_one, jnp.sum(dh_two, axis=0), shift_two]
    )
    small_terms = (gain_grads, shift_grads)
    small_totals = lax.psum((small_terms[0], small_terms[1]), ("dp", "tensor"))
    loss = squared_total / (2.0 * width * token_count)
    return (
        output.reshape(own_seqs, seq_len, width),
        loss,
        grad_inputs.reshape(own_seqs, seq_len, width),
        grad_w_qkv,
        grad_b_qv,
        grad_w_out,
        grad_w_in,
        grad_b_in,
        grad_w_back,
        small_totals[0],
        small_totals[1],
    )


def solution(mesh):
    return jax.shard_map(
        per_device,
        mesh=mesh,
        in_specs=(
            P(("dp", "tensor"), None, None),
            P(None, None, "tensor"),
            P(None, "tensor"),
            P("tensor", None),
            P(None, "tensor"),
            P("tensor"),
            P("tensor", None),
            P(),
            P(),
            P("dp", None),
            P("dp"),
            P(("dp", "tensor"), None, None),
        ),
        out_specs=(
            P(("dp", "tensor"), None, None),
            P(),
            P(("dp", "tensor"), None, None),
            P(None, None, "tensor"),
            P(None, "tensor"),
            P("tensor", None),
            P(None, "tensor"),
            P("tensor"),
            P("tensor", None),
            P(),
            P(),
        ),
        check_vma=False,
    )
```

profile of v0, /device:TPU:0, one launch (start us, length us, event | category | flops | bytes accessed | tf_op | source)
XLA Modules:
  0.0 866.9 jit_solution(11959196759228868608)
XLA Ops:
  20.6 42.4 %psum.71 = f32[]{:T(128)} all-reduce(f32[]{:T(128)S(6)} %convert_element_type.162), channel_id=1, replica_groups=mesh['dp'=8,'tensor'=4] {'dp','tensor'}, use_global_device_ids=true, to_apply=%region_11.12 | all-reduce | flops 1 | bytes 8 | tf_op jit(solution)/shard_map/psum | solution.py:178
  65.1 5.6 all-gather
  71.4 6.0 all-gather.1
  89.5 10.7 %fusion.18 = (f32[12,512]{1,0:T(8,128)S(1)}, f32[12,512,1024]{2,1,0:T(8,128)}) fusion(pred[512,1024]{1,0:T(8,128)(4,1)S(1)} %get-tuple-element.139, bf16[512,12,64]{0,2,1:T(8,128)(2,1)S(1)} %bitcast.142, bf16[1024,12,64]{0,2,1:T(8,128)(2,1)S(1)} %bitcast.136), kind=kOutput, calls=%fused_computation.39 | convolution fusion | flops 824174592 | bytes 28073984 | tf_op jit(solution)/shard_map/while/body/eval_jaxpr/qhd,khd->hqk/dot_general | solution.py:46
  100.3 12.5 %fusion = f32[12,512]{1,0:T(8,128)S(1)} fusion(f32[12,512]{1,0:T(8,128)S(1)} %get-tuple-element.143, f32[12,512,1024]{2,1,0:T(8,128)} %get-tuple-element.144, pred[512,1024]{1,0:T(8,128)(4,1)S(1)} %get-tuple-element.139), kind=kLoop, calls=%fused_computation.12 | loop fusion | flops 25159680 | bytes 25739264 | tf_op jit(solution)/shard_map/while/body/eval_jaxpr/reduce_sum | solution.py:67
  113.4 4.3 add_convert_fusion.3
  118.1 8.5 fusion.55
  126.6 10.7 %fusion.19 = (f32[12,512]{1,0:T(8,128)S(1)}, f32[12,512,1024]{2,1,0:T(8,128)}) fusion(pred[512,1024]{1,0:T(8,128)(4,1)S(1)} %get-tuple-element.140, bf16[512,12,64]{0,2,1:T(8,128)(2,1)S(1)} %bitcast.140, bf16[1024,12,64]{0,2,1:T(8,128)(2,1)S(1)} %bitcast.137), kind=kOutput, calls=%fused_computation.40 | convolution fusion | flops 824174592 | bytes 28073984 | tf_op jit(solution)/shard_map/while/body/eval_jaxpr/qhd,khd->hqk/dot_general | solution.py:46
  137.3 12.9 %fusion.1 = f32[12,512]{1,0:T(8,128)S(1)} fusion(f32[12,512]{1,0:T(8,128)S(1)} %get-tuple-element.141, f32[12,512,1024]{2,1,0:T(8,128)} %get-tuple-element.142, pred[512,1024]{1,0:T(8,128)(4,1)S(1)} %get-tuple-element.140), kind=kLoop, calls=%fused_computation.13 | loop fusion | flops 25159680 | bytes 25739264 | tf_op jit(solution)/shard_map/while/body/eval_jaxpr/reduce_sum | solution.py:67
  152.8 7.8 fusion.56
  162.0 4.2 fusion.80
  167.0 37.9 %multiply_convert_fusion.2 = (bf16[1024,3072]{1,0:T(8,128)(2,1)}, f32[1024,3072]{1,0:T(8,128)}, f32[1024,3072]{1,0:T(8,128)}) fusion(f32[3072]{0:T(1024)S(1)} %bitcast.166, bf16[768,3072]{1,0:T(8,128)(2,1)} %all-gather.11.cloned.1.call-done, f32[1024,768]{0,1:T(8,128)S(1)} %get-tuple-element.146, f32[768]{0:T(1024)S(1)} %copy-done.48, ...), kind=kOutput, calls=%fused_computation.23 | convolution fusion | flops 5043388416 | bytes 39348224 | tf_op jit(solution)/shard_map/dot_general | solution.py:26
  204.9 9.1 %fusion.81 = (f32[1024]{0:T(1024)S(1)}, f32[1024,768]{0,1:T(8,128)S(1)}) fusion(f32[768]{0:T(1024)S(1)} %copy-done.48, f32[768]{0:T(1024)S(1)} %copy-done.37, f32[1024]{0:T(1024)S(1)} %fusion.59, f32[1024,768]{0,1:T(8,128)S(1)} %get-tuple-element.146, f32[1024]{0:T(1024)S(1)} %broadcast_multiply_fusion.1, f32[768]{0:T(1024)S(1)} %copy-done.50, ...), kind=kOutput, calls=%fused_computation.154 | convolution fusion | flops 4837342208 | bytes 17323008 | tf_op jit(solution)/shard_map/dot_general | solution.py:26
  216.0 4.1 multiply_reduce_fusion.2
  222.6 19.5 %fusion.82 = (bf16[3072]{0:T(1024)(128)(2,1)}, bf16[1024,3072]{1,0:T(8,128)(2,1)}) fusion(f32[1024,3072]{1,0:T(8,128)} %get-tuple-element.131, bf16[3072,768]{1,0:T(8,128)(2,1)} %all-gather.13.cloned.1.call-done, f32[1024,768]{0,1:T(8,128)} %get-tuple-element.128, f32[1024]{0:T(1024)S(1)} %negate_multiply_fusion.2, f32[1024,3072]{1,0:T(8,128)} %get-tuple-element.147, ...), kind=kOutput, calls=%fused_computation.155 | convolution fusion | flops 4883739648 | bytes 39344128 | tf_op jit(solution)/shard_map/ne,de->nd/dot_general | solution.py:34
  242.1 10.9 %multiply_reduce_fusion.3 = (f32[768]{0:T(1024)}, f32[1024]{0:T(1024)S(1)}, f32[768]{0:T(1024)}, f32[1024,768]{0,1:T(8,128)S(1)}) fusion(f32[1024,768]{0,1:T(8,128)S(1)} %get-tuple-element.146, f32[1024]{0:T(1024)S(1)} %fusion.59, f32[1024]{0:T(1024)S(1)} %broadcast_multiply_fusion.1, f32[768]{0:T(1024)S(1)} %copy-done.37, ...), kind=kOutput, calls=%fused_computation.49 | convolution fusion | flops 4839699456 | bytes 20472832 | tf_op jit(solution)/shard_map/ne,de->nd/dot_general | solution.py:34
  262.1 13.1 %fusion.5 = f32[12,64,1024]{2,1,0:T(8,128)} fusion(bf16[512,12,64]{0,2,1:T(8,128)(2,1)S(1)} %bitcast.152, f32[12,512]{1,0:T(8,128)S(1)} %copy-done.34, f32[12,512,1024]{2,1,0:T(8,128)} %get-tuple-element.142, pred[512,1024]{1,0:T(8,128)(4,1)S(1)} %copy-done.9), kind=kOutput, calls=%fused_computation.18 | convolution fusion | flops 830472192 | bytes 29646848 | tf_op jit(solution)/shard_map/while/body/eval_jaxpr/hqk,qhd->khd/dot_general | solution.py:90
  275.2 18.0 %multiply_reduce_fusion = (f32[12,512]{1,0:T(8,128)S(1)}, f32[12,512,1024]{2,1,0:T(8,128)}) fusion(f32[12,512]{1,0:T(8,128)S(1)} %copy-done.34, f32[12,512,1024]{2,1,0:T(8,128)} %get-tuple-element.142, pred[512,1024]{1,0:T(8,128)(4,1)S(1)} %copy-done.9, bf16[512,12,64]{0,2,1:T(8,128)(2,1)} %bitcast.153, bf16[1024,12,64]{0,2,1:T(8,128)(2,1)S(1)} %bitcast.146), kind=kOutput, calls=%fused_computation.1 | convolution fusion | flops 836757504 | bytes 53264384 | tf_op jit(solution)/shard_map/while/body/eval_jaxpr/qhd,khd->hqk/dot_general | solution.py:93
  293.3 21.4 %multiply_reduce_fusion.1 = (f32[12,512]{1,0:T(8,128)S(1)}, f32[12,512,1024]{2,1,0:T(8,128)}) fusion(f32[12,512]{1,0:T(8,128)S(1)} %copy-done.33, f32[12,512,1024]{2,1,0:T(8,128)} %get-tuple-element.144, pred[512,1024]{1,0:T(8,128)(4,1)S(1)} %copy-done.7, bf16[512,12,64]{0,2,1:T(8,128)(2,1)S(1)} %bitcast.150, bf16[1024,12,64]{0,2,1:T(8,128)(2,1)S(1)} %bitcast.147), kind=kOutput, calls=%fused_computation.4 | convolution fusion | flops 836757504 | bytes 53264384 | tf_op jit(solution)/shard_map/while/body/eval_jaxpr/qhd,khd->hqk/dot_general | solution.py:93
  314.7 13.8 %bitcast_reduce_fusion = (bf16[12,64]{1,0:T(8,128)(2,1)S(1)}, bf16[12,64,1024]{2,1,0:T(8,128)(2,1)}) fusion(f32[12,64,1024]{2,1,0:T(8,128)} %fusion.5, bf16[512,12,64]{0,2,1:T(8,128)(2,1)S(1)} %bitcast.151, f32[12,512]{1,0:T(8,128)S(1)} %copy-done.33, f32[12,512,1024]{2,1,0:T(8,128)} %get-tuple-element.144, pred[512,1024]{1,0:T(8,128)(4,1)S(1)} %copy-done.7), kind=kOutput, calls=%fused_computation.79 | convolution fusion | flops 832830720 | bytes 31221248 | tf_op jit(solution)/shard_map/while/body/eval_jaxpr/hqk,qhd->khd/dot_general | solution.py:90
  328.6 41.8 %multiply_convert_fusion = (bf16[12,512,1024]{2,1,0:T(8,128)(2,1)}, bf16[12,512,1024]{2,1,0:T(8,128)(2,1)}) fusion(f32[12,512,1024]{2,1,0:T(8,128)} %get-tuple-element.152, f32[12,512]{1,0:T(8,128)S(1)} %get-tuple-element.151, f32[12,512]{1,0:T(8,128)S(1)} %copy-done.34, f32[12,512,1024]{2,1,0:T(8,128)} %get-tuple-element.142, ...), kind=kLoop, calls=%fused_computation | loop fusion | flops 75497472 | bytes 126976000 | tf_op jit(solution)/shard_map/while/body/eval_jaxpr/convert_element_type | solution.py:97
  370.4 10.1 %bitcast_reduce_fusion.1 = (bf16[12,64]{1,0:T(8,128)(2,1)S(1)}, bf16[12,64,512]{2,1,0:T(8,128)(2,1)}) fusion(bf16[1024,12,64]{0,2,1:T(8,128)(2,1)} %bitcast.138, bf16[12,512,1024]{2,1,0:T(8,128)(2,1)} %get-tuple-element.163), kind=kOutput, calls=%fused_computation.107 | convolution fusion | flops 806485248 | bytes 14943744 | tf_op jit(solution)/shard_map/while/body/eval_jaxpr/hqk,khd->qhd/dot_general | solution.py:99
  380.5 6.2 bitcast_reduce_fusion.2
  394.3 7.1 fusion.83
  409.1 9.7 %convolution_convert_fusion.1 = bf16[768,3072]{1,0:T(8,128)(2,1)} fusion(bf16[1024,3072]{1,0:T(8,128)(2,1)} %get-tuple-element.162, f32[1024,768]{0,1:T(8,128)S(1)} %copy-done.12, f32[768]{0:T(1024)S(1)} %copy-done.49, f32[768]{0:T(1024)S(1)} %copy-done.37, f32[1024]{0:T(1024)S(1)} %fusion.59, f32[1024]{0:T(1024)S(1)} %broadcast_multiply_fusion.1), kind=kOutput, calls=%fused_computation.42 | convolution fusion | flops 4838129664 | bytes 14170112 | tf_op jit(solution)/shard_map/nd,ne->de/dot_general | solution.py:30
  420.7 9.8 %convolution_convert_fusion = bf16[3072,768]{1,0:T(8,128)(2,1)} fusion(bf16[1024,3072]{1,0:T(8,128)(2,1)} %get-tuple-element.130, f32[1024,768]{0,1:T(8,128)S(1)} %copy-done.13, f32[1024]{0:T(1024)S(1)} %copy-done.43), kind=kOutput, calls=%fused_computation.41 | convolution fusion | flops 4835770368 | bytes 14159872 | tf_op jit(solution)/shard_map/nd,ne->de/dot_general | solution.py:30
  436.5 40.7 %all-reduce.1 = (f32[]{:T(128)}, f32[2,768]{1,0:T(2,128)}, f32[4,768]{1,0:T(4,128)}) all-reduce(f32[]{:T(128)} %select_reduce_fusion, f32[2,768]{1,0:T(2,128)S(1)} %pad_maximum_fusion.6, f32[4,768]{1,0:T(4,128)S(1)} %pad_maximum_fusion.5), channel_id=1, replica_groups=mesh['dp'=8,'tensor'=4] {'dp','tensor'}, use_global_device_ids=true, to_apply=%region_10.11 | all-reduce | flops 4609 | bytes 36872 | tf_op jit(solution)/shard_map/psum | solution.py:178
  488.9 4.4 copy.48
  494.0 7.0 all-reduce
  502.0 27.4 %reduce-scatter.12.cloned.1.call-done = bf16[768,768]{1,0:T(8,128)(2,1)} async-done(((bf16[768,3072]{1,0:T(8,128)(2,1)}), bf16[768,768]{1,0:T(8,128)(2,1)}) %reduce-scatter.12.cloned.1.call-update) | async-done | bytes 1179664 | tf_op jit(solution)/shard_map/reduce_scatter | solution.py:189
  529.4 50.6 %reduce-scatter.14.cloned.1.call-done = bf16[768,768]{1,0:T(8,128)(2,1)} async-done(((bf16[3072,768]{1,0:T(8,128)(2,1)}), bf16[768,768]{1,0:T(8,128)(2,1)}) %reduce-scatter.14.cloned.1.call-update) | async-done | bytes 1179664 | tf_op jit(solution)/shard_map/reduce_scatter | solution.py:195
  579.9 279.0 %all-reduce.4 = (f32[3,768,192]{1,2,0:T(8,128)}, f32[2,192]{1,0:T(2,128)}, f32[192,768]{1,0:T(8,128)}, f32[768,768]{1,0:T(8,128)}, f32[768]{0:T(1024)}, /*index=5*/f32[768,768]{1,0:T(8,128)}) all-reduce(bf16[3,768,192]{1,2,0:T(8,128)(2,1)} %reduce-scatter.8.cloned.1.call-done, ...), channel_id=1, replica_groups=mesh['dp'=8,'tensor'=4] {'dp'}, use_global_device_ids=true, to_apply=%region_19.20 | all-reduce | flops 1770624 | bytes 10625280 | tf_op jit(solution)/shard_map/psum | solution.py:252
  (220 shorter events, 79.9 us)
Async XLA Ops:
  7.2 75.8 %all-gather.7.cloned.1.call-start = ((), (), s32[]{:S(2)}) async-start(), calls=%async_computation.5 | async-start | bytes 4423680 | tf_op jit(solution)/shard_map/all_gather | solution.py:137
  9.9 152.1 %all-gather.9.cloned.1.call-start = ((), (), s32[]{:S(2)}) async-start(), calls=%async_computation.6 | async-start | bytes 1474560 | tf_op jit(solution)/shard_map/all_gather | solution.py:138
  10.7 156.0 %all-gather.11.cloned.1.call-start = ((), (), s32[]{:S(2)}) async-start(), calls=%async_computation.7 | async-start | bytes 5898240 | tf_op jit(solution)/shard_map/all_gather | solution.py:139
  11.9 193.0 %all-gather.13.cloned.1.call-start = ((), (), s32[]{:S(2)}) async-start(), calls=%async_computation.8 | async-start | bytes 5898240 | tf_op jit(solution)/shard_map/all_gather | solution.py:140
  14.9 486.1 %reduce-scatter.16.cloned.1.call-start = ((), (), s32[]{:S(2)}) async-start(), calls=%async_computation.13 | async-start | bytes 245760
  18.2 44.8 %copy-start.51 = (f32[768]{0:T(1024)S(1)}, f32[768]{0:T(1024)}, u32[]{:S(2)}) copy-start(f32[768]{0:T(1024)} %param.17) | copy-start | bytes 9220
  18.2 46.7 %copy-start.54 = (s32[4,1024]{1,0:T(4,128)S(1)}, s32[4,1024]{1,0:T(4,128)}, u32[]{:S(2)}) copy-start(s32[4,1024]{1,0:T(4,128)} %param.21) | copy-start | bytes 49156
  18.2 46.9 %copy-start.55 = (f32[2,192]{1,0:T(2,128)S(1)}, f32[2,192]{1,0:T(2,128)}, u32[]{:S(2)}) copy-start(f32[2,192]{1,0:T(2,128)} %param.14) | copy-start | bytes 4612
  18.2 52.5 %copy-start.46 = (f32[2,768]{1,0:T(2,128)S(1)}, f32[2,768]{1,0:T(2,128)}, u32[]{:S(2)}) copy-start(f32[2,768]{1,0:T(2,128)} %param.19) | copy-start | bytes 18436
  18.2 59.2 %copy-start.44 = (f32[4,768]{1,0:T(4,128)S(1)}, f32[4,768]{1,0:T(4,128)}, u32[]{:S(2)}) copy-start(f32[4,768]{1,0:T(4,128)} %param.20) | copy-start | bytes 36868
  83.0 34.8 %copy-start.6 = (pred[512,1024]{1,0:T(8,128)(4,1)}, pred[512,1024]{1,0:T(8,128)(4,1)S(1)}, u32[]{:S(2)}) copy-start(pred[512,1024]{1,0:T(8,128)(4,1)S(1)} %get-tuple-element.139) | copy-start | bytes 1572868
  83.0 67.9 %copy-start.8 = (pred[512,1024]{1,0:T(8,128)(4,1)}, pred[512,1024]{1,0:T(8,128)(4,1)S(1)}, u32[]{:S(2)}) copy-start(pred[512,1024]{1,0:T(8,128)(4,1)S(1)} %get-tuple-element.140) | copy-start | bytes 1572868
  86.2 40.3 %copy-start.15 = (bf16[512,768]{0,1:T(8,128)(2,1)}, bf16[512,768]{0,1:T(8,128)(2,1)S(1)}, u32[]{:S(2)}) copy-start(bf16[512,768]{0,1:T(8,128)(2,1)S(1)} %get-tuple-element.136) | copy-start | bytes 2359300
  89.5 37.1 %copy-start.5 = (bf16[1024,768]{0,1:T(8,128)(2,1)}, bf16[1024,768]{0,1:T(8,128)(2,1)S(1)}, u32[]{:S(2)}) copy-start(bf16[1024,768]{0,1:T(8,128)(2,1)S(1)} %convolution_convert_fusion.3) | copy-start | bytes 4718596
  100.3 17.8 %copy-start = (f32[12,512,1024]{2,1,0:T(8,128)S(1)}, f32[12,512,1024]{2,1,0:T(8,128)}, u32[]{:S(2)}) copy-start(f32[12,512,1024]{2,1,0:T(8,128)} %get-tuple-element.144) | copy-start | bytes 75497472
  117.8 33.1 %copy-start.19 = (bf16[1024,768]{0,1:T(8,128)(2,1)}, bf16[1024,768]{0,1:T(8,128)(2,1)S(1)}, u32[]{:S(2)}) copy-start(bf16[1024,768]{0,1:T(8,128)(2,1)S(1)} %add_convert_fusion.3) | copy-start | bytes 4718596
  137.3 15.5 %copy-start.1 = (f32[12,512,1024]{2,1,0:T(8,128)S(1)}, f32[12,512,1024]{2,1,0:T(8,128)}, u32[]{:S(2)}) copy-start(f32[12,512,1024]{2,1,0:T(8,128)} %get-tuple-element.142) | copy-start | bytes 75497472
  152.8 7.8 copy-start.30
  166.2 75.9 %copy-start.11 = (f32[1024,768]{0,1:T(8,128)}, f32[1024,768]{0,1:T(8,128)S(1)}, u32[]{:S(2)}) copy-start(f32[1024,768]{0,1:T(8,128)S(1)} %get-tuple-element.146) | copy-start | bytes 9437188
  167.0 37.9 %copy-start.50 = (f32[768]{0:T(1024)S(1)}, f32[768]{0:T(1024)}, u32[]{:S(2)}) copy-start(f32[768]{0:T(1024)} %get-tuple-element.111) | copy-start | bytes 9220
  222.6 19.5 %copy-start.42 = (f32[1024]{0:T(1024)}, f32[1024]{0:T(1024)S(1)}, u32[]{:S(2)}) copy-start(f32[1024]{0:T(1024)S(1)} %negate_multiply_fusion.2) | copy-start | bytes 12292
  262.1 13.1 %copy-start.20 = (bf16[1024,768]{0,1:T(8,128)(2,1)S(1)}, bf16[1024,768]{0,1:T(8,128)(2,1)}, u32[]{:S(2)}) copy-start(bf16[1024,768]{0,1:T(8,128)(2,1)} %copy-done.19) | copy-start | bytes 4718596
  275.2 18.0 %copy-start.7 = (pred[512,1024]{1,0:T(8,128)(4,1)S(1)}, pred[512,1024]{1,0:T(8,128)(4,1)}, u32[]{:S(2)}) copy-start(pred[512,1024]{1,0:T(8,128)(4,1)} %copy-done.6) | copy-start | bytes 1572868
  275.2 18.0 %copy-start.33 = (f32[12,512]{1,0:T(8,128)S(1)}, f32[12,512]{1,0:T(8,128)}, u32[]{:S(2)}) copy-start(f32[12,512]{1,0:T(8,128)} %log_add_fusion.1) | copy-start | bytes 73732
  370.4 10.1 %copy-start.2 = (bf16[12,512,1024]{2,1,0:T(8,128)(2,1)S(1)}, bf16[12,512,1024]{2,1,0:T(8,128)(2,1)}, u32[]{:S(2)}) copy-start(bf16[12,512,1024]{2,1,0:T(8,128)(2,1)} %get-tuple-element.164) | copy-start | bytes 37748740
  387.7 114.2 %reduce-scatter.10.cloned.1.call-start = ((), (), s32[]{:S(2)}) async-start(), calls=%async_computation.10 | async-start | bytes 1474560 | tf_op jit(solution)/shard_map/reduce_scatter | solution.py:248
  391.2 110.7 %reduce-scatter.8.cloned.1.call-start = ((), (), s32[]{:S(2)}) async-start(), calls=%async_computation.9 | async-start | bytes 4423680 | tf_op jit(solution)/shard_map/reduce_scatter | solution.py:242
  391.5 9.9 %slice-start = ((s8[12582912]{0:T(1024)(128)(4,1)}), s8[4194304]{0:T(1024)(128)(4,1)S(1)}, s32[]{:S(2)}) async-start(s8[12582912]{0:T(1024)(128)(4,1)} %bitcast.134), calls=%async_computation.14 | async-start | bytes 8388608
  394.2 7.2 slice-start.1
  394.2 7.2 slice-start.2
  407.2 122.1 %reduce-scatter.12.cloned.1.call-start = ((), (), s32[]{:S(2)}) async-start(), calls=%async_computation.11 | async-start | bytes 5898240 | tf_op jit(solution)/shard_map/reduce_scatter | solution.py:189
  418.8 161.1 %reduce-scatter.14.cloned.1.call-start = ((), (), s32[]{:S(2)}) async-start(), calls=%async_computation.12 | async-start | bytes 5898240 | tf_op jit(solution)/shard_map/reduce_scatter | solution.py:195
  (38 other events, 100.0 us)
Sparse Core Ops, SparseCore 0:
  10.2 34.1 all-gather.6
  45.9 18.0 all-gather.8
  65.6 37.4 all-gather.10
  104.4 37.4 all-gather.12
  387.8 18.9 reduce-scatter.15
  409.2 25.7 reduce-scatter.9
  437.8 41.1 reduce-scatter.7
  481.5 47.8 reduce-scatter.11
  532.1 47.8 reduce-scatter.13
where the time goes:
time: 870 us; the launch traced here: 867 us
  blocking collectives  381 us (44%)
  matrix products  262 us (30%)
  other arithmetic  98 us (11%)
  waiting for transfers between devices  78.2 us (9%)
  local copies, waits for them, and re-layouts  27.6 us (3%)
  between operations  19.6 us (2%)
    psum x1, blocking collectives, per_device(): lax.psum((grad_w_qkv, grad_b_qv, grad_w_out, grad_w_in, grad_b_in, grad_w...  279 us
    psum x2, blocking collectives, per_device(): lax.psum((squared_sum, own_count), ('dp', 'tensor'))  83.1 us
    dot_general x6, matrix products, matmul_f32(): return jnp.dot(left, right, preferred_element_type=jnp.float32)  61.8 us
    reduce_scatter x1, waiting for transfers between devices, per_device(): lax.psum_scatter(grad_w_back.astype(jnp.bfloat16), 'tensor', scatter_dime...  50.6 us
    convert_element_type x1, other arithmetic, attend_backward(): score_grad = (probs * (prob_grad - delta)).astype(jnp.bfloat16)  41.8 us
    dot_general x6, matrix products, right_cross(): jnp.einsum('ne,de->nd', left, right, preferred_element_type=jnp.float32)  41.1 us
    dot_general x2, matrix products, attend_backward(): jnp.einsum('qhd,khd->hqk', grad_block, values, preferred_element_type=jnp...  39.5 us
    dot_general x6, matrix products, left_cross(): jnp.einsum('nd,ne->de', left, right, preferred_element_type=jnp.float32)  29.5 us
  transfers between devices with their start and end apart: 9, of which 2 were waited for; matrix products, arithmetic and copies ran while one was open for 23% of the time, Pallas kernels for 0%

commit v1 on v0

v1 whole, which is shorter than its diff:
```python
import functools
import math

import jax
import jax.numpy as jnp
from jax import lax
from jax.experimental import pallas as pl
from jax.experimental.pallas import tpu as pltpu
from jax.sharding import PartitionSpec as P

HD = 64
LN_EPSILON = 1e-05
MASKED_SCORE = -1000000000.0
QB = 256
KB = 128
NT = ((1,), (1,))


def layer_norm(values, gain, shift):
    centred = values - jnp.mean(values, axis=-1, keepdims=True)
    spread = jnp.mean(centred * centred, axis=-1, keepdims=True)
    return centred * lax.rsqrt(spread + LN_EPSILON) * gain + shift


def exact_gelu(values):
    return jax.nn.gelu(values, approximate=False)


def matmul_f32(left, right):
    return jnp.dot(left, right, preferred_element_type=jnp.float32)


def left_cross(left, right):
    return jnp.einsum("nd,ne->de", left, right, preferred_element_type=jnp.float32)


def right_cross(left, right):
    return jnp.einsum("ne,de->nd", left, right, preferred_element_type=jnp.float32)


def dot(left, right, dims=((1,), (0,))):
    return lax.dot_general(left, right, (dims, ((), ())), preferred_element_type=jnp.float32)


def span_tables(segments, valid, seq):
    blocks = seq // QB
    firsts, lasts = segments[::QB], segments[QB - 1 :: QB]
    low = jnp.sum((segments[None, :] < firsts[:, None]).astype(jnp.int32), axis=1)
    high = jnp.sum((segments[None, :] <= lasts[:, None]).astype(jnp.int32), axis=1)
    own_end = (jnp.arange(blocks, dtype=jnp.int32) + 1) * QB
    high = jnp.maximum(jnp.minimum(high, valid), own_end)
    low_block = low // KB
    high_block = (high + KB - 1) // KB
    return jnp.stack([low_block, high_block - low_block]).astype(jnp.int32)


def make_bias(bias_ref, block, low, count, code_ref, seg_ref):
    shape = (count * KB, QB)
    codes = code_ref[pl.ds(low * KB, count * KB), :]
    segs = seg_ref[:, pl.ds(block * QB, QB)]
    key_at = low * KB + lax.broadcasted_iota(jnp.int32, shape, 0)
    query_at = block * QB + lax.broadcasted_iota(jnp.int32, shape, 1)
    allowed = (codes == segs) | (key_at == query_at)
    bias_ref[block, : count * KB, :] = jnp.where(allowed, 0.0, MASKED_SCORE)


def one_head(values, head):
    lane = lax.broadcasted_iota(jnp.int32, values.shape, 1)
    keep = (lane < HD) if head == 0 else (lane >= HD)
    return jnp.where(keep, values, jnp.zeros_like(values))


def forward_kernel(
    table_ref, q_ref, k_ref, v_ref, code_ref, seg_ref, ctx_ref, lse_ref, vt_ref, bias_ref
):
    pair, block = pl.program_id(0), pl.program_id(1)
    low, total = table_ref[0, block], table_ref[1, block]

    @pl.when(block == 0)
    def _():
        vt_ref[...] = v_ref[...].T

    def run(count):
        @pl.when(pair == 0)
        def _():
            make_bias(bias_ref, block, low, count, code_ref, seg_ref)

        bias = bias_ref[block, : count * KB, :]
        rows = pl.ds(pl.multiple_of(low * KB, KB), count * KB)
        keys = k_ref[rows, :]
        queries = q_ref[...] * jnp.asarray(0.125, q_ref.dtype)
        outs, sums = [], []
        for head in range(2):
            scores = dot(keys, one_head(queries, head), NT) + bias
            peak = jnp.max(scores, axis=0, keepdims=True)
            powers = jnp.exp(scores - peak)
            mass = jnp.sum(powers, axis=0, keepdims=True)
            probs = (powers * (1.0 / mass)).astype(jnp.bfloat16)
            outs.append(dot(vt_ref[head * HD : (head + 1) * HD, rows], probs))
            sums.append(peak + jnp.log(mass))
        ctx_ref[...] = jnp.concatenate(outs, axis=0).T.astype(ctx_ref.dtype)
        lse_ref[0, 0:1, :] = sums[0]
        lse_ref[0, 1:2, :] = sums[1]

    for count in range(2, k_ref.shape[0] // KB + 1):
        pl.when(total == count)(functools.partial(run, count))


def backward_kernel(
    table_ref,
    q_ref,
    k_ref,
    v_ref,
    g_ref,
    lse_ref,
    code_ref,
    seg_ref,
    dq_ref,
    dk_ref,
    dv_ref,
    kt_ref,
    bias_ref,
    dk_sum,
    dv_sum,
):
    pair, block = pl.program_id(0), pl.program_id(1)
    low, total = table_ref[0, block], table_ref[1, block]

    @pl.when(block == 0)
    def _():
        kt_ref[...] = k_ref[...].T
        dk_sum[...] = jnp.zeros_like(dk_sum)
        dv_sum[...] = jnp.zeros_like(dv_sum)

    def run(count):
        @pl.when(pair == 0)
        def _():
            make_bias(bias_ref, block, low, count, code_ref, seg_ref)

        bias = bias_ref[block, : count * KB, :]
        rows = pl.ds(pl.multiple_of(low * KB, KB), count * KB)
        keys, values = k_ref[rows, :], v_ref[rows, :]
        queries = q_ref[...] * jnp.asarray(0.125, q_ref.dtype)
        grads = g_ref[...]
        outs = []
        for head in range(2):
            query, grad = one_head(queries, head), one_head(grads, head)
            probs = jnp.exp(dot(keys, query, NT) + bias - lse_ref[0, head : head + 1, :])
            dv_sum[rows, :] += dot(probs.astype(jnp.bfloat16), grad)
            prob_grad = dot(values, grad, NT)
            delta = jnp.sum(probs * prob_grad, axis=0, keepdims=True)
            score_grad = (probs * (prob_grad - delta)).astype(jnp.bfloat16)
            dk_sum[rows, :] += dot(score_grad, query)
            outs.append(dot(kt_ref[head * HD : (head + 1) * HD, rows], score_grad))
        dq_ref[...] = (jnp.concatenate(outs, axis=0).T * 0.125).astype(dq_ref.dtype)

    for count in range(2, k_ref.shape[0] // KB + 1):
        pl.when(total == count)(functools.partial(run, count))

    @pl.when(block == pl.num_programs(1) - 1)
    def _():
        dk_ref[...] = dk_sum[...].astype(dk_ref.dtype)
        dv_ref[...] = dv_sum[...].astype(dv_ref.dtype)


def attend_forward(table, qkv, code, seg):
    seq, width = qkv.shape[0], qkv.shape[1] // 3
    pairs, blocks = width // 128, seq // QB
    return pl.pallas_call(
        forward_kernel,
        out_shape=(
            jax.ShapeDtypeStruct((seq, width), jnp.bfloat16),
            jax.ShapeDtypeStruct((pairs, 8, seq), jnp.float32),
        ),
        grid_spec=pltpu.PrefetchScalarGridSpec(
            num_scalar_prefetch=1,
            grid=(pairs, blocks),
            in_specs=[
                pl.BlockSpec((QB, 128), lambda p, i, t: (i, p)),
                pl.BlockSpec((seq, 128), lambda p, i, t: (0, pairs + p)),
                pl.BlockSpec((seq, 128), lambda p, i, t: (0, 2 * pairs + p)),
                pl.BlockSpec((seq, 1), lambda p, i, t: (0, 0)),
                pl.BlockSpec((1, seq), lambda p, i, t: (0, 0)),
            ],
            out_specs=[
                pl.BlockSpec((QB, 128), lambda p, i, t: (i, p)),
                pl.BlockSpec((1, 8, QB), lambda p, i, t: (p, 0, i)),
            ],
            scratch_shapes=[
                pltpu.VMEM((128, seq), jnp.bfloat16),
                pltpu.VMEM((blocks, seq, QB), jnp.float32),
            ],
        ),
        compiler_params=pltpu.CompilerParams(vmem_limit_bytes=32 << 20),
        cost_estimate=pl.CostEstimate(
            flops=8 * seq * seq * width, bytes_accessed=8 * seq * width, transcendentals=seq * seq * pairs
        ),
        name="attend_forward",
    )(table, qkv, qkv, qkv, code, seg)


def attend_backward(table, qkv, grad, lse, code, seg):
    seq, width = grad.shape
    pairs, blocks = width // 128, seq // QB
    block = pl.BlockSpec((QB, 128), lambda p, i, t: (i, p))
    return pl.pallas_call(
        backward_kernel,
        out_shape=(jax.ShapeDtypeStruct((seq, width), jnp.bfloat16),) * 3,
        grid_spec=pltpu.PrefetchScalarGridSpec(
            num_scalar_prefetch=1,
            grid=(pairs, blocks),
            in_specs=[
                block,
                pl.BlockSpec((seq, 128), lambda p, i, t: (0, pairs + p)),
                pl.BlockSpec((seq, 128), lambda p, i, t: (0, 2 * pairs + p)),
                block,
                pl.BlockSpec((1, 8, QB), lambda p, i, t: (p, 0, i)),
                pl.BlockSpec((seq, 1), lambda p, i, t: (0, 0)),
                pl.BlockSpec((1, seq), lambda p, i, t: (0, 0)),
            ],
            out_specs=[
                block,
                pl.BlockSpec((seq, 128), lambda p, i, t: (0, p)),
                pl.BlockSpec((seq, 128), lambda p, i, t: (0, p)),
            ],
            scratch_shapes=[
                pltpu.VMEM((128, seq), jnp.bfloat16),
                pltpu.VMEM((blocks, seq, QB), jnp.float32),
                pltpu.VMEM((seq, 128), jnp.float32),
                pltpu.VMEM((seq, 128), jnp.float32),
            ],
        ),
        compiler_params=pltpu.CompilerParams(vmem_limit_bytes=32 << 20),
        cost_estimate=pl.CostEstimate(
            flops=16 * seq * seq * width, bytes_accessed=16 * seq * width, transcendentals=seq * seq * pairs
        ),
        name="attend_backward",
    )(table, qkv, qkv, qkv, grad, lse, code, seg)


def swap(values, axis, bit):
    size = lax.axis_size(axis)
    return lax.ppermute(values, axis, [(i, i ^ (1 << bit)) for i in range(size)])


def bits_of(axis):
    return int(math.log2(lax.axis_size(axis)))


def pick(values, bit_set, axis=0):
    half = values.shape[axis] // 2
    keep = lax.dynamic_slice_in_dim(values, bit_set * half, half, axis)
    send = lax.dynamic_slice_in_dim(values, (1 - bit_set) * half, half, axis)
    return keep, send


def join(mine, other, bit_set, axis=0):
    low = jnp.where(bit_set == 0, mine, other)
    high = jnp.where(bit_set == 0, other, mine)
    return jnp.concatenate([low, high], axis=axis)


def reduce_rows(pieces):
    low = jnp.bfloat16
    from_core = swap(jnp.stack([pieces[1], pieces[3]]).astype(low), "tensor", 0)
    away = (pieces[2] + from_core[1].astype(jnp.float32)).astype(low)
    from_y = swap(away, "tensor", 1)
    total = pieces[0] + from_core[0].astype(jnp.float32) + from_y.astype(jnp.float32)
    place = lax.axis_index("dp")
    count = bits_of("dp")
    sides = [(place >> bit) & 1 for bit in range(count)]
    for bit in range(count):
        keep, send = pick(total, sides[bit])
        total = keep + swap(send.astype(low), "dp", bit).astype(jnp.float32)
    total = total.astype(low)
    for bit in reversed(range(count)):
        total = join(total, swap(total, "dp", bit), sides[bit])
    return total.astype(jnp.float32)


def reduce_all(values):
    for bit in range(bits_of("tensor")):
        values = values + swap(values, "tensor", bit)
    for bit in range(bits_of("dp")):
        values = values + swap(values, "dp", bit)
    return values


def gather(own):
    far = swap(own, "tensor", 1)
    return [own, swap(own, "tensor", 0), far, swap(far, "tensor", 0)]


def per_device(
    inputs,
    w_qkv,
    b_qv,
    w_out,
    w_in,
    b_in,
    w_back,
    norm_gains,
    shifts,
    segment_ids,
    valid_lengths,
    teacher,
):
    own_seqs, seq_len, width = inputs.shape
    assert own_seqs == 1 and lax.axis_size("tensor") == 4
    total_slots = seq_len * lax.axis_size("tensor") * lax.axis_size("dp")
    low = jnp.bfloat16
    index = lax.axis_index("tensor")
    x_rows = inputs.reshape(seq_len, width)
    valid = lax.dynamic_index_in_dim(valid_lengths, index, keepdims=False)
    segments = lax.dynamic_index_in_dim(segment_ids, index, keepdims=False)
    positions = jnp.arange(seq_len, dtype=jnp.int32)
    live = positions < valid
    live_mask = live.astype(jnp.float32)
    code = jnp.where(live, segments, -1)[:, None]
    seg = segments[None, :]
    table = span_tables(segments, valid, seq_len)
    token_count = jnp.sum(valid_lengths)
    for bit in range(bits_of("dp")):
        token_count = token_count + swap(token_count, "dp", bit)
    token_count = token_count.astype(jnp.float32)

    qkv_parts = gather(w_qkv.astype(low))
    bias_parts = gather(jnp.concatenate([b_qv.reshape(-1), b_in]))
    out_parts = gather(w_out.astype(low))
    in_parts = gather(w_in.astype(low))
    back_parts = gather(w_back.astype(low))
    piece = w_qkv.shape[2]
    bias_in = jnp.concatenate([part[2 * piece :] for part in bias_parts])
    out_low = jnp.concatenate(out_parts, axis=0)
    in_low = jnp.concatenate(in_parts, axis=1)
    back_low = jnp.concatenate(back_parts, axis=0)

    x_low = x_rows.astype(low)
    groups = []
    for parts, biases in ((qkv_parts[:2], bias_parts[:2]), (qkv_parts[2:], bias_parts[2:])):
        weights = jnp.concatenate([part[i] for i in range(3) for part in parts], axis=1)
        bias = jnp.concatenate(
            [part[:piece] for part in biases]
            + [jnp.zeros((2 * piece,), jnp.float32)]
            + [part[piece : 2 * piece] for part in biases]
        )
        qkv = (matmul_f32(x_low, weights) + bias).astype(low)
        context, lse = attend_forward(table, qkv, code, seg)
        groups.append((weights, qkv, context, lse))
    context_low = jnp.concatenate([group[2] for group in groups], axis=1)

    attn_rows = matmul_f32(context_low, out_low)
    mid_state, norm_one_back = jax.vjp(
        layer_norm, attn_rows + shifts[0] + x_rows, norm_gains[0], shifts[1]
    )
    mid_low = mid_state.astype(low)
    hidden, gelu_back = jax.vjp(exact_gelu, matmul_f32(mid_low, in_low) + bias_in)
    hidden_low = hidden.astype(low)
    ffn_rows = matmul_f32(hidden_low, back_low)
    output, norm_two_back = jax.vjp(
        layer_norm, ffn_rows + shifts[2] + mid_state, norm_gains[1], shifts[3]
    )
    distance = output - teacher.reshape(seq_len, width)
    squared_sum = jnp.sum(live_mask * jnp.sum(distance * distance, axis=-1))
    out_grad = total_slots / token_count * live_mask[:, None] * distance
    dh_two, gain_two, shift_two = norm_two_back(out_grad)
    dh_two_low = dh_two.astype(low)
    hidden_grad = right_cross(dh_two_low, back_low)
    grad_w_back = left_cross(hidden_low, dh_two_low)
    (pre_grad,) = gelu_back(hidden_grad)
    pre_grad_low = pre_grad.astype(low)
    grad_b_in = jnp.sum(pre_grad_low.astype(jnp.float32), axis=0)
    grad_w_in = left_cross(mid_low, pre_grad_low)
    units = w_in.shape[1]
    grad_w_back = reduce_rows([grad_w_back[i * units : (i + 1) * units] for i in range(4)])
    grad_w_in = reduce_rows([grad_w_in[:, i * units : (i + 1) * units] for i in range(4)])

    mid_grad = right_cross(pre_grad_low, in_low) + dh_two
    dh_one, gain_one, shift_one = norm_one_back(mid_grad)
    dh_one_low = dh_one.astype(low)
    context_grad = right_cross(dh_one_low, out_low).astype(low)
    grad_w_out = left_cross(context_low, dh_one_low)
    grad_w_out = reduce_rows([grad_w_out[i * piece : (i + 1) * piece] for i in range(4)])

    pieces = [None] * 4
    bias_pieces = [None] * 4
    grad_inputs = dh_one
    for at in (1, 0):
        weights, qkv, context, lse = groups[at]
        half = 2 * piece
        grads = attend_backward(
            table, qkv, context_grad[:, at * half : (at + 1) * half], lse, code, seg
        )
        crosses = [left_cross(x_low, grad) for grad in grads]
        sums = [jnp.sum(grads[i].astype(jnp.float32), axis=0) for i in (0, 2)]
        for side in range(2):
            cols = slice(side * piece, (side + 1) * piece)
            pieces[2 * at + side] = jnp.concatenate([c[:, cols] for c in crosses], axis=1)
            bias_pieces[2 * at + side] = jnp.concatenate([s[cols] for s in sums])
        grad_inputs = grad_inputs + right_cross(jnp.concatenate(grads, axis=1), weights)
    grad_w_qkv = reduce_rows(pieces)
    grad_w_qkv = grad_w_qkv.reshape(width, 3, piece).transpose(1, 0, 2)

    bias_grads = jnp.stack(
        [
            jnp.concatenate([bias_pieces[i], grad_b_in[i * units : (i + 1) * units]])
            for i in range(4)
        ]
    )
    wide = bias_grads.shape[1]
    bias_grads = jnp.stack([bias_grads[0], bias_grads[1], bias_grads[2], bias_grads[3]])
    natural = lax.dynamic_index_in_dim(
        jnp.stack([jnp.stack([bias_grads[i ^ j] for i in range(4)]) for j in range(4)]),
        index,
        keepdims=False,
    )
    small = jnp.concatenate(
        [
            natural.reshape(-1),
            gain_one,
            gain_two,
            jnp.sum(dh_one, axis=0),
            shift_one,
            jnp.sum(dh_two, axis=0),
            shift_two,
            squared_sum[None],
        ]
    )
    small = reduce_all(small)
    own = lax.dynamic_slice_in_dim(small, index * wide, wide)
    rest = small[4 * wide :]
    grad_gains = rest[: 2 * width].reshape(2, width)
    grad_shifts = rest[2 * width : 6 * width].reshape(4, width)
    loss = rest[6 * width] / (2.0 * width * token_count)
    return (
        output.reshape(own_seqs, seq_len, width),
        loss,
        grad_inputs.reshape(own_seqs, seq_len, width),
        grad_w_qkv,
        own[: 2 * piece].reshape(2, piece),
        grad_w_out,
        grad_w_in,
        own[2 * piece :],
        grad_w_back,
        grad_gains,
        grad_shifts,
    )


def solution(mesh):
    return jax.shard_map(
        per_device,
        mesh=mesh,
        in_specs=(
            P(("dp", "tensor"), None, None),
            P(None, None, "tensor"),
            P(None, "tensor"),
            P("tensor", None),
            P(None, "tensor"),
            P("tensor"),
            P("tensor", None),
            P(),
            P(),
            P("dp", None),
            P("dp"),
            P(("dp", "tensor"), None, None),
        ),
        out_specs=(
            P(("dp", "tensor"), None, None),
            P(),
            P(("dp", "tensor"), None, None),
            P(None, None, "tensor"),
            P(None, "tensor"),
            P("tensor", None),
            P(None, "tensor"),
            P("tensor"),
            P("tensor", None),
            P(),
            P(),
        ),
        check_vma=False,
    )
```

time: 870 us -> 497 us (0.57)
  blocking collectives: 381 us -> 0 us
  matrix products: 262 us -> 127 us
  starting transfers between devices: 0.58 us -> 85.7 us
  Pallas kernels: 0 us -> 67 us
  other arithmetic: 98 us -> 48.1 us
  waiting for transfers between devices: 78.2 us -> 109 us
  local copies, waits for them, and re-layouts: 27.6 us -> 48.7 us
  between operations: 19.6 us -> 7.05 us
    psum x3 -> x0, blocking collectives: 362 us -> none  [the longest x1 279 us: per_device(): lax.psum((grad_w_qkv, grad_b_qv, grad_w_out, grad_w_in, grad_b_in, grad_w...]
    dot_general x12 -> x0, matrix products: 130 us -> none  [the longest x2 39.5 us: attend_backward(): jnp.einsum('qhd,khd->hqk', grad_block, values, preferred_element_type=jnp...]
    ppermute x0 -> x55, waiting for transfers between devices: none -> 109 us  [swap(): return lax.ppermute(values, axis, [(i, i ^ 1 << bit) for i in range(size)])]
    ppermute x0 -> x55, starting transfers between devices: none -> 85.7 us  [swap(): return lax.ppermute(values, axis, [(i, i ^ 1 << bit) for i in range(size)])]
    reduce_scatter x4 -> x0, waiting for transfers between devices: 78 us -> none  [the longest x1 50.6 us: per_device(): lax.psum_scatter(grad_w_back.astype(jnp.bfloat16), 'tensor', scatter_dime...]
    pallas_call x0 -> x4, Pallas kernels: none -> 67 us  [the longest x2 36.2 us: attend_backward(): pl.pallas_call(backward_kernel, out_shape=(jax.ShapeDtypeStruct((seq, wid...]
    convert_element_type x7 -> x16, other arithmetic: 50.6 us -> 18.4 us  [the longest x4 4.77 us: reduce_rows(): away = (pieces[2] + from_core[1].astype(jnp.float32)).astype(low)]
    reduce_sum x3 -> x6, other arithmetic: 25.5 us -> 2.19 us  [the longest x1 1.29 us: per_device(): token_count = jnp.sum(valid_lengths)]
  transfers between devices with their start and end apart: 9 -> 55, of which waited for: 2 -> 23; matrix products, arithmetic and copies ran while one was open for 23% -> 26% of each run, Pallas kernels for 0% -> 6%
where the time goes in v1:
time: 497 us; the launch traced here: 492 us
  matrix products  127 us (26%)
  waiting for transfers between devices  109 us (22%)
  starting transfers between devices  85.7 us (17%)
  Pallas kernels  67 us (13%)
  local copies, waits for them, and re-layouts  48.7 us (10%)
  other arithmetic  48.1 us (10%)
  between operations  7.05 us (1%)
    ppermute x55, waiting for transfers between devices, swap(): return lax.ppermute(values, axis, [(i, i ^ 1 << bit) for i in range(size)])  109 us
    ppermute x55, starting transfers between devices, swap(): return lax.ppermute(values, axis, [(i, i ^ 1 << bit) for i in range(size)])  85.7 us
    dot_general x5, matrix products, matmul_f32(): return jnp.dot(left, right, preferred_element_type=jnp.float32)  56.9 us
    dot_general x5, matrix products, right_cross(): jnp.einsum('ne,de->nd', left, right, preferred_element_type=jnp.float32)  38.6 us
    pallas_call x2, Pallas kernels, attend_backward(): pl.pallas_call(backward_kernel, out_shape=(jax.ShapeDtypeStruct((seq, wid...  36.2 us
    unnamed x173, local copies, waits for them, and re-layouts  34.6 us
    dot_general x9, matrix products, left_cross(): jnp.einsum('nd,ne->de', left, right, preferred_element_type=jnp.float32)  31.4 us
    pallas_call x2, Pallas kernels, attend_forward(): pl.pallas_call(forward_kernel, out_shape=(jax.ShapeDtypeStruct((seq, widt...  30.8 us
  transfers between devices with their start and end apart: 55, of which 23 were waited for; matrix products, arithmetic and copies ran while one was open for 26% of the time, Pallas kernels for 6%

profile of v1, /device:TPU:0, one launch (start us, length us, event | category | flops | bytes accessed | tf_op | source)
XLA Modules:
  0.0 492.2 jit_solution(12020574709492654542)
XLA Ops:
  25.9 3.6 copy.46
  36.9 4.0 collective-permute-start.17
  55.8 3.7 fusion.6.q_ref.k_ref.v_ref
  59.6 15.3 %attend_forward.2 = (bf16[1024,384]{1,0:T(8,128)(2,1)S(1)}, f32[3,8,1024]{2,1,0:T(8,128)S(1)}) custom-call(s32[2,4]{1,0:T(2,128)S(1)} %pad_add_fusion.table_ref, bf16[1024,1152]{1,0:T(8,128)(2,1)S(1)} %fusion.6.q_ref.k_ref.v_ref, bf16[1024,1152]{1,0:T(8,128)(2,1)S(1)} %fusion.6.q_ref.k_ref.v_ref, bf16[1024,1152]{1,0:T(8,128)(2,1)S(1)} %fusion.6.q_ref.k_ref.v_ref, ...), custom_call_target="tpu_custom_call" | custom-call | flops 3221225472 | bytes 3145728 | tf_op jit(solution)/shard_map/attend_forward/pallas_call | solution.py:169
  85.5 15.5 %attend_forward.3 = (bf16[1024,384]{1,0:T(8,128)(2,1)S(1)}, f32[3,8,1024]{2,1,0:T(8,128)S(1)}) custom-call(s32[2,4]{1,0:T(2,128)S(1)} %pad_add_fusion.table_ref, bf16[1024,1152]{1,0:T(8,128)(2,1)S(1)} %fusion.7.q_ref.k_ref.v_ref, bf16[1024,1152]{1,0:T(8,128)(2,1)S(1)} %fusion.7.q_ref.k_ref.v_ref, bf16[1024,1152]{1,0:T(8,128)(2,1)S(1)} %fusion.7.q_ref.k_ref.v_ref, ...), custom_call_target="tpu_custom_call" | custom-call | flops 3221225472 | bytes 3145728 | tf_op jit(solution)/shard_map/attend_forward/pallas_call | solution.py:169
  109.7 39.3 %multiply_convert_fusion = (bf16[1024,3072]{1,0:T(8,128)(2,1)}, f32[1024,3072]{1,0:T(8,128)}, f32[1024,3072]{1,0:T(8,128)}) fusion(f32[3072]{0:T(1024)S(1)} %pad_maximum_fusion.21, bf16[768,768]{1,0:T(8,128)(2,1)S(1)} %collective-permute-done.11, bf16[768,768]{1,0:T(8,128)(2,1)} %collective-permute-done.10, bf16[768,768]{1,0:T(8,128)(2,1)S(1)} %collective-permute-done.9, ...), kind=kOutput, calls=%fused_computation.4 | convolution fusion | flops 5062262784 | bytes 39348224 | tf_op jit(solution)/shard_map/dot_general | solution.py:30
  150.5 9.0 %fusion.81 = (f32[1024]{0:T(1024)S(1)}, f32[1024,768]{0,1:T(8,128)S(1)}) fusion(f32[768]{0:T(1024)S(1)} %copy-done.56, f32[768]{0:T(1024)S(1)} %copy-done.50, f32[1024]{0:T(1024)S(1)} %fusion.52, f32[1024,768]{0,1:T(8,128)S(1)} %get-tuple-element.146, f32[1024]{0:T(1024)S(1)} %broadcast_multiply_fusion.1, f32[768]{0:T(1024)S(1)} %copy-done.57, ...), kind=kOutput, calls=%fused_computation.284 | convolution fusion | flops 4856216576 | bytes 17323008 | tf_op jit(solution)/shard_map/dot_general | solution.py:30
  168.5 18.8 %convert_reduce_fusion = (f32[3072]{0:T(1024)S(1)}, bf16[1024,3072]{1,0:T(8,128)(2,1)}) fusion(f32[1024,3072]{1,0:T(8,128)} %get-tuple-element.85, bf16[768,768]{1,0:T(8,128)(2,1)} %copy-done.64, bf16[768,768]{1,0:T(8,128)(2,1)} %copy-done.60, bf16[768,768]{1,0:T(8,128)(2,1)} %copy-done.63, bf16[768,768]{1,0:T(8,128)(2,1)S(1)} %copy-done.37, ...), kind=kOutput, calls=%fused_computation.2 | convolution fusion | flops 4905759744 | bytes 39350272 | tf_op jit(solution)/shard_map/ne,de->nd/dot_general | solution.py:38
  187.3 10.7 %multiply_reduce_fusion.2 = (f32[768]{0:T(1024)S(1)}, f32[1024]{0:T(1024)S(1)}, f32[768]{0:T(1024)S(1)}, f32[1024,768]{0,1:T(8,128)S(1)}) fusion(f32[1024,768]{0,1:T(8,128)} %copy-done.23, f32[1024]{0:T(1024)S(1)} %fusion.52, f32[1024]{0:T(1024)S(1)} %broadcast_multiply_fusion.1, f32[768]{0:T(1024)S(1)} %copy-done.50, f32[1024,768]{0,1:T(8,128)} %get-tuple-element.82, ...), kind=kOutput, calls=%fused_computation.32 | convolution fusion | flops 4858573824 | bytes 20472832 | tf_op jit(solution)/shard_map/ne,de->nd/dot_general | solution.py:38
  204.6 17.9 %attend_backward.2 = (bf16[1024,384]{1,0:T(8,128)(2,1)S(1)}, bf16[1024,384]{1,0:T(8,128)(2,1)S(1)}, bf16[1024,384]{1,0:T(8,128)(2,1)S(1)}) custom-call(s32[2,4]{1,0:T(2,128)S(1)} %pad_add_fusion.table_ref, bf16[1024,1152]{1,0:T(8,128)(2,1)S(1)} %copy-done.13, bf16[1024,1152]{1,0:T(8,128)(2,1)S(1)} %copy-done.13, bf16[1024,1152]{1,0:T(8,128)(2,1)S(1)} %copy-done.13, ...), custom_call_target="tpu_custom_call" | custom-call | flops 6442450944 | bytes 6291456 | tf_op jit(solution)/shard_map/attend_backward/pallas_call | solution.py:206
  226.6 18.3 %attend_backward.3 = (bf16[1024,384]{1,0:T(8,128)(2,1)S(1)}, bf16[1024,384]{1,0:T(8,128)(2,1)S(1)}, bf16[1024,384]{1,0:T(8,128)(2,1)S(1)}) custom-call(s32[2,4]{1,0:T(2,128)S(1)} %copy-done.7, bf16[1024,1152]{1,0:T(8,128)(2,1)S(1)} %copy-done.15, bf16[1024,1152]{1,0:T(8,128)(2,1)S(1)} %copy-done.15, bf16[1024,1152]{1,0:T(8,128)(2,1)S(1)} %copy-done.15, ...), custom_call_target="tpu_custom_call" | custom-call | flops 6442450944 | bytes 6291456 | tf_op jit(solution)/shard_map/attend_backward/pallas_call | solution.py:206
  252.2 8.7 %fusion.83 = (bf16[768,3072]{1,0:T(8,128)(2,1)}, f32[768,3072]{1,0:T(8,128)}) fusion(bf16[1024,3072]{1,0:T(8,128)(2,1)S(1)} %bitcast.204, f32[1024,768]{0,1:T(8,128)S(1)} %copy-done.24, f32[768]{0:T(1024)S(1)} %copy-done.56, f32[768]{0:T(1024)S(1)} %copy-done.50, f32[1024]{0:T(1024)S(1)} %fusion.52, f32[1024]{0:T(1024)S(1)} %broadcast_multiply_fusion.1), kind=kOutput, calls=%fused_computation.286 | convolution fusion | flops 4838129664 | bytes 23607296 | tf_op jit(solution)/shard_map/nd,ne->de/dot_general | solution.py:34
  260.9 8.7 %fusion.84 = (bf16[3072,768]{1,0:T(8,128)(2,1)}, f32[3072,768]{1,0:T(8,128)}) fusion(bf16[1024,3072]{1,0:T(8,128)(2,1)S(1)} %bitcast.202, f32[1024,768]{0,1:T(8,128)S(1)} %copy-done.21, f32[1024]{0:T(1024)S(1)} %negate_multiply_fusion.2), kind=kOutput, calls=%fused_computation.287 | convolution fusion | flops 4835770368 | bytes 23597056 | tf_op jit(solution)/shard_map/nd,ne->de/dot_general | solution.py:34
  282.9 4.2 collective-permute-start.32
  287.4 7.2 %collective-permute-done.32 = bf16[192,768]{1,0:T(8,128)(2,1)S(1)} collective-permute-done((bf16[192,768]{1,0:T(8,128)(2,1)S(1)}, bf16[192,768]{1,0:T(8,128)(2,1)S(1)}, u32[]{:S(2)}, u32[]{:S(2)}) %collective-permute-start.32) | collective-permute-done | bytes 294944 | tf_op jit(solution)/shard_map/ppermute | solution.py:243
  294.7 4.1 collective-permute-start.33
  302.7 4.5 collective-permute-start.34
  309.7 5.9 %collective-permute-start.35 = (bf16[24,768]{1,0:T(8,128)(2,1)S(1)}, bf16[24,768]{1,0:T(8,128)(2,1)S(1)}, u32[]{:S(2)}, u32[]{:S(2)}) collective-permute-start(bf16[24,768]{1,0:T(8,128)(2,1)S(1)} %dynamic-slice_convert_fusion.11), channel_id=1, source_target_pairs={{0,16},{4,20},{8,24},{12,28},{16,0},{20,4},{24,8},{28,12},{1,17},{... | collective-permute-start | bytes 110600 | tf_op jit(solution)/shard_map/ppermute | solution.py:243
  330.1 9.7 %collective-permute-done.24 = bf16[768,576]{0,1:T(8,128)(2,1)S(1)} collective-permute-done((bf16[768,576]{0,1:T(8,128)(2,1)S(1)}, bf16[768,576]{0,1:T(8,128)(2,1)S(1)}, u32[]{:S(2)}, u32[]{:S(2)}) %collective-permute-start.24) | collective-permute-done | bytes 884768 | tf_op jit(solution)/shard_map/ppermute | solution.py:243
  342.7 4.2 add_bitcast_fusion
  350.5 3.8 copy.51
  368.5 3.6 collective-permute-start.27
  379.4 4.5 collective-permute-done.28
  386.7 7.7 %collective-permute-done.40 = bf16[768,768]{1,0:T(8,128)(2,1)S(1)} collective-permute-done((bf16[768,768]{1,0:T(8,128)(2,1)S(1)}, bf16[768,768]{1,0:T(8,128)(2,1)S(1)}, u32[]{:S(2)}, u32[]{:S(2)}) %collective-permute-start.40) | collective-permute-done | bytes 1179680 | tf_op jit(solution)/shard_map/ppermute | solution.py:243
  397.3 18.9 %collective-permute-done.48 = bf16[768,768]{1,0:T(8,128)(2,1)S(1)} collective-permute-done((bf16[768,768]{1,0:T(8,128)(2,1)S(1)}, bf16[768,768]{1,0:T(8,128)(2,1)S(1)}, u32[]{:S(2)}, u32[]{:S(2)}) %collective-permute-start.48) | collective-permute-done | bytes 1179680 | tf_op jit(solution)/shard_map/ppermute | solution.py:243
  421.8 13.2 %collective-permute-done.49 = bf16[384,768]{1,0:T(8,128)(2,1)S(1)} collective-permute-done((bf16[384,768]{1,0:T(8,128)(2,1)S(1)}, bf16[384,768]{1,0:T(8,128)(2,1)S(1)}, u32[]{:S(2)}, u32[]{:S(2)}) %collective-permute-start.49) | collective-permute-done | bytes 589856 | tf_op jit(solution)/shard_map/ppermute | solution.py:243
  435.6 3.6 collective-permute-start.43
  439.2 5.7 %collective-permute-done.50 = bf16[192,768]{1,0:T(8,128)(2,1)S(1)} collective-permute-done((bf16[192,768]{1,0:T(8,128)(2,1)S(1)}, bf16[192,768]{1,0:T(8,128)(2,1)S(1)}, u32[]{:S(2)}, u32[]{:S(2)}) %collective-permute-start.50) | collective-permute-done | bytes 294944 | tf_op jit(solution)/shard_map/ppermute | solution.py:243
  448.1 6.4 %collective-permute-done.51 = bf16[96,768]{1,0:T(8,128)(2,1)S(1)} collective-permute-done((bf16[96,768]{1,0:T(8,128)(2,1)S(1)}, bf16[96,768]{1,0:T(8,128)(2,1)S(1)}, u32[]{:S(2)}, u32[]{:S(2)}) %collective-permute-start.51) | collective-permute-done | bytes 147488 | tf_op jit(solution)/shard_map/ppermute | solution.py:243
  460.9 4.1 collective-permute-start.53
  472.8 9.9 %collective-permute-done.46 = bf16[384,768]{1,0:T(8,128)(2,1)S(1)} collective-permute-done((bf16[384,768]{1,0:T(8,128)(2,1)S(1)}, bf16[384,768]{1,0:T(8,128)(2,1)S(1)}, u32[]{:S(2)}, u32[]{:S(2)}) %collective-permute-start.46) | collective-permute-done | bytes 589856 | tf_op jit(solution)/shard_map/ppermute | solution.py:243
  484.4 4.5 collective-permute-done.54
  (446 shorter events, 185.7 us)
Async XLA Ops:
  3.2 43.5 %collective-permute-start = (bf16[3,768,192]{1,2,0:T(8,128)(2,1)}, bf16[3,768,192]{1,2,0:T(8,128)(2,1)}, u32[]{:S(2)}, u32[]{:S(2)}) collective-permute-start(bf16[3,768,192]{1,2,0:T(8,128)(2,1)} %convert_element_type.242), channel_id=1, source_target_pairs={{0,1},{1,0},{2,3},{3,2},{4,5},{5,4},{6,7},{7,6},{8,9},{9,8},{10,11... | collective-permute-start | bytes 2654216 | tf_op jit(solution)/shard_map/ppermute | solution.py:243
  3.6 51.7 %collective-permute-start.2 = (bf16[3,768,192]{1,2,0:T(8,128)(2,1)}, bf16[3,768,192]{1,2,0:T(8,128)(2,1)}, u32[]{:S(2)}, u32[]{:S(2)}) collective-permute-start(bf16[3,768,192]{1,2,0:T(8,128)(2,1)} %convert_element_type.242), channel_id=1, source_target_pairs={{0,2},{1,3},{2,0},{3,1},{4,6},{5,7},{6,4},{7,5},{8,10},{9,11},{10,... | collective-permute-start | bytes 2654216 | tf_op jit(solution)/shard_map/ppermute | solution.py:243
  7.6 36.9 %collective-permute-start.1 = (f32[1152]{0:T(1024)S(1)}, f32[1152]{0:T(1024)S(1)}, u32[]{:S(2)}, u32[]{:S(2)}) collective-permute-start(f32[1152]{0:T(1024)S(1)} %constant_dynamic-update-slice_fusion.4), channel_id=1, source_target_pairs={{0,1},{1,0},{2,3},{3,2},{4,5},{5,4},{6,7},{7,6},{8,9},{9,8},{10,11... | collective-permute-start | bytes 13832 | tf_op jit(solution)/shard_map/ppermute | solution.py:243
  7.9 36.5 %collective-permute-start.4 = (f32[1152]{0:T(1024)S(1)}, f32[1152]{0:T(1024)S(1)}, u32[]{:S(2)}, u32[]{:S(2)}) collective-permute-start(f32[1152]{0:T(1024)S(1)} %constant_dynamic-update-slice_fusion.4), channel_id=1, source_target_pairs={{0,2},{1,3},{2,0},{3,1},{4,6},{5,7},{6,4},{7,5},{8,10},{9,11},{10,... | collective-permute-start | bytes 13832 | tf_op jit(solution)/shard_map/ppermute | solution.py:243
  9.4 21.9 %collective-permute-start.15 = (s32[]{:T(128)}, s32[]{:T(128)}, u32[]{:S(2)}, u32[]{:S(2)}) collective-permute-start(s32[]{:T(128)} %reduce_sum.257), channel_id=1, source_target_pairs={{0,4},{4,0},{8,12},{12,8},{16,20},{20,16},{24,28},{28,24},{1,5},{5... | collective-permute-start | bytes 20 | tf_op jit(solution)/shard_map/ppermute | solution.py:243
  41.5 34.6 %collective-permute-start.7 = (bf16[192,768]{1,0:T(8,128)(2,1)S(1)}, bf16[192,768]{1,0:T(8,128)(2,1)}, u32[]{:S(2)}, u32[]{:S(2)}) collective-permute-start(bf16[192,768]{1,0:T(8,128)(2,1)S(1)} %convert_element_type.248), channel_id=1, source_target_pairs={{0,2},{1,3},{2,0},{3,1},{4,6},{5,7},{6,4},{7,5},{8,10},{9,11},{10,... | collective-permute-start | bytes 884744 | tf_op jit(solution)/shard_map/ppermute | solution.py:243
  44.4 56.8 %collective-permute-start.6 = (bf16[192,768]{1,0:T(8,128)(2,1)S(1)}, bf16[192,768]{1,0:T(8,128)(2,1)}, u32[]{:S(2)}, u32[]{:S(2)}) collective-permute-start(bf16[192,768]{1,0:T(8,128)(2,1)S(1)} %convert_element_type.248), channel_id=1, source_target_pairs={{0,1},{1,0},{2,3},{3,2},{4,5},{5,4},{6,7},{7,6},{8,9},{9,8},{10,11... | collective-permute-start | bytes 884744 | tf_op jit(solution)/shard_map/ppermute | solution.py:243
  46.0 56.7 %collective-permute-start.10 = (bf16[768,768]{1,0:T(8,128)(2,1)}, bf16[768,768]{1,0:T(8,128)(2,1)}, u32[]{:S(2)}, u32[]{:S(2)}) collective-permute-start(bf16[768,768]{1,0:T(8,128)(2,1)} %convert_element_type.250), channel_id=1, source_target_pairs={{0,2},{1,3},{2,0},{3,1},{4,6},{5,7},{6,4},{7,5},{8,10},{9,11},{10,... | collective-permute-start | bytes 3538952 | tf_op jit(solution)/shard_map/ppermute | solution.py:243
  46.7 61.3 %collective-permute-start.9 = (bf16[768,768]{1,0:T(8,128)(2,1)}, bf16[768,768]{1,0:T(8,128)(2,1)S(1)}, u32[]{:S(2)}, u32[]{:S(2)}) collective-permute-start(bf16[768,768]{1,0:T(8,128)(2,1)} %convert_element_type.250), channel_id=1, source_target_pairs={{0,1},{1,0},{2,3},{3,2},{4,5},{5,4},{6,7},{7,6},{8,9},{9,8},{10,11... | collective-permute-start | bytes 3538952 | tf_op jit(solution)/shard_map/ppermute | solution.py:243
  55.3 22.4 %collective-permute-start.3 = (bf16[3,768,192]{1,2,0:T(8,128)(2,1)}, bf16[3,768,192]{1,2,0:T(8,128)(2,1)S(1)}, u32[]{:S(2)}, u32[]{:S(2)}) collective-permute-start(bf16[3,768,192]{1,2,0:T(8,128)(2,1)} %collective-permute-done.2), channel_id=1, source_target_pairs={{0,1},{1,0},{2,3},{3,2},{4,5},{5,4},{6,7},{7,6},{8,9},{9,8},{10,11... | collective-permute-start | bytes 2654216 | tf_op jit(solution)/shard_map/ppermute | solution.py:243
  76.1 27.6 %collective-permute-start.13 = (bf16[768,768]{1,0:T(8,128)(2,1)S(1)}, bf16[768,768]{1,0:T(8,128)(2,1)S(1)}, u32[]{:S(2)}, u32[]{:S(2)}) collective-permute-start(bf16[768,768]{1,0:T(8,128)(2,1)S(1)} %copy-done.36), channel_id=1, source_target_pairs={{0,2},{1,3},{2,0},{3,1},{4,6},{5,7},{6,4},{7,5},{8,10},{9,11},{10,... | collective-permute-start | bytes 3538952 | tf_op jit(solution)/shard_map/ppermute | solution.py:243
  77.7 27.1 %collective-permute-start.8 = (bf16[192,768]{1,0:T(8,128)(2,1)}, bf16[192,768]{1,0:T(8,128)(2,1)S(1)}, u32[]{:S(2)}, u32[]{:S(2)}) collective-permute-start(bf16[192,768]{1,0:T(8,128)(2,1)} %collective-permute-done.7), channel_id=1, source_target_pairs={{0,1},{1,0},{2,3},{3,2},{4,5},{5,4},{6,7},{7,6},{8,9},{9,8},{10,11... | collective-permute-start | bytes 884744 | tf_op jit(solution)/shard_map/ppermute | solution.py:243
  101.2 47.8 %collective-permute-start.12 = (bf16[768,768]{1,0:T(8,128)(2,1)S(1)}, bf16[768,768]{1,0:T(8,128)(2,1)S(1)}, u32[]{:S(2)}, u32[]{:S(2)}) collective-permute-start(bf16[768,768]{1,0:T(8,128)(2,1)S(1)} %copy-done.36), channel_id=1, source_target_pairs={{0,1},{1,0},{2,3},{3,2},{4,5},{5,4},{6,7},{7,6},{8,9},{9,8},{10,11... | collective-permute-start | bytes 3538952 | tf_op jit(solution)/shard_map/ppermute | solution.py:243
  103.7 45.3 %collective-permute-start.14 = (bf16[768,768]{1,0:T(8,128)(2,1)S(1)}, bf16[768,768]{1,0:T(8,128)(2,1)S(1)}, u32[]{:S(2)}, u32[]{:S(2)}) collective-permute-start(bf16[768,768]{1,0:T(8,128)(2,1)S(1)} %collective-permute-done.13), channel_id=1, source_target_pairs={{0,1},{1,0},{2,3},{3,2},{4,5},{5,4},{6,7},{7,6},{8,9},{9,8},{10,11... | collective-permute-start | bytes 3538952 | tf_op jit(solution)/shard_map/ppermute | solution.py:243
  275.4 45.1 %collective-permute-start.23 = (bf16[2,768,576]{1,2,0:T(8,128)(2,1)S(1)}, bf16[2,768,576]{1,2,0:T(8,128)(2,1)S(1)}, u32[]{:S(2)}, u32[]{:S(2)}) collective-permute-start(bf16[2,768,576]{1,2,0:T(8,128)(2,1)S(1)} %pad_maximum_fusion.4), channel_id=1, source_target_pairs={{0,1},{1,0},{2,3},{3,2},{4,5},{5,4},{6,7},{7,6},{8,9},{9,8},{10,11... | collective-permute-start | bytes 5308424 | tf_op jit(solution)/shard_map/ppermute | solution.py:243
  282.9 11.7 %collective-permute-start.32 = (bf16[192,768]{1,0:T(8,128)(2,1)S(1)}, bf16[192,768]{1,0:T(8,128)(2,1)S(1)}, u32[]{:S(2)}, u32[]{:S(2)}) collective-permute-start(bf16[192,768]{1,0:T(8,128)(2,1)S(1)} %fusion.33), channel_id=1, source_target_pairs={{0,2},{1,3},{2,0},{3,1},{4,6},{5,7},{6,4},{7,5},{8,10},{9,11},{10,... | collective-permute-start | bytes 884744 | tf_op jit(solution)/shard_map/ppermute | solution.py:243
  317.2 46.0 %collective-permute-start.39 = (bf16[2,768,768]{2,1,0:T(8,128)(2,1)}, bf16[2,768,768]{2,1,0:T(8,128)(2,1)}, u32[]{:S(2)}, u32[]{:S(2)}) collective-permute-start(bf16[2,768,768]{2,1,0:T(8,128)(2,1)} %pad_maximum_fusion.2), channel_id=1, source_target_pairs={{0,1},{1,0},{2,3},{3,2},{4,5},{5,4},{6,7},{7,6},{8,9},{9,8},{10,11... | collective-permute-start | bytes 7077896 | tf_op jit(solution)/shard_map/ppermute | solution.py:243
  320.7 19.1 %collective-permute-start.24 = (bf16[768,576]{0,1:T(8,128)(2,1)S(1)}, bf16[768,576]{0,1:T(8,128)(2,1)S(1)}, u32[]{:S(2)}, u32[]{:S(2)}) collective-permute-start(bf16[768,576]{0,1:T(8,128)(2,1)S(1)} %fusion.27), channel_id=1, source_target_pairs={{0,2},{1,3},{2,0},{3,1},{4,6},{5,7},{6,4},{7,5},{8,10},{9,11},{10,... | collective-permute-start | bytes 2654216 | tf_op jit(solution)/shard_map/ppermute | solution.py:243
  326.5 45.7 %collective-permute-start.47 = (bf16[2,768,768]{2,1,0:T(8,128)(2,1)}, bf16[2,768,768]{2,1,0:T(8,128)(2,1)}, u32[]{:S(2)}, u32[]{:S(2)}) collective-permute-start(bf16[2,768,768]{2,1,0:T(8,128)(2,1)} %pad_maximum_fusion.3), channel_id=1, source_target_pairs={{0,1},{1,0},{2,3},{3,2},{4,5},{5,4},{6,7},{7,6},{8,9},{9,8},{10,11... | collective-permute-start | bytes 7077896 | tf_op jit(solution)/shard_map/ppermute | solution.py:243
  326.6 27.7 %collective-permute-start.22 = (f32[9217]{0:T(1024)S(1)}, f32[9217]{0:T(1024)}, u32[]{:S(2)}, u32[]{:S(2)}) collective-permute-start(f32[9217]{0:T(1024)S(1)} %add.329), channel_id=1, source_target_pairs={{0,16},{4,20},{8,24},{12,28},{16,0},{20,4},{24,8},{28,12},{1,17},{... | collective-permute-start | bytes 110612 | tf_op jit(solution)/shard_map/ppermute | solution.py:243
  330.0 28.8 %collective-permute-start.38 = (bf16[96,768]{1,0:T(8,128)(2,1)}, bf16[96,768]{1,0:T(8,128)(2,1)}, u32[]{:S(2)}, u32[]{:S(2)}) collective-permute-start(bf16[96,768]{1,0:T(8,128)(2,1)} %pad_maximum_fusion.19), channel_id=1, source_target_pairs={{0,4},{4,0},{8,12},{12,8},{16,20},{20,16},{24,28},{28,24},{1,5},{5... | collective-permute-start | bytes 442376 | tf_op jit(solution)/shard_map/ppermute | solution.py:243
  341.0 18.9 %collective-permute-start.25 = (bf16[384,576]{0,1:T(8,128)(2,1)}, bf16[384,576]{0,1:T(8,128)(2,1)}, u32[]{:S(2)}, u32[]{:S(2)}) collective-permute-start(bf16[384,576]{0,1:T(8,128)(2,1)} %dynamic-slice_convert_fusion.2), channel_id=1, source_target_pairs={{0,4},{4,0},{8,12},{12,8},{16,20},{20,16},{24,28},{28,24},{1,5},{5... | collective-permute-start | bytes 1327112 | tf_op jit(solution)/shard_map/ppermute | solution.py:243
  365.4 29.0 %collective-permute-start.40 = (bf16[768,768]{1,0:T(8,128)(2,1)S(1)}, bf16[768,768]{1,0:T(8,128)(2,1)S(1)}, u32[]{:S(2)}, u32[]{:S(2)}) collective-permute-start(bf16[768,768]{1,0:T(8,128)(2,1)S(1)} %fusion.12), channel_id=1, source_target_pairs={{0,2},{1,3},{2,0},{3,1},{4,6},{5,7},{6,4},{7,5},{8,10},{9,11},{10,... | collective-permute-start | bytes 3538952 | tf_op jit(solution)/shard_map/ppermute | solution.py:243
  374.4 41.8 %collective-permute-start.48 = (bf16[768,768]{1,0:T(8,128)(2,1)S(1)}, bf16[768,768]{1,0:T(8,128)(2,1)S(1)}, u32[]{:S(2)}, u32[]{:S(2)}) collective-permute-start(bf16[768,768]{1,0:T(8,128)(2,1)S(1)} %fusion.10), channel_id=1, source_target_pairs={{0,2},{1,3},{2,0},{3,1},{4,6},{5,7},{6,4},{7,5},{8,10},{9,11},{10,... | collective-permute-start | bytes 3538952 | tf_op jit(solution)/shard_map/ppermute | solution.py:243
  384.0 35.0 %collective-permute-start.29 = (bf16[192,576]{0,1:T(8,128)(2,1)S(1)}, bf16[192,576]{0,1:T(8,128)(2,1)S(1)}, u32[]{:S(2)}, u32[]{:S(2)}) collective-permute-start(bf16[192,576]{0,1:T(8,128)(2,1)S(1)} %pad_maximum_fusion.14), channel_id=1, source_target_pairs={{0,8},{4,12},{8,0},{12,4},{16,24},{20,28},{24,16},{28,20},{1,9},{5... | collective-permute-start | bytes 663560 | tf_op jit(solution)/shard_map/ppermute | solution.py:243
  396.8 24.4 %collective-permute-start.41 = (bf16[384,768]{1,0:T(8,128)(2,1)S(1)}, bf16[384,768]{1,0:T(8,128)(2,1)S(1)}, u32[]{:S(2)}, u32[]{:S(2)}) collective-permute-start(bf16[384,768]{1,0:T(8,128)(2,1)S(1)} %dynamic-slice_convert_fusion.1), channel_id=1, source_target_pairs={{0,4},{4,0},{8,12},{12,8},{16,20},{20,16},{24,28},{28,24},{1,5},{5... | collective-permute-start | bytes 1769480 | tf_op jit(solution)/shard_map/ppermute | solution.py:243
  418.6 16.3 %collective-permute-start.49 = (bf16[384,768]{1,0:T(8,128)(2,1)S(1)}, bf16[384,768]{1,0:T(8,128)(2,1)S(1)}, u32[]{:S(2)}, u32[]{:S(2)}) collective-permute-start(bf16[384,768]{1,0:T(8,128)(2,1)S(1)} %dynamic-slice_convert_fusion), channel_id=1, source_target_pairs={{0,4},{4,0},{8,12},{12,8},{16,20},{20,16},{24,28},{28,24},{1,5},{5... | collective-permute-start | bytes 1769480 | tf_op jit(solution)/shard_map/ppermute | solution.py:243
  419.5 48.8 %collective-permute-start.30 = (bf16[384,576]{0,1:T(8,128)(2,1)S(1)}, bf16[384,576]{0,1:T(8,128)(2,1)S(1)}, u32[]{:S(2)}, u32[]{:S(2)}) collective-permute-start(bf16[384,576]{0,1:T(8,128)(2,1)S(1)} %pad_maximum_fusion.13), channel_id=1, source_target_pairs={{0,4},{4,0},{8,12},{12,8},{16,20},{20,16},{24,28},{28,24},{1,5},{5... | collective-permute-start | bytes 1327112 | tf_op jit(solution)/shard_map/ppermute | solution.py:243
  421.4 14.1 %collective-permute-start.42 = (bf16[192,768]{1,0:T(8,128)(2,1)S(1)}, bf16[192,768]{1,0:T(8,128)(2,1)S(1)}, u32[]{:S(2)}, u32[]{:S(2)}) collective-permute-start(bf16[192,768]{1,0:T(8,128)(2,1)S(1)} %dynamic-slice_convert_fusion.4), channel_id=1, source_target_pairs={{0,8},{4,12},{8,0},{12,4},{16,24},{20,28},{24,16},{28,20},{1,9},{5... | collective-permute-start | bytes 884744 | tf_op jit(solution)/shard_map/ppermute | solution.py:243
  435.6 12.4 %collective-permute-start.43 = (bf16[96,768]{1,0:T(8,128)(2,1)S(1)}, bf16[96,768]{1,0:T(8,128)(2,1)S(1)}, u32[]{:S(2)}, u32[]{:S(2)}) collective-permute-start(bf16[96,768]{1,0:T(8,128)(2,1)S(1)} %dynamic-slice_convert_fusion.7), channel_id=1, source_target_pairs={{0,16},{4,20},{8,24},{12,28},{16,0},{20,4},{24,8},{28,12},{1,17},{... | collective-permute-start | bytes 442376 | tf_op jit(solution)/shard_map/ppermute | solution.py:243
  467.5 15.2 %collective-permute-start.46 = (bf16[384,768]{1,0:T(8,128)(2,1)S(1)}, bf16[384,768]{1,0:T(8,128)(2,1)S(1)}, u32[]{:S(2)}, u32[]{:S(2)}) collective-permute-start(bf16[384,768]{1,0:T(8,128)(2,1)S(1)} %pad_maximum_fusion.11), channel_id=1, source_target_pairs={{0,4},{4,0},{8,12},{12,8},{16,20},{20,16},{24,28},{28,24},{1,5},{5... | collective-permute-start | bytes 1769480 | tf_op jit(solution)/shard_map/ppermute | solution.py:243
  470.6 18.3 %collective-permute-start.54 = (bf16[384,768]{1,0:T(8,128)(2,1)S(1)}, bf16[384,768]{1,0:T(8,128)(2,1)S(1)}, u32[]{:S(2)}, u32[]{:S(2)}) collective-permute-start(bf16[384,768]{1,0:T(8,128)(2,1)S(1)} %pad_maximum_fusion.12), channel_id=1, source_target_pairs={{0,4},{4,0},{8,12},{12,8},{16,20},{20,16},{24,28},{28,24},{1,5},{5... | collective-permute-start | bytes 1769480 | tf_op jit(solution)/shard_map/ppermute | solution.py:243
  (102 other events, 1597.6 us)

commit v2 on v1

v2 whole, which is shorter than its diff:
```python
import functools
import math

import jax
import jax.numpy as jnp
from jax import lax
from jax.experimental import pallas as pl
from jax.experimental.pallas import tpu as pltpu
from jax.sharding import PartitionSpec as P

HD = 64
LN_EPSILON = 1e-05
MASKED_SCORE = -1000000000.0
QB = 256
KB = 128
RB = 256
FR = 256
NT = ((1,), (1,))
TN = ((0,), (0,))
PHI = (
    0.09255110872,
    0.09001568156,
    0.1049848251,
    0.006341010132,
    0.2381524984,
    -0.2150534404,
    0.2551771707,
    -0.07216888208,
)
PHI_STEP = 0.23164188826636045

VMEM = pl.BlockSpec(memory_space=pltpu.VMEM)
SMEM = pl.BlockSpec(memory_space=pltpu.SMEM)
HBM = pl.BlockSpec(memory_space=pl.ANY)
LOW = jnp.bfloat16
F32 = jnp.float32


def dot(left, right, dims=((1,), (0,))):
    return lax.dot_general(left, right, (dims, ((), ())), preferred_element_type=jnp.float32)


def shape(dims, dtype):
    return jax.ShapeDtypeStruct(dims, dtype)


def three_parts(values):
    first = values.astype(LOW)
    rest = values - first.astype(F32)
    second = rest.astype(LOW)
    return first, second, (rest - second.astype(F32)).astype(LOW)


def round_qkv_kernel(side_ref, w_ref, bqv_ref, bin_ref, out_ref):
    piece = w_ref.shape[2]
    width = w_ref.shape[1]
    half = bin_ref.shape[1] // 2
    for i in range(3):
        out_ref[i * piece : (i + 1) * piece, :] = w_ref[i].T.astype(LOW)
    mine = bin_ref[:, pl.ds(pl.multiple_of(side_ref[0] * half, half), half)]
    other = bin_ref[:, pl.ds(pl.multiple_of((1 - side_ref[0]) * half, half), half)]
    pad = jnp.zeros((1, width - piece), F32)
    rows = [jnp.concatenate([mine, other], axis=1)]
    rows += [jnp.concatenate([bqv_ref[i : i + 1, :], pad], axis=1) for i in range(2)]
    parts = [part.astype(F32) for row in rows for part in three_parts(row)]
    parts += [jnp.zeros((1, width), F32)] * 7
    out_ref[3 * piece :, :] = jnp.concatenate(parts, axis=0).astype(LOW)


def round_qkv(side, w_qkv, b_qv, b_in):
    _, width, piece = w_qkv.shape
    return pl.pallas_call(
        round_qkv_kernel,
        out_shape=shape((3 * piece + 16, width), LOW),
        in_specs=[SMEM, VMEM, VMEM, VMEM],
        out_specs=VMEM,
        name="round_qkv",
    )(side, w_qkv, b_qv, b_in)


def round_rest_kernel(side_ref, wo_ref, wi_ref, wb_ref, x_ref, first_ref, second_ref, x_low_ref):
    rows, width = wo_ref.shape
    half = width // 2
    for c in range(2):
        first_ref[c * rows : (c + 1) * rows, :] = wo_ref[:, c * half : (c + 1) * half].astype(LOW)
    for out, base, side in ((first_ref, 2 * rows, side_ref[0]), (second_ref, 0, 1 - side_ref[0])):
        at = pl.ds(pl.multiple_of(side * half, half), half)
        out[base : base + width, :] = wi_ref[:, at].astype(LOW)
        for c in range(2):
            start = base + width + c * half
            out[start : start + half, :] = wb_ref[at, c * half : (c + 1) * half].astype(LOW)
    x_low_ref[...] = x_ref[...].astype(LOW)


def round_rest(side, w_out, w_in, w_back, x):
    rows, width = w_out.shape
    half = width // 2
    return pl.pallas_call(
        round_rest_kernel,
        out_shape=(
            shape((2 * rows + 2 * width, half), LOW),
            shape((2 * width, half), LOW),
            shape(x.shape, LOW),
        ),
        in_specs=[SMEM, VMEM, VMEM, VMEM, VMEM],
        out_specs=(VMEM, VMEM, VMEM),
        compiler_params=pltpu.CompilerParams(vmem_limit_bytes=40 << 20),
        name="round_rest",
    )(side, w_out, w_in, w_back, x)


def span_tables(segments, valid, seq):
    blocks = seq // QB
    firsts, lasts = segments[::QB], segments[QB - 1 :: QB]
    low = jnp.sum((segments[None, :] < firsts[:, None]).astype(jnp.int32), axis=1)
    high = jnp.sum((segments[None, :] <= lasts[:, None]).astype(jnp.int32), axis=1)
    own_end = (jnp.arange(blocks, dtype=jnp.int32) + 1) * QB
    high = jnp.maximum(jnp.minimum(high, valid), own_end)
    low_block = low // KB
    high_block = (high + KB - 1) // KB
    return jnp.stack([low_block, high_block - low_block]).astype(jnp.int32)


def make_bias(bias_ref, block, low, count, code_ref, seg_ref):
    dims = (count * KB, QB)
    codes = code_ref[pl.ds(pl.multiple_of(low * KB, KB), count * KB), :]
    segs = seg_ref[:, pl.ds(pl.multiple_of(block * QB, QB), QB)]
    key_at = low * KB + lax.broadcasted_iota(jnp.int32, dims, 0)
    query_at = block * QB + lax.broadcasted_iota(jnp.int32, dims, 1)
    allowed = (codes == segs) | (key_at == query_at)
    bias_ref[block, : count * KB, :] = jnp.where(allowed, 0.0, MASKED_SCORE)


def one_head(values, head):
    lane = lax.broadcasted_iota(jnp.int32, values.shape, 1)
    keep = (lane < HD) if head == 0 else (lane >= HD)
    return jnp.where(keep, values, jnp.zeros_like(values))


def forward_kernel(
    table_ref,
    x_ref,
    w0_ref,
    w1_ref,
    code_ref,
    seg_ref,
    q_ref,
    k_ref,
    v_ref,
    ctx_ref,
    lse_ref,
    weights,
    biases,
    vt_ref,
    bias_ref,
):
    pair, block = pl.program_id(0), pl.program_id(1)
    low, total = table_ref[0, block], table_ref[1, block]
    piece = (w0_ref.shape[0] - 16) // 3

    @pl.when((pair == 0) & (block == 0))
    def _():
        for i in range(3):
            for n, ref in enumerate((w0_ref, w1_ref)):
                at = 0
                while at < piece:
                    spot = n * piece + at
                    size = min(128 - spot % 128, piece - at)
                    weights[spot // 128, i * 128 + spot % 128 : i * 128 + spot % 128 + size, :] = ref[
                        i * piece + at : i * piece + at + size, :
                    ]
                    at += size
        lane = lax.broadcasted_iota(jnp.int32, (1, x_ref.shape[1]), 1)
        for i in range(3):
            if i == 1:
                continue
            base = 3 * piece + (3 if i == 0 else 6)
            both = [
                sum(ref[base + part : base + part + 1, :].astype(F32) for part in range(3))
                for ref in (w0_ref, w1_ref)
            ]
            row = jnp.where(lane < piece, both[0], pltpu.roll(both[1], piece, 1))
            for p in range(2 * piece // 128):
                biases[p, :, i * 128 : (i + 1) * 128] = row[:, p * 128 : (p + 1) * 128]
        for p in range(2 * piece // 128):
            biases[p, :, 128:256] = jnp.zeros((1, 128), F32)

    @pl.when(block == 0)
    def _():
        qkv = (dot(x_ref[...], weights[pair], NT) + biases[pair]).astype(LOW)
        q_ref[...] = qkv[:, :128]
        k_ref[...] = qkv[:, 128:256]
        v_ref[...] = qkv[:, 256:]
        vt_ref[...] = qkv[:, 256:].T

    def run(count):
        @pl.when(pair == 0)
        def _():
            make_bias(bias_ref, block, low, count, code_ref, seg_ref)

        bias = bias_ref[block, : count * KB, :]
        rows = pl.ds(pl.multiple_of(low * KB, KB), count * KB)
        keys = k_ref[rows, :]
        queries = q_ref[pl.ds(pl.multiple_of(block * QB, QB), QB), :] * jnp.asarray(0.125, LOW)
        outs, sums = [], []
        for head in range(2):
            scores = dot(keys, one_head(queries, head), NT) + bias
            peak = jnp.max(scores, axis=0, keepdims=True)
            powers = jnp.exp(scores - peak)
            mass = jnp.sum(powers, axis=0, keepdims=True)
            probs = (powers * (1.0 / mass)).astype(LOW)
            outs.append(dot(vt_ref[head * HD : (head + 1) * HD, rows], probs))
            sums.append(peak + jnp.log(mass))
        ctx_ref[...] = jnp.concatenate(outs, axis=0).T.astype(LOW)
        lse_ref[0, 0:1, :] = sums[0]
        lse_ref[0, 1:2, :] = sums[1]

    for count in range(2, k_ref.shape[0] // KB + 1):
        pl.when(total == count)(functools.partial(run, count))


def backward_kernel(
    table_ref,
    q_ref,
    k_ref,
    v_ref,
    g_ref,
    lse_ref,
    code_ref,
    seg_ref,
    dq_ref,
    dk_ref,
    dv_ref,
    kt_ref,
    bias_ref,
    dk_sum,
    dv_sum,
):
    pair, block = pl.program_id(0), pl.program_id(1)
    low, total = table_ref[0, block], table_ref[1, block]

    @pl.when(block == 0)
    def _():
        kt_ref[...] = k_ref[...].T
        dk_sum[...] = jnp.zeros_like(dk_sum)
        dv_sum[...] = jnp.zeros_like(dv_sum)

    def run(count):
        @pl.when(pair == 0)
        def _():
            make_bias(bias_ref, block, low, count, code_ref, seg_ref)

        bias = bias_ref[block, : count * KB, :]
        rows = pl.ds(pl.multiple_of(low * KB, KB), count * KB)
        keys, values = k_ref[rows, :], v_ref[rows, :]
        queries = q_ref[...] * jnp.asarray(0.125, LOW)
        grads = g_ref[...]
        outs = []
        for head in range(2):
            query, grad = one_head(queries, head), one_head(grads, head)
            probs = jnp.exp(dot(keys, query, NT) + bias - lse_ref[0, head : head + 1, :])
            dv_sum[rows, :] += dot(probs.astype(LOW), grad)
            prob_grad = dot(values, grad, NT)
            delta = jnp.sum(probs * prob_grad, axis=0, keepdims=True)
            score_grad = (probs * (prob_grad - delta)).astype(LOW)
            dk_sum[rows, :] += dot(score_grad, query)
            outs.append(dot(kt_ref[head * HD : (head + 1) * HD, rows], score_grad))
        dq_ref[...] = (jnp.concatenate(outs, axis=0).T * 0.125).astype(LOW)

    for count in range(2, k_ref.shape[0] // KB + 1):
        pl.when(total == count)(functools.partial(run, count))

    @pl.when(block == pl.num_programs(1) - 1)
    def _():
        dk_ref[...] = dk_sum[...].astype(LOW)
        dv_ref[...] = dv_sum[...].astype(LOW)


def attend_forward(table, x, first, second, code, seg):
    seq, width = x.shape
    piece = (first.shape[0] - 16) // 3
    pairs, blocks = 2 * piece // 128, seq // QB
    column = pl.BlockSpec((seq, 128), lambda p, i, t: (0, p))
    whole = lambda p, i, t: (0, 0)
    return pl.pallas_call(
        forward_kernel,
        out_shape=(shape((seq, 2 * piece), LOW),) * 4 + (shape((pairs, 8, seq), F32),),
        grid_spec=pltpu.PrefetchScalarGridSpec(
            num_scalar_prefetch=1,
            grid=(pairs, blocks),
            in_specs=[
                pl.BlockSpec((seq, width), whole),
                pl.BlockSpec(first.shape, whole),
                pl.BlockSpec(second.shape, whole),
                pl.BlockSpec((seq, 1), whole),
                pl.BlockSpec((1, seq), whole),
            ],
            out_specs=[
                column,
                column,
                column,
                pl.BlockSpec((QB, 128), lambda p, i, t: (i, p)),
                pl.BlockSpec((1, 8, QB), lambda p, i, t: (p, 0, i)),
            ],
            scratch_shapes=[
                pltpu.VMEM((pairs, 384, width), LOW),
                pltpu.VMEM((pairs, 1, 384), F32),
                pltpu.VMEM((128, seq), LOW),
                pltpu.VMEM((blocks, seq, QB), F32),
            ],
        ),
        compiler_params=pltpu.CompilerParams(vmem_limit_bytes=40 << 20),
        cost_estimate=pl.CostEstimate(
            flops=16 * seq * seq * piece + 12 * seq * width * piece,
            bytes_accessed=16 * seq * piece,
            transcendentals=seq * seq * pairs,
        ),
        name="attend_forward",
    )(table, x, first, second, code, seg)


def attend_backward(table, q, k, v, grad, lse, code, seg):
    seq, width = grad.shape
    pairs, blocks = width // 128, seq // QB
    block = pl.BlockSpec((QB, 128), lambda p, i, t: (i, p))
    column = pl.BlockSpec((seq, 128), lambda p, i, t: (0, p))
    return pl.pallas_call(
        backward_kernel,
        out_shape=(shape((seq, width), LOW),) * 3,
        grid_spec=pltpu.PrefetchScalarGridSpec(
            num_scalar_prefetch=1,
            grid=(pairs, blocks),
            in_specs=[
                block,
                column,
                column,
                block,
                pl.BlockSpec((1, 8, QB), lambda p, i, t: (p, 0, i)),
                pl.BlockSpec((seq, 1), lambda p, i, t: (0, 0)),
                pl.BlockSpec((1, seq), lambda p, i, t: (0, 0)),
            ],
            out_specs=[block, column, column],
            scratch_shapes=[
                pltpu.VMEM((128, seq), LOW),
                pltpu.VMEM((blocks, seq, QB), F32),
                pltpu.VMEM((seq, 128), F32),
                pltpu.VMEM((seq, 128), F32),
            ],
        ),
        compiler_params=pltpu.CompilerParams(vmem_limit_bytes=32 << 20),
        cost_estimate=pl.CostEstimate(
            flops=16 * seq * seq * width,
            bytes_accessed=16 * seq * width,
            transcendentals=seq * seq * pairs,
        ),
        name="attend_backward",
    )(table, q, k, v, grad, lse, code, seg)


def gelu_parts(pre):
    t = 1.0 / (1.0 + PHI_STEP * jnp.abs(pre))
    poly = PHI[7] * t + PHI[6]
    for factor in PHI[5::-1]:
        poly = poly * t + factor
    bell = jnp.exp(-0.5 * (pre * pre))
    tail = poly * t * bell
    cdf = jnp.where(pre < 0, tail, 1.0 - tail)
    return pre * cdf, cdf + pre * (bell * 0.3989422804014327)


def norm_stats(values):
    width = values.shape[-1]
    mean = jnp.sum(values, axis=-1, keepdims=True) * (1.0 / width)
    centred = values - mean
    spread = jnp.sum(centred * centred, axis=-1, keepdims=True) * (1.0 / width)
    rate = lax.rsqrt(spread + LN_EPSILON)
    return centred * rate, rate


def norm_back(grad, gain, xhat, rate):
    width = grad.shape[-1]
    scaled = grad * gain
    mean = jnp.sum(scaled, axis=-1, keepdims=True) * (1.0 / width)
    along = jnp.sum(scaled * xhat, axis=-1, keepdims=True) * (1.0 / width)
    return rate * (scaled - mean - xhat * along)


def column_sum(values):
    return jnp.sum(values, axis=0, keepdims=True)


def middle_kernel(
    valid_ref,
    scale_ref,
    ctx_a,
    ctx_b,
    gains,
    shifts,
    bias_in,
    x_hbm,
    teacher_hbm,
    r0a,
    r0b,
    r0c,
    r0d,
    r1a,
    r1b,
    r1c,
    r1d,
    out_hbm,
    dh_hbm,
    cg_a,
    cg_b,
    ffn_send,
    ffn_keep,
    out_send,
    out_keep,
    sums,
    bias_sums,
    w_in,
    w_back,
    w_out,
    xhat_one,
    rate_one,
    mid_low,
    hidden,
    slope,
    acc,
    dh_low,
    pre_grad,
    rows_in,
    rows_out,
    stage16,
    stage32,
    w_sem,
    in_sem,
    out_sem,
    g_sem,
):
    seq, width = acc.shape
    blocks = seq // RB
    half = width // 2
    first, second = (r0a, r0b, r0c, r0d), (r1a, r1b, r1c, r1d)
    out_rows = w_out.shape[0] // 4
    units = w_in.shape[2]
    side = units // 2

    def rows(i):
        return pl.ds(i * RB, RB)

    def fetch(source, i, slot):
        return pltpu.make_async_copy(source.at[rows(i), :], rows_in.at[slot], in_sem.at[slot])

    def out_weights(p, c):
        return pltpu.make_async_copy(
            first[p].at[pl.ds(c * out_rows, out_rows), :],
            w_out.at[pl.ds(p * out_rows, out_rows), pl.ds(c * half, half)],
            w_sem.at[p, c],
        )

    def ffn_weights(p, r):
        source, base = (first[p], 2 * out_rows) if r == 0 else (second[p], 0)
        copies = [
            pltpu.make_async_copy(
                source.at[pl.ds(base, width), :],
                w_in.at[p, :, pl.ds(r * side, side)],
                w_sem.at[p, 2 + 3 * r],
            )
        ]
        for c in range(2):
            copies.append(
                pltpu.make_async_copy(
                    source.at[pl.ds(base + width + c * side, side), :],
                    w_back.at[p, pl.ds(r * side, side), pl.ds(c * half, half)],
                    w_sem.at[p, 3 + 3 * r + c],
                )
            )
        return copies

    out_copies = [out_weights(p, c) for p in range(4) for c in range(2)]
    for copy in out_copies:
        copy.start()
    fetch(x_hbm, 0, 0).start()
    for p in range(4):
        for r in range(2):
            for copy in ffn_weights(p, r):
                copy.start()
    for copy in out_copies:
        copy.wait()

    for i in range(blocks):
        if i + 1 < blocks:
            fetch(x_hbm, i + 1, (i + 1) % 2).start()
        fetch(x_hbm, i, i % 2).wait()
        context = jnp.concatenate([ctx_a[rows(i), :], ctx_b[rows(i), :]], axis=1)
        xhat, rate = norm_stats(dot(context, w_out[...]) + shifts[0:1, :] + rows_in[i % 2])
        xhat_one[rows(i), :] = xhat
        rate_one[rows(i), :] = rate
        mid_low[rows(i), :] = (xhat * gains[0:1, :] + shifts[1:2, :]).astype(LOW)
        acc[rows(i), :] = jnp.zeros((RB, width), F32)
    fetch(teacher_hbm, 0, 0).start()

    for p in range(4):
        for r in range(2):
            for copy in ffn_weights(p, r):
                copy.wait()
        for k in range(seq // FR):
            at = pl.ds(k * FR, FR)
            pre = dot(mid_low[at, :], w_in[p]) + bias_in[:, p * units : (p + 1) * units]
            act, der = gelu_parts(pre)
            act = act.astype(LOW)
            hidden[p, at, :] = act
            slope[p, at, :] = der
            acc[at, :] += dot(act, w_back[p])

    zero = jnp.zeros((1, width), F32)
    squares, gain_two, shift_two, shift_mid = zero, zero, zero, zero
    stores = []
    for i in range(blocks):
        if i + 1 < blocks:
            fetch(teacher_hbm, i + 1, (i + 1) % 2).start()
        fetch(teacher_hbm, i, i % 2).wait()
        mid = xhat_one[rows(i), :] * gains[0:1, :] + shifts[1:2, :]
        xhat, rate = norm_stats(acc[rows(i), :] + shifts[2:3, :] + mid)
        output = xhat * gains[1:2, :] + shifts[3:4, :]
        if i >= 2:
            stores[i - 2].wait()
        rows_out[i % 2] = output
        stores.append(
            pltpu.make_async_copy(rows_out.at[i % 2], out_hbm.at[rows(i), :], out_sem.at[i % 2])
        )
        stores[i].start()
        live = (i * RB + lax.broadcasted_iota(jnp.int32, (RB, 1), 0)) < valid_ref[0]
        distance = jnp.where(live, output - rows_in[i % 2], 0.0)
        squares += column_sum(distance * distance)
        out_grad = scale_ref[0] * distance
        gain_two += column_sum(out_grad * xhat)
        shift_two += column_sum(out_grad)
        dh_two = norm_back(out_grad, gains[1:2, :], xhat, rate)
        shift_mid += column_sum(dh_two)
        acc[rows(i), :] = dh_two
        dh_low[rows(i), :] = dh_two.astype(LOW)
    for store in stores[-2:]:
        store.wait()

    pending = {}
    sides = (pl.ds(0, side), pl.ds(side, side))

    def put(key, values, stage, slot, moves):
        for copy in pending.get(key, ()):
            copy.wait()
        stage[slot] = values.astype(stage.dtype)
        pending[key] = [
            pltpu.make_async_copy(stage.at[slot].at[source], target, g_sem.at[key, n])
            for n, (source, target) in enumerate(moves)
        ]
        for copy in pending[key]:
            copy.start()

    for p in (1, 3, 2, 0):
        total = jnp.zeros((1, units), F32)
        for k in range(seq // FR):
            at = pl.ds(k * FR, FR)
            grad = (dot(dh_low[at, :], w_back[p], NT) * slope[p, at, :]).astype(LOW)
            pre_grad[at, :] = grad
            acc[at, :] += dot(grad, w_in[p], NT)
            total += column_sum(grad.astype(F32))
        bias_sums[:, p * units : (p + 1) * units] = total
        stage, target, key = (stage16, ffn_send, 0) if p % 2 else (stage32, ffn_keep, 2)
        target = target.at[p // 2]
        put(
            key,
            dot(mid_low[...], pre_grad[...], TN),
            stage,
            0,
            [((slice(None), sides[r]), target.at[r, 0]) for r in range(2)],
        )
        put(
            key + 1,
            dot(hidden[p], dh_low[...], TN),
            stage,
            1,
            [
                ((sides[r], sides[c]), target.at[r, 1, sides[c], :])
                for r in range(2)
                for c in range(2)
            ],
        )
    for copies in pending.values():
        for copy in copies:
            copy.wait()

    gain_one, shift_one, shift_out = zero, zero, zero
    stores = []
    for i in range(blocks):
        grad, xhat = acc[rows(i), :], xhat_one[rows(i), :]
        gain_one += column_sum(grad * xhat)
        shift_one += column_sum(grad)
        dh_one = norm_back(grad, gains[0:1, :], xhat, rate_one[rows(i), :])
        shift_out += column_sum(dh_one)
        if i >= 2:
            stores[i - 2].wait()
        rows_out[i % 2] = dh_one
        stores.append(
            pltpu.make_async_copy(rows_out.at[i % 2], dh_hbm.at[rows(i), :], out_sem.at[i % 2])
        )
        stores[i].start()
        dh_one = dh_one.astype(LOW)
        dh_low[rows(i), :] = dh_one
        grad = dot(dh_one, w_out[...], NT).astype(LOW)
        cg_a[rows(i), :] = grad[:, :half]
        cg_b[rows(i), :] = grad[:, half:]
    for store in stores[-2:]:
        store.wait()
    for group, context in enumerate((ctx_a, ctx_b)):
        grad = dot(context[...], dh_low[...], TN)
        out_keep[group] = grad[:out_rows]
        out_send[group] = grad[out_rows:].astype(LOW)
    sums[...] = jnp.concatenate(
        [gain_one, gain_two, shift_out, shift_one, shift_mid, shift_two, squares, zero], axis=0
    )


def middle(valid, scale, ctx_a, ctx_b, gains, shifts, bias_in, x, teacher, first, second):
    seq, width = x.shape
    half = width // 2
    out_rows = ctx_a.shape[1] // 2
    units = bias_in.shape[1] // 4
    return pl.pallas_call(
        middle_kernel,
        out_shape=(
            shape((seq, width), F32),
            shape((seq, width), F32),
            shape((seq, half), LOW),
            shape((seq, half), LOW),
            shape((2, 2, 2, width, units // 2), LOW),
            shape((2, 2, 2, width, units // 2), F32),
            shape((2, out_rows, width), LOW),
            shape((2, out_rows, width), F32),
            shape((8, width), F32),
            shape((1, 4 * units), F32),
        ),
        in_specs=[SMEM, SMEM, VMEM, VMEM, VMEM, VMEM, VMEM, HBM, HBM] + [HBM] * 8,
        out_specs=(HBM, HBM, VMEM, VMEM, HBM, HBM, VMEM, VMEM, VMEM, VMEM),
        scratch_shapes=[
            pltpu.VMEM((4, width, units), LOW),
            pltpu.VMEM((4, units, width), LOW),
            pltpu.VMEM((4 * out_rows, width), LOW),
            pltpu.VMEM((seq, width), F32),
            pltpu.VMEM((seq, 1), F32),
            pltpu.VMEM((seq, width), LOW),
            pltpu.VMEM((4, seq, units), LOW),
            pltpu.VMEM((4, seq, units), F32),
            pltpu.VMEM((seq, width), F32),
            pltpu.VMEM((seq, width), LOW),
            pltpu.VMEM((seq, units), LOW),
            pltpu.VMEM((2, RB, width), F32),
            pltpu.VMEM((2, RB, width), F32),
            pltpu.VMEM((2, width, units), LOW),
            pltpu.VMEM((2, width, units), F32),
            pltpu.SemaphoreType.DMA((4, 8)),
            pltpu.SemaphoreType.DMA((2,)),
            pltpu.SemaphoreType.DMA((2,)),
            pltpu.SemaphoreType.DMA((4, 4)),
        ],
        compiler_params=pltpu.CompilerParams(vmem_limit_bytes=63 << 20),
        cost_estimate=pl.CostEstimate(
            flops=6 * seq * width * (8 * units + width),
            bytes_accessed=30 << 20,
            transcendentals=2 * seq * 4 * units,
        ),
        name="middle",
    )(valid, scale, ctx_a, ctx_b, gains, shifts, bias_in, x, teacher, *first, *second)


def projection_kernel(side_ref, x_ref, w0, w1, w2, w3, dqa, dka, dva, dqb, dkb, dvb, osend, okeep, dh_hbm, gx_hbm, send, keep, bias_ref, rows_in, rows_out, in_sem, out_sem):
    seq, width = x_ref.shape
    half = width // 2
    piece = dqa.shape[1] // 2
    blocks = seq // RB
    grads = ((dqa, dka, dva), (dqb, dkb, dvb))
    mine = pl.ds(pl.multiple_of(side_ref[0] * half, half), half)
    other = pl.ds(pl.multiple_of((1 - side_ref[0]) * half, half), half)

    def fetch(i, slot):
        return pltpu.make_async_copy(dh_hbm.at[pl.ds(i * RB, RB), :], rows_in.at[slot], in_sem.at[slot])

    fetch(0, 0).start()
    for g in range(2):
        for i in range(3):
            cross = dot(grads[g][i][...], x_ref[...], TN)
            rows_out[:2 * piece, :] = cross
            for n, at in enumerate((mine, other)):
                keep[g, n, i * piece : (i + 1) * piece, :] = rows_out[:piece, at]
                send[g, n, i * piece : (i + 1) * piece, :] = rows_out[piece : 2 * piece, at].astype(LOW)
            bias_ref[g, i : i + 1, :] = column_sum(grads[g][i][...].astype(F32))
        for n, at in enumerate((mine, other)):
            keep[g, n, 3 * piece :, :] = okeep[g, :, at]
            send[g, n, 3 * piece :, :] = osend[g, :, at]
    weights = ((w0, w1), (w2, w3))
    stores = []
    for b in range(blocks):
        at = pl.ds(b * RB, RB)
        if b + 1 < blocks:
            fetch(b + 1, (b + 1) % 2).start()
        fetch(b, b % 2).wait()
        total = rows_in[b % 2]
        for g in range(2):
            for i in range(3):
                w = jnp.concatenate([ref[i * piece : (i + 1) * piece, :] for ref in weights[g]], axis=0)
                total += dot(grads[g][i][at, :], w)
        if b >= 1:
            stores[b - 1].wait()
        rows_out[:RB, :] = total
        stores.append(pltpu.make_async_copy(rows_out.at[pl.ds(0, RB), :], gx_hbm.at[at, :], out_sem))
        stores[b].start()
    stores[-1].wait()


def projections(side, x, weights, grads, osend, okeep, dh):
    seq, width = x.shape
    half = width // 2
    piece = grads[0].shape[1] // 2
    total = 3 * piece + osend.shape[1]
    return pl.pallas_call(
        projection_kernel,
        out_shape=(
            shape((seq, width), F32),
            shape((2, 2, total, half), LOW),
            shape((2, 2, total, half), F32),
            shape((2, 8, 2 * piece), F32),
        ),
        in_specs=[SMEM] + [VMEM] * 13 + [HBM],
        out_specs=(HBM, VMEM, VMEM, VMEM),
        scratch_shapes=[
            pltpu.VMEM((2, RB, width), F32),
            pltpu.VMEM((2 * piece, width), F32),
            pltpu.SemaphoreType.DMA((2,)),
            pltpu.SemaphoreType.DMA,
        ],
        compiler_params=pltpu.CompilerParams(vmem_limit_bytes=50 << 20),
        cost_estimate=pl.CostEstimate(
            flops=24 * seq * width * piece * 2, bytes_accessed=30 << 20, transcendentals=0
        ),
        name="projections",
    )(side, x, *weights, *grads, osend, okeep, dh)


def swap(values, axis, bit):
    size = lax.axis_size(axis)
    return lax.ppermute(values, axis, [(i, i ^ (1 << bit)) for i in range(size)])


def bits_of(axis):
    return int(math.log2(lax.axis_size(axis)))


def halves(values, bit_set, axis):
    half = values.shape[axis] // 2
    keep = lax.dynamic_slice_in_dim(values, bit_set * half, half, axis)
    send = lax.dynamic_slice_in_dim(values, (1 - bit_set) * half, half, axis)
    return keep, send


def join(mine, other, bit_set, axis):
    low = jnp.where(bit_set == 0, mine, other)
    high = jnp.where(bit_set == 0, other, mine)
    return jnp.concatenate([low, high], axis=axis)


def reduce_pieces(send, keep):
    from_core = swap(send, "tensor", 0)
    away = (keep[1] + from_core[1].astype(F32)).astype(LOW)
    from_y = swap(away, "tensor", 1)
    total = keep[0] + from_core[0].astype(F32) + from_y.astype(F32)
    total = total[0] + swap(total[1].astype(LOW), "dp", 0).astype(F32)
    place = lax.axis_index("dp")
    for bit in range(1, bits_of("dp")):
        mine, other = halves(total, (place >> bit) & 1, total.ndim - 2)
        total = mine + swap(other.astype(LOW), "dp", bit).astype(F32)
    total = total.astype(LOW)
    for bit in reversed(range(1, bits_of("dp"))):
        total = join(total, swap(total, "dp", bit), (place >> bit) & 1, total.ndim - 2)
    side = place & 1
    other = swap(total, "dp", 0)
    return jnp.where(side == 0, total, other).astype(F32), jnp.where(side == 0, other, total).astype(F32)


def reduce_all(values):
    for bit in range(bits_of("tensor")):
        values = values + swap(values, "tensor", bit)
    for bit in range(bits_of("dp")):
        values = values + swap(values, "dp", bit)
    return values


def per_device(
    inputs,
    w_qkv,
    b_qv,
    w_out,
    w_in,
    b_in,
    w_back,
    norm_gains,
    shifts,
    segment_ids,
    valid_lengths,
    teacher,
):
    own_seqs, seq, width = inputs.shape
    assert own_seqs == 1 and lax.axis_size("tensor") == 4
    total_slots = seq * lax.axis_size("tensor") * lax.axis_size("dp")
    half = width // 2
    piece = w_qkv.shape[2]
    units = w_in.shape[1]
    index = lax.axis_index("tensor")
    side = (lax.axis_index("dp") & 1).astype(jnp.int32)
    side_row = side.reshape(1)
    x = inputs.reshape(seq, width)

    near = round_qkv(side_row, w_qkv, b_qv, b_in[None, :])
    core = swap(near, "tensor", 0)
    far = swap(near, "tensor", 1)
    first, second, x_low = round_rest(side_row, w_out, w_in, w_back, x)
    first_far = swap(first, "tensor", 1)

    valid = lax.dynamic_index_in_dim(valid_lengths, index, keepdims=False)
    segments = lax.dynamic_index_in_dim(segment_ids, index, keepdims=False)
    positions = jnp.arange(seq, dtype=jnp.int32)
    code = jnp.where(positions < valid, segments, -1)[:, None]
    seg = segments[None, :]
    table = span_tables(segments, valid, seq)

    qa, ka, va, ctx_a, lse_a = attend_forward(table, x_low, near, core, code, seg)
    core_far = swap(far, "tensor", 0)
    first_core = swap(first, "tensor", 0)
    second_core = swap(second, "tensor", 0)
    token_count = jnp.sum(valid_lengths)
    for bit in range(bits_of("dp")):
        token_count = token_count + swap(token_count, "dp", bit)
    token_count = token_count.astype(F32)
    qb, kb, vb, ctx_b, lse_b = attend_forward(table, x_low, far, core_far, code, seg)
    second_far = swap(first_far[2 * piece :], "dp", 0)
    first_core_far = swap(first_far, "tensor", 0)
    second_core_far = swap(second_far, "tensor", 0)
    at = 3 * piece
    bias_in = jnp.concatenate(
        [
            part[at : at + 1].astype(F32) + part[at + 1 : at + 2].astype(F32) + part[at + 2 : at + 3].astype(F32)
            for part in (near, core, far, core_far)
        ],
        axis=1,
    )
    scale = (total_slots / token_count).reshape(1)
    output, dh_one, cg_a, cg_b, ffn_send, ffn_keep, out_send, out_keep, sums, bias_sums = middle(
        valid.reshape(1),
        scale,
        ctx_a,
        ctx_b,
        norm_gains,
        shifts,
        bias_in,
        x,
        teacher.reshape(seq, width),
        (first, first_core, first_far, first_core_far),
        (second, second_core, second_far, second_core_far),
    )
    low_ffn, high_ffn = reduce_pieces(ffn_send, ffn_keep)
    grads_a = attend_backward(table, qa, ka, va, cg_a, lse_a, code, seg)
    grads_b = attend_backward(table, qb, kb, vb, cg_b, lse_b, code, seg)
    grad_inputs, send, keep, bias_qv = projections(
        side_row, x_low, (near, core, far, core_far), grads_a + grads_b, out_send, out_keep, dh_one
    )
    low_qkv, high_qkv = reduce_pieces(send, keep)

    grad_w_in = jnp.concatenate([low_ffn[0], high_ffn[0]], axis=1)
    grad_w_back = jnp.concatenate(
        [
            jnp.concatenate([part[1, :half], part[1, half:]], axis=1)
            for part in (low_ffn, high_ffn)
        ],
        axis=0,
    )
    rows = jnp.concatenate([low_qkv, high_qkv], axis=1)
    grad_w_qkv = rows[: 3 * piece].reshape(3, piece, width).transpose(0, 2, 1)
    grad_w_out = rows[3 * piece :]

    bias_in_sums = bias_sums.reshape(4, 2, units // 2)
    bias_in_sums = jnp.where(side == 0, bias_in_sums, bias_in_sums[:, ::-1]).reshape(4, units)
    bias_qv_sums = bias_qv[:, (0, 2), :].reshape(2, 2, 2, piece).transpose(0, 2, 1, 3).reshape(4, 2 * piece)
    by_shard = jnp.concatenate([bias_qv_sums, bias_in_sums], axis=1)
    flipped = jnp.where((index & 1) == 0, by_shard, by_shard[jnp.array([1, 0, 3, 2])])
    natural = jnp.where((index & 2) == 0, flipped, flipped[jnp.array([2, 3, 0, 1])])
    wide = by_shard.shape[1]
    small = reduce_all(jnp.concatenate([natural.reshape(-1), sums[:7].reshape(-1)]))
    own = lax.dynamic_slice_in_dim(small, index * wide, wide)
    rest = small[4 * wide :].reshape(7, width)
    loss = jnp.sum(rest[6]) / (2.0 * width * token_count)
    return (
        output.reshape(own_seqs, seq, width),
        loss,
        grad_inputs.reshape(own_seqs, seq, width),
        grad_w_qkv,
        own[: 2 * piece].reshape(2, piece),
        grad_w_out,
        grad_w_in,
        own[2 * piece :],
        grad_w_back,
        rest[:2],
        rest[2:6],
    )


def solution(mesh):
    return jax.shard_map(
        per_device,
        mesh=mesh,
        in_specs=(
            P(("dp", "tensor"), None, None),
            P(None, None, "tensor"),
            P(None, "tensor"),
            P("tensor", None),
            P(None, "tensor"),
            P("tensor"),
            P("tensor", None),
            P(),
            P(),
            P("dp", None),
            P("dp"),
            P(("dp", "tensor"), None, None),
        ),
        out_specs=(
            P(("dp", "tensor"), None, None),
            P(),
            P(("dp", "tensor"), None, None),
            P(None, None, "tensor"),
            P(None, "tensor"),
            P("tensor", None),
            P(None, "tensor"),
            P("tensor"),
            P("tensor", None),
            P(),
            P(),
        ),
        check_vma=False,
    )
```

time: 497 us -> 533 us (1.072)
  matrix products: 127 us -> 0 us
  Pallas kernels: 67 us -> 167 us
  waiting for transfers between devices: 109 us -> 203 us
  other arithmetic: 48.1 us -> 28.4 us
  starting transfers between devices: 85.7 us -> 70.5 us
    dot_general x19 -> x0, matrix products: 127 us -> none  [the longest x5 56.9 us: matmul_f32(): return jnp.dot(left, right, preferred_element_type=jnp.float32)]
    pallas_call x4 -> x8, Pallas kernels: 67 us -> 167 us  [the longest x1 64.9 us: middle(): pl.pallas_call(middle_kernel, out_shape=(shape((seq, width), F32), shape(...]
    ppermute x55 -> x33, waiting for transfers between devices: 109 us -> 203 us  [swap(): return lax.ppermute(values, axis, [(i, i ^ 1 << bit) for i in range(size)])]
    ppermute x55 -> x33, starting transfers between devices: 85.7 us -> 70.5 us  [swap(): return lax.ppermute(values, axis, [(i, i ^ 1 << bit) for i in range(size)])]
    convert_element_type x16 -> x5, other arithmetic: 18.4 us -> 4.1 us  [the longest x2 2.61 us: reduce_pieces(): away = (keep[1] + from_core[1].astype(F32)).astype(LOW)]
    reduce_sum x12 -> x0, other arithmetic: 9.92 us -> none  [the longest x2 3.39 us: layer_norm(): centred = values - jnp.mean(values, axis=-1, keepdims=True)]
    unnamed x173 -> x114, local copies, waits for them, and re-layouts: 34.6 us -> 30.2 us
  transfers between devices with their start and end apart: 55 -> 33, of which waited for: 23 -> 18; matrix products, arithmetic and copies ran while one was open for 26% -> 8% of each run, Pallas kernels for 6% -> 19%
where the time goes in v2:
time: 533 us; the launch traced here: 524 us
  waiting for transfers between devices  203 us (38%)
  Pallas kernels  167 us (31%)
  starting transfers between devices  70.5 us (13%)
  local copies, waits for them, and re-layouts  48.2 us (9%)
  other arithmetic  28.4 us (5%)
  between operations  6.22 us (1%)
    ppermute x33, waiting for transfers between devices, swap(): return lax.ppermute(values, axis, [(i, i ^ 1 << bit) for i in range(size)])  203 us
    ppermute x33, starting transfers between devices, swap(): return lax.ppermute(values, axis, [(i, i ^ 1 << bit) for i in range(size)])  70.5 us
    pallas_call x1, Pallas kernels, middle(): pl.pallas_call(middle_kernel, out_shape=(shape((seq, width), F32), shape(...  64.9 us
    pallas_call x2, Pallas kernels, attend_forward(): pl.pallas_call(forward_kernel, out_shape=(shape((seq, 2 * piece), LOW),)...  38.2 us
    pallas_call x2, Pallas kernels, attend_backward(): pl.pallas_call(backward_kernel, out_shape=(shape((seq, width), LOW),) * 3...  37.5 us
    unnamed x114, local copies, waits for them, and re-layouts  30.2 us
    pallas_call x1, Pallas kernels, projections(): pl.pallas_call(projection_kernel, out_shape=(shape((seq, width), F32), sh...  22.2 us
  transfers between devices with their start and end apart: 33, of which 18 were waited for; matrix products, arithmetic and copies ran while one was open for 8% of the time, Pallas kernels for 19%

profile of v2, /device:TPU:0, one launch (start us, length us, event | category | flops | bytes accessed | tf_op | source)
XLA Modules:
  0.0 523.6 jit_solution(1294756992941406138)
XLA Ops:
  10.7 3.0 collective-permute-start.7
  16.1 3.1 round_qkv.1.w0_ref.w0
  24.0 23.1 %collective-permute-done.7.r0c = bf16[1920,384]{1,0:T(8,128)(2,1)} collective-permute-done((bf16[1920,384]{1,0:T(8,128)(2,1)}, bf16[1920,384]{1,0:T(8,128)(2,1)}, u32[]{:S(2)}, u32[]{:S(2)}) %collective-permute-start.7) | collective-permute-done | bytes 1474592 | tf_op jit(solution)/shard_map/ppermute | solution.py:751
  47.1 2.4 slice.225
  55.6 2.9 collective-permute-start.1
  60.0 4.0 collective-permute-start.2
  67.7 18.9 %attend_forward.2 = (bf16[1024,384]{1,0:T(8,128)(2,1)S(1)}, bf16[1024,384]{1,0:T(8,128)(2,1)S(1)}, bf16[1024,384]{1,0:T(8,128)(2,1)S(1)}, bf16[1024,384]{1,0:T(8,128)(2,1)S(1)}, f32[3,8,1024]{2,1,0:T(8,128)S(1)}) custom-call(s32[2,4]{1,0:T(2,128)S(1)} %pad_add_fusion.table_ref, bf16[1024,768]{1,0:T(8,128)(2,1)S(1)} %copy-done.13, ...), custom_call_target="tpu_custom_call" | custom-call | flops 5033164800 | bytes 3145728 | tf_op jit(solution)/shard_map/attend_forward/pallas_call | solution.py:285
  90.7 19.3 %attend_forward.3 = (bf16[1024,384]{1,0:T(8,128)(2,1)S(1)}, bf16[1024,384]{1,0:T(8,128)(2,1)S(1)}, bf16[1024,384]{1,0:T(8,128)(2,1)S(1)}, bf16[1024,384]{1,0:T(8,128)(2,1)S(1)}, f32[3,8,1024]{2,1,0:T(8,128)S(1)}) custom-call(s32[2,4]{1,0:T(2,128)S(1)} %pad_add_fusion.table_ref, bf16[1024,768]{1,0:T(8,128)(2,1)S(1)} %copy-done.13, ...), custom_call_target="tpu_custom_call" | custom-call | flops 5033164800 | bytes 3145728 | tf_op jit(solution)/shard_map/attend_forward/pallas_call | solution.py:285
  115.1 64.9 %middle.1 = (f32[1024,768]{1,0:T(8,128)}, f32[1024,768]{1,0:T(8,128)}, bf16[1024,384]{1,0:T(8,128)(2,1)}, bf16[1024,384]{1,0:T(8,128)(2,1)}, bf16[2,2,2,768,384]...) custom-call(s32[1]{0:T(128)} %dynamic_slice.35.valid_ref, ...), custom_call_target="tpu_custom_call" | custom-call | flops 32614907904 | bytes 31457280 | tf_op jit(solution)/shard_map/middle/pallas_call | solution.py:629
  184.7 18.7 %attend_backward.3 = (bf16[1024,384]{1,0:T(8,128)(2,1)S(1)}, bf16[1024,384]{1,0:T(8,128)(2,1)S(1)}, bf16[1024,384]{1,0:T(8,128)(2,1)S(1)}) custom-call(s32[2,4]{1,0:T(2,128)S(1)} %pad_add_fusion.table_ref, bf16[1024,384]{1,0:T(8,128)(2,1)S(1)} %copy-done.26, bf16[1024,384]{1,0:T(8,128)(2,1)S(1)} %copy-done.28, bf16[1024,384]{1,0:T(8,128)(2,1)S(1)} %copy-done.30, ...), custom_call_target="tpu_custom_call" | custom-call | flops 6442450944 | bytes 6291456 | tf_op jit(solution)/shard_map/attend_backward/pallas_call | solution.py:327
  205.3 18.7 %attend_backward.2 = (bf16[1024,384]{1,0:T(8,128)(2,1)S(1)}, bf16[1024,384]{1,0:T(8,128)(2,1)S(1)}, bf16[1024,384]{1,0:T(8,128)(2,1)S(1)}) custom-call(s32[2,4]{1,0:T(2,128)S(1)} %pad_add_fusion.table_ref, bf16[1024,384]{1,0:T(8,128)(2,1)S(1)} %copy-done.19, bf16[1024,384]{1,0:T(8,128)(2,1)S(1)} %copy-done.21, bf16[1024,384]{1,0:T(8,128)(2,1)S(1)} %copy-done.23, ...), custom_call_target="tpu_custom_call" | custom-call | flops 6442450944 | bytes 6291456 | tf_op jit(solution)/shard_map/attend_backward/pallas_call | solution.py:327
  224.1 22.2 %projections.1 = (f32[1024,768]{1,0:T(8,128)}, bf16[2,2,768,384]{3,2,1,0:T(8,128)(2,1)}, f32[2,2,768,384]{3,2,1,0:T(8,128)}, f32[2,8,384]{2,1,0:T(8,128)S(1)}) custom-call(s32[1]{0:T(128)} %bitcast.5.side_ref, bf16[1024,768]{1,0:T(8,128)(2,1)} %copy-done.12, bf16[592,768]{1,0:T(8,128)(2,1)} %round_qkv.1.w0_ref.w0, bf16[592,768]{1,0:T(8,128)(2,1)} %copy-done.10, ...), custom_call_target="tpu_custom_call" | custom-call | flops 7247757312 | bytes 31457280 | tf_op jit(solution)/shard_map/projections/pallas_call | solution.py:725
  246.8 2.3 fusion
  249.1 8.1 %collective-permute-start.26 = (bf16[2,2,768,384]{3,2,1,0:T(8,128)(2,1)S(1)}, bf16[2,2,768,384]{3,2,1,0:T(8,128)(2,1)S(1)}, u32[]{:S(2)}, u32[]{:S(2)}) collective-permute-start(bf16[2,2,768,384]{3,2,1,0:T(8,128)(2,1)S(1)} %fusion), channel_id=1, source_target_pairs={{0,2},{1,3},{2,0},{3,1},{4,6},{5,7},{6,4},{7,5},{8,10},{9,11},{10,... | collective-permute-start | bytes 7077896 | tf_op jit(solution)/shard_map/ppermute | solution.py:751
  257.5 2.3 collective-permute-start.18
  259.8 74.5 %collective-permute-done.18 = bf16[2,768,384]{2,1,0:T(8,128)(2,1)S(1)} collective-permute-done((bf16[2,768,384]{2,1,0:T(8,128)(2,1)S(1)}, bf16[2,768,384]{2,1,0:T(8,128)(2,1)S(1)}, u32[]{:S(2)}, u32[]{:S(2)}) %collective-permute-start.18) | collective-permute-done | bytes 1179680 | tf_op jit(solution)/shard_map/ppermute | solution.py:751
  334.7 2.4 bitcast_add_fusion
  344.3 36.9 %collective-permute-done.19 = bf16[768,384]{1,0:T(8,128)(2,1)} collective-permute-done((bf16[768,384]{1,0:T(8,128)(2,1)S(1)}, bf16[768,384]{1,0:T(8,128)(2,1)}, u32[]{:S(2)}, u32[]{:S(2)}) %collective-permute-start.19) | collective-permute-done | bytes 589856 | tf_op jit(solution)/shard_map/ppermute | solution.py:751
  382.5 4.2 collective-permute-start.20
  392.0 2.4 collective-permute-done.20
  395.6 10.7 %collective-permute-start.21 = (bf16[192,384]{1,0:T(8,128)(2,1)S(1)}, bf16[192,384]{1,0:T(8,128)(2,1)S(1)}, u32[]{:S(2)}, u32[]{:S(2)}) collective-permute-start(bf16[192,384]{1,0:T(8,128)(2,1)S(1)} %dynamic-slice_convert_fusion.3), channel_id=1, source_target_pairs={{0,16},{4,20},{8,24},{12,28},{16,0},{20,4},{24,8},{28,12},{1,17},{... | collective-permute-start | bytes 442376 | tf_op jit(solution)/shard_map/ppermute | solution.py:751
  409.5 10.5 %collective-permute-start.29 = (bf16[2,192,384]{2,1,0:T(8,128)(2,1)S(1)}, bf16[2,192,384]{2,1,0:T(8,128)(2,1)S(1)}, u32[]{:S(2)}, u32[]{:S(2)}) collective-permute-start(bf16[2,192,384]{2,1,0:T(8,128)(2,1)S(1)} %dynamic-slice_convert_fusion.1), channel_id=1, source_target_pairs={{0,16},{4,20},{8,24},{12,28},{16,0},{20,4},{24,8},{28,12},{1,17},{... | collective-permute-start | bytes 884744 | tf_op jit(solution)/shard_map/ppermute | solution.py:751
  420.7 15.6 %collective-permute-done.29 = bf16[2,192,384]{2,1,0:T(8,128)(2,1)S(1)} collective-permute-done((bf16[2,192,384]{2,1,0:T(8,128)(2,1)S(1)}, bf16[2,192,384]{2,1,0:T(8,128)(2,1)S(1)}, u32[]{:S(2)}, u32[]{:S(2)}) %collective-permute-start.29) | collective-permute-done | bytes 294944 | tf_op jit(solution)/shard_map/ppermute | solution.py:751
  438.4 6.8 %collective-permute-start.23 = (bf16[384,384]{1,0:T(8,128)(2,1)S(1)}, bf16[384,384]{1,0:T(8,128)(2,1)S(1)}, u32[]{:S(2)}, u32[]{:S(2)}) collective-permute-start(bf16[384,384]{1,0:T(8,128)(2,1)S(1)} %pad_maximum_fusion.4), channel_id=1, source_target_pairs={{0,8},{4,12},{8,0},{12,4},{16,24},{20,28},{24,16},{28,20},{1,9},{5... | collective-permute-start | bytes 884744 | tf_op jit(solution)/shard_map/ppermute | solution.py:751
  445.2 5.5 %collective-permute-done.30 = bf16[2,192,384]{2,1,0:T(8,128)(2,1)S(1)} collective-permute-done((bf16[2,192,384]{2,1,0:T(8,128)(2,1)S(1)}, bf16[2,192,384]{2,1,0:T(8,128)(2,1)S(1)}, u32[]{:S(2)}, u32[]{:S(2)}) %collective-permute-start.30) | collective-permute-done | bytes 294944 | tf_op jit(solution)/shard_map/ppermute | solution.py:751
  452.2 4.6 collective-permute-done.23
  459.1 9.6 %collective-permute-done.31 = bf16[2,384,384]{2,1,0:T(8,128)(2,1)S(1)} collective-permute-done((bf16[2,384,384]{2,1,0:T(8,128)(2,1)S(1)}, bf16[2,384,384]{2,1,0:T(8,128)(2,1)S(1)}, u32[]{:S(2)}, u32[]{:S(2)}) %collective-permute-start.31) | collective-permute-done | bytes 589856 | tf_op jit(solution)/shard_map/ppermute | solution.py:751
  478.2 2.7 collective-permute-done.13
  481.7 16.7 %collective-permute-done.14 = f32[9984]{0:T(1024)S(1)} collective-permute-done((f32[9984]{0:T(1024)S(1)}, f32[9984]{0:T(1024)S(1)}, u32[]{:S(2)}, u32[]{:S(2)}) %collective-permute-start.14) | collective-permute-done | bytes 39968 | tf_op jit(solution)/shard_map/ppermute | solution.py:751
  498.4 4.0 collective-permute-done.15
  503.1 3.5 collective-permute-start.16
  506.6 2.3 collective-permute-done.16
  (242 shorter events, 90.3 us)
Async XLA Ops:
  10.7 36.4 %collective-permute-start.7 = (bf16[1920,384]{1,0:T(8,128)(2,1)}, bf16[1920,384]{1,0:T(8,128)(2,1)}, u32[]{:S(2)}, u32[]{:S(2)}) collective-permute-start(bf16[1920,384]{1,0:T(8,128)(2,1)} %get-tuple-element.47.r0a), channel_id=1, source_target_pairs={{0,2},{1,3},{2,0},{3,1},{4,6},{5,7},{6,4},{7,5},{8,10},{9,11},{10,... | collective-permute-start | bytes 4423688 | tf_op jit(solution)/shard_map/ppermute | solution.py:751
  19.2 46.4 %collective-permute-start.4 = (bf16[592,768]{1,0:T(8,128)(2,1)}, bf16[592,768]{1,0:T(8,128)(2,1)S(1)}, u32[]{:S(2)}, u32[]{:S(2)}) collective-permute-start(bf16[592,768]{1,0:T(8,128)(2,1)} %round_qkv.1.w0_ref.w0), channel_id=1, source_target_pairs={{0,2},{1,3},{2,0},{3,1},{4,6},{5,7},{6,4},{7,5},{8,10},{9,11},{10,... | collective-permute-start | bytes 2727944 | tf_op jit(solution)/shard_map/ppermute | solution.py:751
  19.2 46.6 %collective-permute-start.3 = (bf16[592,768]{1,0:T(8,128)(2,1)}, bf16[592,768]{1,0:T(8,128)(2,1)S(1)}, u32[]{:S(2)}, u32[]{:S(2)}) collective-permute-start(bf16[592,768]{1,0:T(8,128)(2,1)} %round_qkv.1.w0_ref.w0), channel_id=1, source_target_pairs={{0,1},{1,0},{2,3},{3,2},{4,5},{5,4},{6,7},{7,6},{8,9},{9,8},{10,11... | collective-permute-start | bytes 2727944 | tf_op jit(solution)/shard_map/ppermute | solution.py:751
  19.2 94.4 %collective-permute-start.6 = (bf16[1920,384]{1,0:T(8,128)(2,1)}, bf16[1920,384]{1,0:T(8,128)(2,1)}, u32[]{:S(2)}, u32[]{:S(2)}) collective-permute-start(bf16[1920,384]{1,0:T(8,128)(2,1)} %get-tuple-element.47.r0a), channel_id=1, source_target_pairs={{0,1},{1,0},{2,3},{3,2},{4,5},{5,4},{6,7},{7,6},{8,9},{9,8},{10,11... | collective-permute-start | bytes 4423688 | tf_op jit(solution)/shard_map/ppermute | solution.py:751
  20.3 34.0 %collective-permute-start = (s32[]{:T(128)}, s32[]{:T(128)}, u32[]{:S(2)}, u32[]{:S(2)}) collective-permute-start(s32[]{:T(128)} %reduce_sum.38), channel_id=1, source_target_pairs={{0,4},{4,0},{8,12},{12,8},{16,20},{20,16},{24,28},{28,24},{1,5},{5... | collective-permute-start | bytes 20 | tf_op jit(solution)/shard_map/ppermute | solution.py:751
  49.5 40.1 %collective-permute-start.10 = (bf16[1536,384]{1,0:T(8,128)(2,1)}, bf16[1536,384]{1,0:T(8,128)(2,1)}, u32[]{:S(2)}, u32[]{:S(2)}) collective-permute-start(bf16[1536,384]{1,0:T(8,128)(2,1)} %slice.225), channel_id=1, source_target_pairs={{0,4},{4,0},{8,12},{12,8},{16,20},{20,16},{24,28},{28,24},{1,5},{5... | collective-permute-start | bytes 3538952 | tf_op jit(solution)/shard_map/ppermute | solution.py:751
  55.6 3.7 collective-permute-start.1
  60.0 4.5 collective-permute-start.2
  64.4 49.1 %collective-permute-start.9 = (bf16[1536,384]{1,0:T(8,128)(2,1)}, bf16[1536,384]{1,0:T(8,128)(2,1)}, u32[]{:S(2)}, u32[]{:S(2)}) collective-permute-start(bf16[1536,384]{1,0:T(8,128)(2,1)} %copy-done.14), channel_id=1, source_target_pairs={{0,1},{1,0},{2,3},{3,2},{4,5},{5,4},{6,7},{7,6},{8,9},{9,8},{10,11... | collective-permute-start | bytes 3538952 | tf_op jit(solution)/shard_map/ppermute | solution.py:751
  65.6 24.3 %collective-permute-start.5 = (bf16[592,768]{1,0:T(8,128)(2,1)S(1)}, bf16[592,768]{1,0:T(8,128)(2,1)S(1)}, u32[]{:S(2)}, u32[]{:S(2)}) collective-permute-start(bf16[592,768]{1,0:T(8,128)(2,1)S(1)} %collective-permute-done.4.w0_ref.w2), channel_id=1, source_target_pairs={{0,1},{1,0},{2,3},{3,2},{4,5},{5,4},{6,7},{7,6},{8,9},{9,8},{10,11... | collective-permute-start | bytes 2727944 | tf_op jit(solution)/shard_map/ppermute | solution.py:751
  89.3 24.2 %collective-permute-start.8 = (bf16[1920,384]{1,0:T(8,128)(2,1)}, bf16[1920,384]{1,0:T(8,128)(2,1)S(1)}, u32[]{:S(2)}, u32[]{:S(2)}) collective-permute-start(bf16[1920,384]{1,0:T(8,128)(2,1)} %collective-permute-done.7.r0c), channel_id=1, source_target_pairs={{0,1},{1,0},{2,3},{3,2},{4,5},{5,4},{6,7},{7,6},{8,9},{9,8},{10,11... | collective-permute-start | bytes 4423688 | tf_op jit(solution)/shard_map/ppermute | solution.py:751
  89.5 24.1 %collective-permute-start.11 = (bf16[1536,384]{1,0:T(8,128)(2,1)}, bf16[1536,384]{1,0:T(8,128)(2,1)S(1)}, u32[]{:S(2)}, u32[]{:S(2)}) collective-permute-start(bf16[1536,384]{1,0:T(8,128)(2,1)} %collective-permute-done.10.r1c), channel_id=1, source_target_pairs={{0,1},{1,0},{2,3},{3,2},{4,5},{5,4},{6,7},{7,6},{8,9},{9,8},{10,11... | collective-permute-start | bytes 3538952 | tf_op jit(solution)/shard_map/ppermute | solution.py:751
  179.9 66.8 %collective-permute-start.25 = (bf16[2,2,2,768,384]{4,3,2,1,0:T(8,128)(2,1)}, bf16[2,2,2,768,384]{4,3,2,1,0:T(8,128)(2,1)}, u32[]{:S(2)}, u32[]{:S(2)}) collective-permute-start(bf16[2,2,2,768,384]{4,3,2,1,0:T(8,128)(2,1)} %get-tuple-element.76), channel_id=1, source_target_pairs={{0,1},{1,0},{2,3},{3,2},{4,5},{5,4},{6,7},{7,6},{8,9},{9,8},{10,11... | collective-permute-start | bytes 14155784 | tf_op jit(solution)/shard_map/ppermute | solution.py:751
  246.3 10.8 %collective-permute-start.17 = (bf16[2,2,768,384]{3,2,1,0:T(8,128)(2,1)}, bf16[2,2,768,384]{3,2,1,0:T(8,128)(2,1)S(1)}, u32[]{:S(2)}, u32[]{:S(2)}) collective-permute-start(bf16[2,2,768,384]{3,2,1,0:T(8,128)(2,1)} %get-tuple-element.74), channel_id=1, source_target_pairs={{0,1},{1,0},{2,3},{3,2},{4,5},{5,4},{6,7},{7,6},{8,9},{9,8},{10,11... | collective-permute-start | bytes 7077896 | tf_op jit(solution)/shard_map/ppermute | solution.py:751
  249.1 85.6 %collective-permute-start.26 = (bf16[2,2,768,384]{3,2,1,0:T(8,128)(2,1)S(1)}, bf16[2,2,768,384]{3,2,1,0:T(8,128)(2,1)S(1)}, u32[]{:S(2)}, u32[]{:S(2)}) collective-permute-start(bf16[2,2,768,384]{3,2,1,0:T(8,128)(2,1)S(1)} %fusion), channel_id=1, source_target_pairs={{0,2},{1,3},{2,0},{3,1},{4,6},{5,7},{6,4},{7,5},{8,10},{9,11},{10,... | collective-permute-start | bytes 7077896 | tf_op jit(solution)/shard_map/ppermute | solution.py:751
  257.5 76.9 %collective-permute-start.18 = (bf16[2,768,384]{2,1,0:T(8,128)(2,1)S(1)}, bf16[2,768,384]{2,1,0:T(8,128)(2,1)S(1)}, u32[]{:S(2)}, u32[]{:S(2)}) collective-permute-start(bf16[2,768,384]{2,1,0:T(8,128)(2,1)S(1)} %fusion.2), channel_id=1, source_target_pairs={{0,2},{1,3},{2,0},{3,1},{4,6},{5,7},{6,4},{7,5},{8,10},{9,11},{10,... | collective-permute-start | bytes 3538952 | tf_op jit(solution)/shard_map/ppermute | solution.py:751
  340.5 46.2 %collective-permute-start.27 = (bf16[2,768,384]{2,1,0:T(8,128)(2,1)}, bf16[2,768,384]{2,1,0:T(8,128)(2,1)}, u32[]{:S(2)}, u32[]{:S(2)}) collective-permute-start(bf16[2,768,384]{2,1,0:T(8,128)(2,1)} %fusion.3), channel_id=1, source_target_pairs={{0,4},{4,0},{8,12},{12,8},{16,20},{20,16},{24,28},{28,24},{1,5},{5... | collective-permute-start | bytes 3538952 | tf_op jit(solution)/shard_map/ppermute | solution.py:751
  341.9 39.4 %collective-permute-start.19 = (bf16[768,384]{1,0:T(8,128)(2,1)S(1)}, bf16[768,384]{1,0:T(8,128)(2,1)}, u32[]{:S(2)}, u32[]{:S(2)}) collective-permute-start(bf16[768,384]{1,0:T(8,128)(2,1)S(1)} %fusion.5), channel_id=1, source_target_pairs={{0,4},{4,0},{8,12},{12,8},{16,20},{20,16},{24,28},{28,24},{1,5},{5... | collective-permute-start | bytes 1769480 | tf_op jit(solution)/shard_map/ppermute | solution.py:751
  382.5 11.9 %collective-permute-start.20 = (bf16[384,384]{1,0:T(8,128)(2,1)S(1)}, bf16[384,384]{1,0:T(8,128)(2,1)S(1)}, u32[]{:S(2)}, u32[]{:S(2)}) collective-permute-start(bf16[384,384]{1,0:T(8,128)(2,1)S(1)} %dynamic-slice_convert_fusion.2), channel_id=1, source_target_pairs={{0,8},{4,12},{8,0},{12,4},{16,24},{20,28},{24,16},{28,20},{1,9},{5... | collective-permute-start | bytes 884744 | tf_op jit(solution)/shard_map/ppermute | solution.py:751
  389.8 17.5 %collective-permute-start.28 = (bf16[2,384,384]{2,1,0:T(8,128)(2,1)}, bf16[2,384,384]{2,1,0:T(8,128)(2,1)}, u32[]{:S(2)}, u32[]{:S(2)}) collective-permute-start(bf16[2,384,384]{2,1,0:T(8,128)(2,1)} %dynamic-slice_convert_fusion), channel_id=1, source_target_pairs={{0,8},{4,12},{8,0},{12,4},{16,24},{20,28},{24,16},{28,20},{1,9},{5... | collective-permute-start | bytes 1769480 | tf_op jit(solution)/shard_map/ppermute | solution.py:751
  395.6 25.0 %collective-permute-start.21 = (bf16[192,384]{1,0:T(8,128)(2,1)S(1)}, bf16[192,384]{1,0:T(8,128)(2,1)S(1)}, u32[]{:S(2)}, u32[]{:S(2)}) collective-permute-start(bf16[192,384]{1,0:T(8,128)(2,1)S(1)} %dynamic-slice_convert_fusion.3), channel_id=1, source_target_pairs={{0,16},{4,20},{8,24},{12,28},{16,0},{20,4},{24,8},{28,12},{1,17},{... | collective-permute-start | bytes 442376 | tf_op jit(solution)/shard_map/ppermute | solution.py:751
  409.5 26.9 %collective-permute-start.29 = (bf16[2,192,384]{2,1,0:T(8,128)(2,1)S(1)}, bf16[2,192,384]{2,1,0:T(8,128)(2,1)S(1)}, u32[]{:S(2)}, u32[]{:S(2)}) collective-permute-start(bf16[2,192,384]{2,1,0:T(8,128)(2,1)S(1)} %dynamic-slice_convert_fusion.1), channel_id=1, source_target_pairs={{0,16},{4,20},{8,24},{12,28},{16,0},{20,4},{24,8},{28,12},{1,17},{... | collective-permute-start | bytes 884744 | tf_op jit(solution)/shard_map/ppermute | solution.py:751
  420.6 17.7 %collective-permute-start.22 = (bf16[192,384]{1,0:T(8,128)(2,1)S(1)}, bf16[192,384]{1,0:T(8,128)(2,1)S(1)}, u32[]{:S(2)}, u32[]{:S(2)}) collective-permute-start(bf16[192,384]{1,0:T(8,128)(2,1)S(1)} %add_convert_fusion.3), channel_id=1, source_target_pairs={{0,16},{4,20},{8,24},{12,28},{16,0},{20,4},{24,8},{28,12},{1,17},{... | collective-permute-start | bytes 442376 | tf_op jit(solution)/shard_map/ppermute | solution.py:751
  437.5 13.2 %collective-permute-start.30 = (bf16[2,192,384]{2,1,0:T(8,128)(2,1)S(1)}, bf16[2,192,384]{2,1,0:T(8,128)(2,1)S(1)}, u32[]{:S(2)}, u32[]{:S(2)}) collective-permute-start(bf16[2,192,384]{2,1,0:T(8,128)(2,1)S(1)} %add_convert_fusion.2), channel_id=1, source_target_pairs={{0,16},{4,20},{8,24},{12,28},{16,0},{20,4},{24,8},{28,12},{1,17},{... | collective-permute-start | bytes 884744 | tf_op jit(solution)/shard_map/ppermute | solution.py:751
  438.4 18.4 %collective-permute-start.23 = (bf16[384,384]{1,0:T(8,128)(2,1)S(1)}, bf16[384,384]{1,0:T(8,128)(2,1)S(1)}, u32[]{:S(2)}, u32[]{:S(2)}) collective-permute-start(bf16[384,384]{1,0:T(8,128)(2,1)S(1)} %pad_maximum_fusion.4), channel_id=1, source_target_pairs={{0,8},{4,12},{8,0},{12,4},{16,24},{20,28},{24,16},{28,20},{1,9},{5... | collective-permute-start | bytes 884744 | tf_op jit(solution)/shard_map/ppermute | solution.py:751
  450.8 17.9 %collective-permute-start.31 = (bf16[2,384,384]{2,1,0:T(8,128)(2,1)S(1)}, bf16[2,384,384]{2,1,0:T(8,128)(2,1)S(1)}, u32[]{:S(2)}, u32[]{:S(2)}) collective-permute-start(bf16[2,384,384]{2,1,0:T(8,128)(2,1)S(1)} %pad_maximum_fusion.3), channel_id=1, source_target_pairs={{0,8},{4,12},{8,0},{12,4},{16,24},{20,28},{24,16},{28,20},{1,9},{5... | collective-permute-start | bytes 1769480 | tf_op jit(solution)/shard_map/ppermute | solution.py:751
  457.8 57.8 %collective-permute-start.24 = (bf16[768,384]{1,0:T(8,128)(2,1)}, bf16[768,384]{1,0:T(8,128)(2,1)S(1)}, u32[]{:S(2)}, u32[]{:S(2)}) collective-permute-start(bf16[768,384]{1,0:T(8,128)(2,1)} %pad_maximum_fusion.2), channel_id=1, source_target_pairs={{0,4},{4,0},{8,12},{12,8},{16,20},{20,16},{24,28},{28,24},{1,5},{5... | collective-permute-start | bytes 1769480 | tf_op jit(solution)/shard_map/ppermute | solution.py:751
  470.1 48.1 %collective-permute-start.32 = (bf16[2,768,384]{2,1,0:T(8,128)(2,1)}, bf16[2,768,384]{2,1,0:T(8,128)(2,1)S(1)}, u32[]{:S(2)}, u32[]{:S(2)}) collective-permute-start(bf16[2,768,384]{2,1,0:T(8,128)(2,1)} %pad_maximum_fusion.1), channel_id=1, source_target_pairs={{0,4},{4,0},{8,12},{12,8},{16,20},{20,16},{24,28},{28,24},{1,5},{5... | collective-permute-start | bytes 3538952 | tf_op jit(solution)/shard_map/ppermute | solution.py:751
  477.0 4.0 collective-permute-start.13
  481.0 17.5 %collective-permute-start.14 = (f32[9984]{0:T(1024)S(1)}, f32[9984]{0:T(1024)S(1)}, u32[]{:S(2)}, u32[]{:S(2)}) collective-permute-start(f32[9984]{0:T(1024)S(1)} %add.185), channel_id=1, source_target_pairs={{0,4},{4,0},{8,12},{12,8},{16,20},{20,16},{24,28},{28,24},{1,5},{5... | collective-permute-start | bytes 119816 | tf_op jit(solution)/shard_map/ppermute | solution.py:751
  498.4 4.0 collective-permute-start.15
  503.1 5.8 %collective-permute-start.16 = (f32[9984]{0:T(1024)}, f32[9984]{0:T(1024)}, u32[]{:S(2)}, u32[]{:S(2)}) collective-permute-start(f32[9984]{0:T(1024)} %add.187), channel_id=1, source_target_pairs={{0,16},{4,20},{8,24},{12,28},{16,0},{20,4},{24,8},{28,12},{1,17},{... | collective-permute-start | bytes 119816 | tf_op jit(solution)/shard_map/ppermute | solution.py:751
  (56 other events, 557.8 us)

commit v3 on v2

--- a/solution.py
+++ b/solution.py
@@ -29,6 +29,7 @@
 )
 PHI_STEP = 0.23164188826636045
 
+VMEM_LIMIT = 63 << 20
 VMEM = pl.BlockSpec(memory_space=pltpu.VMEM)
 SMEM = pl.BlockSpec(memory_space=pltpu.SMEM)
 HBM = pl.BlockSpec(memory_space=pl.ANY)
@@ -74,6 +75,7 @@
         out_shape=shape((3 * piece + 16, width), LOW),
         in_specs=[SMEM, VMEM, VMEM, VMEM],
         out_specs=VMEM,
+        compiler_params=pltpu.CompilerParams(vmem_limit_bytes=VMEM_LIMIT),
         name="round_qkv",
     )(side, w_qkv, b_qv, b_in)
 
@@ -104,7 +106,7 @@
         ),
         in_specs=[SMEM, VMEM, VMEM, VMEM, VMEM],
         out_specs=(VMEM, VMEM, VMEM),
-        compiler_params=pltpu.CompilerParams(vmem_limit_bytes=40 << 20),
+        compiler_params=pltpu.CompilerParams(vmem_limit_bytes=VMEM_LIMIT),
         name="round_rest",
     )(side, w_out, w_in, w_back, x)
 
@@ -309,7 +311,7 @@
                 pltpu.VMEM((blocks, seq, QB), F32),
             ],
         ),
-        compiler_params=pltpu.CompilerParams(vmem_limit_bytes=40 << 20),
+        compiler_params=pltpu.CompilerParams(vmem_limit_bytes=VMEM_LIMIT),
         cost_estimate=pl.CostEstimate(
             flops=16 * seq * seq * piece + 12 * seq * width * piece,
             bytes_accessed=16 * seq * piece,
@@ -347,7 +349,7 @@
                 pltpu.VMEM((seq, 128), F32),
             ],
         ),
-        compiler_params=pltpu.CompilerParams(vmem_limit_bytes=32 << 20),
+        compiler_params=pltpu.CompilerParams(vmem_limit_bytes=VMEM_LIMIT),
         cost_estimate=pl.CostEstimate(
             flops=16 * seq * seq * width,
             bytes_accessed=16 * seq * width,
@@ -500,18 +502,31 @@
         acc[rows(i), :] = jnp.zeros((RB, width), F32)
     fetch(teacher_hbm, 0, 0).start()
 
-    for p in range(4):
+    def up(p, carry):
         for r in range(2):
-            for copy in ffn_weights(p, r):
-                copy.wait()
+            pltpu.make_async_copy(
+                first[0].at[pl.ds(0, width), :],
+                w_in.at[p, :, pl.ds(r * side, side)],
+                w_sem.at[p, 2 + 3 * r],
+            ).wait()
+            for c in range(2):
+                pltpu.make_async_copy(
+                    first[0].at[pl.ds(0, side), :],
+                    w_back.at[p, pl.ds(r * side, side), pl.ds(c * half, half)],
+                    w_sem.at[p, 3 + 3 * r + c],
+                ).wait()
         for k in range(seq // FR):
             at = pl.ds(k * FR, FR)
-            pre = dot(mid_low[at, :], w_in[p]) + bias_in[:, p * units : (p + 1) * units]
+            bias = bias_in[:, pl.ds(pl.multiple_of(p * units, units), units)]
+            pre = dot(mid_low[at, :], w_in[p]) + bias
             act, der = gelu_parts(pre)
             act = act.astype(LOW)
             hidden[p, at, :] = act
             slope[p, at, :] = der
             acc[at, :] += dot(act, w_back[p])
+        return carry
+
+    lax.fori_loop(0, 4, up, 0)
 
     zero = jnp.zeros((1, width), F32)
     squares, gain_two, shift_two, shift_mid = zero, zero, zero, zero
@@ -543,21 +558,24 @@
     for store in stores[-2:]:
         store.wait()
 
-    pending = {}
     sides = (pl.ds(0, side), pl.ds(side, side))
 
-    def put(key, values, stage, slot, moves):
-        for copy in pending.get(key, ()):
-            copy.wait()
-        stage[slot] = values.astype(stage.dtype)
-        pending[key] = [
-            pltpu.make_async_copy(stage.at[slot].at[source], target, g_sem.at[key, n])
-            for n, (source, target) in enumerate(moves)
+    def moves(stage, target, key):
+        copies = [
+            (stage.at[0, :, sides[r]], target.at[r, 0], key) for r in range(2)
+        ] + [
+            (stage.at[1, sides[r], sides[c]], target.at[r, 1, sides[c], :], key)
+            for r in range(2)
+            for c in range(2)
         ]
-        for copy in pending[key]:
-            copy.start()
-
-    for p in (1, 3, 2, 0):
+        return [
+            pltpu.make_async_copy(source, to, g_sem.at[key, n])
+            for n, (source, to, key) in enumerate(copies)
+        ]
+
+    def down(n, carry, low_turn):
+        pair = n if low_turn else 1 - n
+        p = 2 * pair + (1 if low_turn else 0)
         total = jnp.zeros((1, units), F32)
         for k in range(seq // FR):
             at = pl.ds(k * FR, FR)
@@ -565,29 +583,25 @@
             pre_grad[at, :] = grad
             acc[at, :] += dot(grad, w_in[p], NT)
             total += column_sum(grad.astype(F32))
-        bias_sums[:, p * units : (p + 1) * units] = total
-        stage, target, key = (stage16, ffn_send, 0) if p % 2 else (stage32, ffn_keep, 2)
-        target = target.at[p // 2]
-        put(
-            key,
-            dot(mid_low[...], pre_grad[...], TN),
-            stage,
-            0,
-            [((slice(None), sides[r]), target.at[r, 0]) for r in range(2)],
-        )
-        put(
-            key + 1,
-            dot(hidden[p], dh_low[...], TN),
-            stage,
-            1,
-            [
-                ((sides[r], sides[c]), target.at[r, 1, sides[c], :])
-                for r in range(2)
-                for c in range(2)
-            ],
-        )
-    for copies in pending.values():
+        bias_sums[:, pl.ds(pl.multiple_of(p * units, units), units)] = total
+        stage, target, key = (stage16, ffn_send, 0) if low_turn else (stage32, ffn_keep, 1)
+        copies = moves(stage, target.at[pair], key)
+
+        @pl.when(n > 0)
+        def _():
+            for copy in copies:
+                copy.wait()
+
+        stage[0] = dot(mid_low[...], pre_grad[...], TN).astype(stage.dtype)
+        stage[1] = dot(hidden[p], dh_low[...], TN).astype(stage.dtype)
         for copy in copies:
+            copy.start()
+        return carry
+
+    lax.fori_loop(0, 2, functools.partial(down, low_turn=True), 0)
+    lax.fori_loop(0, 2, functools.partial(down, low_turn=False), 0)
+    for stage, target, key in ((stage16, ffn_send, 0), (stage32, ffn_keep, 1)):
+        for copy in moves(stage, target.at[0], key):
             copy.wait()
 
     gain_one, shift_one, shift_out = zero, zero, zero
@@ -661,9 +675,9 @@
             pltpu.SemaphoreType.DMA((4, 8)),
             pltpu.SemaphoreType.DMA((2,)),
             pltpu.SemaphoreType.DMA((2,)),
-            pltpu.SemaphoreType.DMA((4, 4)),
+            pltpu.SemaphoreType.DMA((2, 6)),
         ],
-        compiler_params=pltpu.CompilerParams(vmem_limit_bytes=63 << 20),
+        compiler_params=pltpu.CompilerParams(vmem_limit_bytes=VMEM_LIMIT),
         cost_estimate=pl.CostEstimate(
             flops=6 * seq * width * (8 * units + width),
             bytes_accessed=30 << 20,
@@ -673,125 +687,453 @@
     )(valid, scale, ctx_a, ctx_b, gains, shifts, bias_in, x, teacher, *first, *second)
 
 
-def projection_kernel(side_ref, x_ref, w0, w1, w2, w3, dqa, dka, dva, dqb, dkb, dvb, osend, okeep, dh_hbm, gx_hbm, send, keep, bias_ref, rows_in, rows_out, in_sem, out_sem):
+def swap(values, axis, bit):
+    size = lax.axis_size(axis)
+    return lax.ppermute(values, axis, [(i, i ^ (1 << bit)) for i in range(size)])
+
+
+def bits_of(axis):
+    return int(math.log2(lax.axis_size(axis)))
+
+
+def partner(axis, bit):
+    here = {name: lax.axis_index(name) for name in ("dp", "tensor")}
+    here[axis] = here[axis] ^ (1 << bit)
+    return here["dp"], here["tensor"]
+
+
+def greet(partners):
+    barrier = pltpu.get_barrier_semaphore()
+    for device in partners:
+        pl.semaphore_signal(
+            barrier, inc=1, device_id=device, device_id_type=pl.DeviceIdType.MESH
+        )
+    pl.semaphore_wait(barrier, len(partners))
+
+
+def count_kernel(dp_bits, lengths_ref, out_ref, held, send_sem, recv_sem):
+    greet([partner("dp", bit) for bit in range(dp_bits)])
+    total = jnp.full(out_ref.shape, 0, jnp.int32)
+    for i in range(lengths_ref.shape[0]):
+        total += lengths_ref[i]
+    for bit in range(dp_bits):
+        held[2 * bit] = total
+        copy = pltpu.make_async_remote_copy(
+            src_ref=held.at[2 * bit],
+            dst_ref=held.at[2 * bit + 1],
+            send_sem=send_sem.at[bit],
+            recv_sem=recv_sem.at[bit],
+            device_id=partner("dp", bit),
+            device_id_type=pl.DeviceIdType.MESH,
+        )
+        copy.start()
+        copy.wait()
+        total = total + held[2 * bit + 1]
+    out_ref[...] = total
+
+
+def count_tokens(lengths):
+    dp_bits = bits_of("dp")
+    return pl.pallas_call(
+        functools.partial(count_kernel, dp_bits),
+        out_shape=shape((8, 128), jnp.int32),
+        in_specs=[SMEM],
+        out_specs=VMEM,
+        scratch_shapes=[
+            pltpu.VMEM((2 * dp_bits, 8, 128), jnp.int32),
+            pltpu.SemaphoreType.DMA((dp_bits,)),
+            pltpu.SemaphoreType.DMA((dp_bits,)),
+        ],
+        compiler_params=pltpu.CompilerParams(collective_id=1, has_side_effects=True),
+        name="count_tokens",
+    )(lengths)
+
+
+def add_rows(out, terms, chunk=96):
+    rows = out.shape[0]
+    chunk = min(chunk, rows)
+
+    def step(i, carry):
+        at = pl.ds(pl.multiple_of(i * chunk, chunk), chunk)
+        total = terms[0][at, :].astype(F32)
+        for term in terms[1:]:
+            total += term[at, :].astype(F32)
+        out[at, :] = total.astype(out.dtype)
+        return carry
+
+    lax.fori_loop(0, rows // chunk, step, 0)
+
+
+def finish_kernel(
+    dp_bits,
+    x_ref,
+    w0,
+    w1,
+    w2,
+    w3,
+    dqa,
+    dka,
+    dva,
+    dqb,
+    dkb,
+    dvb,
+    osend,
+    okeep,
+    dh_hbm,
+    ffn_keep,
+    ffn_core,
+    ffn_x,
+    ffn_y,
+    small_ref,
+    gx_hbm,
+    result,
+    small_out,
+    loads,
+    loads16,
+    keep,
+    send,
+    core,
+    y_send,
+    y_recv,
+    x_send,
+    x_recv,
+    total,
+    z_send,
+    z_recv,
+    bias_ref,
+    small_held,
+    rows_in,
+    rows_out,
+    cross,
+    load_sem,
+    send_sem,
+    recv_sem,
+    in_sem,
+    out_sem,
+):
     seq, width = x_ref.shape
     half = width // 2
     piece = dqa.shape[1] // 2
     blocks = seq // RB
+    place = lax.axis_index("dp")
+    index = lax.axis_index("tensor")
+    side = place & 1
+    core_at, y_at = partner("tensor", 0), partner("tensor", 1)
+    dp_at = [partner("dp", bit) for bit in range(dp_bits)]
+    greet([core_at, y_at] + dp_at)
+    started = {}
+
+    def remote(key, source, target, device):
+        n = len(started)
+        started[key] = pltpu.make_async_remote_copy(
+            src_ref=source,
+            dst_ref=target,
+            send_sem=send_sem.at[n],
+            recv_sem=recv_sem.at[n],
+            device_id=device,
+            device_id_type=pl.DeviceIdType.MESH,
+        )
+        started[key].start()
+
+    def arrive(key):
+        started[key].wait_recv()
+
+    own = []
+    for n, (pair, r, w) in enumerate(((1, 0, 0), (0, 1, 1), (0, 0, 0), (0, 0, 1))):
+        own.append(
+            [
+                pltpu.make_async_copy(ffn_keep.at[pair, r, w], loads.at[n], load_sem.at[n, 0]),
+                pltpu.make_async_copy(ffn_core.at[pair, r, w], loads16.at[n, 0], load_sem.at[n, 1]),
+                pltpu.make_async_copy(
+                    ffn_x.at[pair] if w == 0 else ffn_y.at[r], loads16.at[n, 1], load_sem.at[n, 2]
+                ),
+            ]
+        )
+        for copy in own[n]:
+            copy.start()
+
+    def fetch(i):
+        return pltpu.make_async_copy(
+            dh_hbm.at[pl.ds(i * RB, RB), :], rows_in.at[i % 2], in_sem.at[i % 2]
+        )
+
+    fetch(0).start()
+
+    def load(n, out):
+        for copy in own[n]:
+            copy.wait()
+        add_rows(out, [loads.at[n], loads16.at[n, 0], loads16.at[n, 1]])
+
+    load(0, y_send.at[2])
+    remote("in y", y_send.at[2], y_recv.at[2], y_at)
+    load(1, x_send.at[1])
+    remote("back x", x_send.at[1], x_recv.at[1], dp_at[0])
+
     grads = ((dqa, dka, dva), (dqb, dkb, dvb))
-    mine = pl.ds(pl.multiple_of(side_ref[0] * half, half), half)
-    other = pl.ds(pl.multiple_of((1 - side_ref[0]) * half, half), half)
-
-    def fetch(i, slot):
-        return pltpu.make_async_copy(dh_hbm.at[pl.ds(i * RB, RB), :], rows_in.at[slot], in_sem.at[slot])
-
-    fetch(0, 0).start()
-    for g in range(2):
+    mine = pl.ds(pl.multiple_of(side * half, half), half)
+    other = pl.ds(pl.multiple_of((1 - side) * half, half), half)
+    for g in (1, 0):
         for i in range(3):
-            cross = dot(grads[g][i][...], x_ref[...], TN)
-            rows_out[:2 * piece, :] = cross
-            for n, at in enumerate((mine, other)):
-                keep[g, n, i * piece : (i + 1) * piece, :] = rows_out[:piece, at]
-                send[g, n, i * piece : (i + 1) * piece, :] = rows_out[piece : 2 * piece, at].astype(LOW)
+            cross[...] = dot(grads[g][i][...], x_ref[...], TN)
+            at = slice(i * piece, (i + 1) * piece)
+            for n, lanes in enumerate((mine, other)):
+                keep[g, n, at, :] = cross[:piece, lanes]
+                send[g, n, at, :] = cross[piece:, lanes].astype(LOW)
             bias_ref[g, i : i + 1, :] = column_sum(grads[g][i][...].astype(F32))
-        for n, at in enumerate((mine, other)):
-            keep[g, n, 3 * piece :, :] = okeep[g, :, at]
-            send[g, n, 3 * piece :, :] = osend[g, :, at]
+        for n, lanes in enumerate((mine, other)):
+            keep[g, n, 3 * piece :, :] = okeep[g, :, lanes]
+            send[g, n, 3 * piece :, :] = osend[g, :, lanes]
+        for n in (1, 0):
+            remote(("core", g, n), send.at[g, n], core.at[g, n], core_at)
+    for n in (1, 0):
+        arrive(("core", 1, n))
+        add_rows(y_send.at[n], [keep.at[1, n], core.at[1, n]])
+        remote(("y", n), y_send.at[n], y_recv.at[n], y_at)
+
+    small_held[0] = jnp.zeros(small_held.shape[1:], F32)
+    small_held[0, 16:24, :] = small_ref[0:8, :]
+    for p in range(4):
+        row = 4 * (index ^ p)
+        g, n = p // 2, p % 2
+        half_mine = small_ref[8 + p : 9 + p, :half]
+        half_other = small_ref[8 + p : 9 + p, half:]
+        low_half = jnp.where(side == 0, half_mine, half_other)
+        high_half = jnp.where(side == 0, half_other, half_mine)
+        small_held[0, pl.ds(row, 1), :] = jnp.concatenate([low_half, high_half], axis=1)
+        for i, k in enumerate((0, 2)):
+            values = bias_ref[g, k : k + 1, :]
+            if n == 1:
+                values = pltpu.roll(values, 2 * piece - piece, 1)
+            small_held[0, pl.ds(row + 1 + i, 1), :half] = values
+
     weights = ((w0, w1), (w2, w3))
     stores = []
-    for b in range(blocks):
+
+    def inputs_rows(b):
         at = pl.ds(b * RB, RB)
         if b + 1 < blocks:
-            fetch(b + 1, (b + 1) % 2).start()
-        fetch(b, b % 2).wait()
-        total = rows_in[b % 2]
+            fetch(b + 1).start()
+        fetch(b).wait()
+        grad = rows_in[b % 2]
         for g in range(2):
             for i in range(3):
-                w = jnp.concatenate([ref[i * piece : (i + 1) * piece, :] for ref in weights[g]], axis=0)
-                total += dot(grads[g][i][at, :], w)
-        if b >= 1:
-            stores[b - 1].wait()
-        rows_out[:RB, :] = total
-        stores.append(pltpu.make_async_copy(rows_out.at[pl.ds(0, RB), :], gx_hbm.at[at, :], out_sem))
+                rows = slice(i * piece, (i + 1) * piece)
+                w = jnp.concatenate([ref[rows, :] for ref in weights[g]], axis=0)
+                grad += dot(grads[g][i][at, :], w)
+        if b >= 2:
+            stores[b - 2].wait()
+        rows_out[b % 2] = grad
+        stores.append(
+            pltpu.make_async_copy(rows_out.at[b % 2], gx_hbm.at[at, :], out_sem.at[b % 2])
+        )
         stores[b].start()
-    stores[-1].wait()
-
-
-def projections(side, x, weights, grads, osend, okeep, dh):
+
+    def small_step(n):
+        bits = [core_at, y_at] + dp_at
+        remote(("small", n), small_held.at[2 * n], small_held.at[2 * n + 1], bits[n])
+
+    def small_sum(n):
+        arrive(("small", n))
+        out = small_held.at[2 * n + 2] if n < dp_bits + 1 else small_out
+        out[...] = small_held[2 * n] + small_held[2 * n + 1]
+
+    rows_of = [width]
+    for bit in range(1, min(dp_bits, 3)):
+        rows_of.append(rows_of[-1] // 2)
+
+    def offset(level):
+        at = 0
+        for bit in range(1, level + 1):
+            at = at + ((place >> bit) & 1) * rows_of[bit]
+        return pl.multiple_of(at, rows_of[level])
+
+    def other_offset(level):
+        return pl.multiple_of(
+            offset(level - 1) + (1 - ((place >> level) & 1)) * rows_of[level], rows_of[level]
+        )
+
+    levels = min(dp_bits, 3) - 1
+
+    def scatter(w, level):
+        size = rows_of[level]
+        out = z_send.at[w, pl.ds(0, size), :] if level == 1 else z_send.at[w, pl.ds(rows_of[1], size), :]
+        into = z_recv.at[w, pl.ds(0, size), :] if level == 1 else z_recv.at[w, pl.ds(rows_of[1], size), :]
+        add_rows(out, [total.at[w, pl.ds(other_offset(level), size), :]])
+        remote((w, "z", level), out, into, dp_at[level])
+
+    def collect(w, level):
+        size = rows_of[level]
+        arrive((w, "z", level))
+        into = z_recv.at[w, pl.ds(0, size), :] if level == 1 else z_recv.at[w, pl.ds(rows_of[1], size), :]
+        mine = total.at[w, pl.ds(offset(level), size), :]
+        add_rows(mine, [mine, into])
+
+    def settle(w):
+        size = rows_of[levels]
+        at = pl.ds(offset(levels), size)
+        add_rows(result.at[w, 0, at, :], [total.at[w, at, :]])
+        for bit in range(levels + 1, dp_bits):
+            spare = result.at[w, 0, at, :]
+            into = z_recv.at[w, pl.ds(rows_of[1] + (bit - levels) * size, size), :]
+            remote((w, "all", bit), spare, into, dp_at[bit])
+            started[(w, "all", bit)].wait_send()
+            arrive((w, "all", bit))
+            add_rows(spare, [spare, into])
+
+    def spread(w, level):
+        if level == 0:
+            remote((w, "gather", 0), result.at[w, 0], result.at[w, 1], dp_at[0])
+        else:
+            rows = result.at[w, 0, pl.ds(offset(level), rows_of[level]), :]
+            remote((w, "gather", level), rows, rows, dp_at[level])
+
+    small_step(0)
+    for b in range(blocks):
+        inputs_rows(b)
+        if b < dp_bits + 2:
+            small_sum(b)
+            if b + 1 < dp_bits + 2:
+                small_step(b + 1)
+
+    load(2, total.at[0])
+    load(3, total.at[1])
+    arrive("in y")
+    add_rows(total.at[0], [total.at[0], y_recv.at[2]])
+    scatter(0, 1)
+    arrive("back x")
+    add_rows(total.at[1], [total.at[1], x_recv.at[1]])
+    scatter(1, 1)
+    for n in range(blocks, dp_bits + 2):
+        small_sum(n)
+        if n + 1 < dp_bits + 2:
+            small_step(n + 1)
+    arrive(("core", 0, 1))
+    arrive(("core", 0, 0))
+    collect(0, 1)
+    scatter(0, 2)
+    arrive(("y", 1))
+    add_rows(x_send.at[0], [keep.at[0, 1], core.at[0, 1], y_recv.at[1]])
+    remote("qkv x", x_send.at[0], x_recv.at[0], dp_at[0])
+    collect(1, 1)
+    scatter(1, 2)
+    collect(0, 2)
+    settle(0)
+    spread(0, 2)
+    collect(1, 2)
+    settle(1)
+    spread(1, 2)
+    arrive((0, "gather", 2))
+    spread(0, 1)
+    arrive(("y", 0))
+    add_rows(total.at[2], [keep.at[0, 0], core.at[0, 0], y_recv.at[0]])
+    arrive("qkv x")
+    add_rows(total.at[2], [total.at[2], x_recv.at[0]])
+    scatter(2, 1)
+    arrive((1, "gather", 2))
+    spread(1, 1)
+    arrive((0, "gather", 1))
+    spread(0, 0)
+    collect(2, 1)
+    scatter(2, 2)
+    arrive((1, "gather", 1))
+    spread(1, 0)
+    collect(2, 2)
+    settle(2)
+    spread(2, 2)
+    arrive((2, "gather", 2))
+    spread(2, 1)
+    arrive((2, "gather", 1))
+    spread(2, 0)
+    for w in range(3):
+        arrive((w, "gather", 0))
+    for key, copy in started.items():
+        if not (isinstance(key, tuple) and len(key) == 3 and key[1] == "all"):
+            copy.wait_send()
+    for store in stores[-2:]:
+        store.wait()
+
+
+def finish(x, weights, grads, osend, okeep, dh, ffn_keep, ffn_core, ffn_x, ffn_y, small):
     seq, width = x.shape
     half = width // 2
     piece = grads[0].shape[1] // 2
-    total = 3 * piece + osend.shape[1]
+    dp_bits = bits_of("dp")
+    slab = (width, half)
+    copies = 9 + dp_bits + 2 + 3 * (2 + 3 + max(dp_bits - 3, 0))
     return pl.pallas_call(
-        projection_kernel,
+        functools.partial(finish_kernel, dp_bits),
         out_shape=(
             shape((seq, width), F32),
-            shape((2, 2, total, half), LOW),
-            shape((2, 2, total, half), F32),
-            shape((2, 8, 2 * piece), F32),
+            shape((3, 2) + slab, LOW),
+            shape((24, width), F32),
         ),
-        in_specs=[SMEM] + [VMEM] * 13 + [HBM],
-        out_specs=(HBM, VMEM, VMEM, VMEM),
+        in_specs=[VMEM] * 13 + [HBM] * 5 + [VMEM],
+        out_specs=(HBM, VMEM, VMEM),
         scratch_shapes=[
+            pltpu.VMEM((4,) + slab, F32),
+            pltpu.VMEM((4, 2) + slab, LOW),
+            pltpu.VMEM((2, 2) + slab, F32),
+            pltpu.VMEM((2, 2) + slab, LOW),
+            pltpu.VMEM((2, 2) + slab, LOW),
+            pltpu.VMEM((3,) + slab, LOW),
+            pltpu.VMEM((3,) + slab, LOW),
+            pltpu.VMEM((2,) + slab, LOW),
+            pltpu.VMEM((2,) + slab, LOW),
+            pltpu.VMEM((3,) + slab, F32),
+            pltpu.VMEM((3, width, half), LOW),
+            pltpu.VMEM((3, 2 * width, half), LOW),
+            pltpu.VMEM((2, 8, 2 * piece), F32),
+            pltpu.VMEM((2 * dp_bits + 4, 24, width), F32),
+            pltpu.VMEM((2, RB, width), F32),
             pltpu.VMEM((2, RB, width), F32),
             pltpu.VMEM((2 * piece, width), F32),
+            pltpu.SemaphoreType.DMA((4, 3)),
+            pltpu.SemaphoreType.DMA((copies,)),
+            pltpu.SemaphoreType.DMA((copies,)),
             pltpu.SemaphoreType.DMA((2,)),
-            pltpu.SemaphoreType.DMA,
+            pltpu.SemaphoreType.DMA((2,)),
         ],
-        compiler_params=pltpu.CompilerParams(vmem_limit_bytes=50 << 20),
+        compiler_params=pltpu.CompilerParams(
+            vmem_limit_bytes=VMEM_LIMIT, collective_id=2, has_side_effects=True
+        ),
         cost_estimate=pl.CostEstimate(
-            flops=24 * seq * width * piece * 2, bytes_accessed=30 << 20, transcendentals=0
+            flops=48 * seq * width * piece, bytes_accessed=50 << 20, transcendentals=0
         ),
-        name="projections",
-    )(side, x, *weights, *grads, osend, okeep, dh)
-
-
-def swap(values, axis, bit):
-    size = lax.axis_size(axis)
-    return lax.ppermute(values, axis, [(i, i ^ (1 << bit)) for i in range(size)])
-
-
-def bits_of(axis):
-    return int(math.log2(lax.axis_size(axis)))
-
-
-def halves(values, bit_set, axis):
-    half = values.shape[axis] // 2
-    keep = lax.dynamic_slice_in_dim(values, bit_set * half, half, axis)
-    send = lax.dynamic_slice_in_dim(values, (1 - bit_set) * half, half, axis)
-    return keep, send
-
-
-def join(mine, other, bit_set, axis):
-    low = jnp.where(bit_set == 0, mine, other)
-    high = jnp.where(bit_set == 0, other, mine)
-    return jnp.concatenate([low, high], axis=axis)
-
-
-def reduce_pieces(send, keep):
-    from_core = swap(send, "tensor", 0)
-    away = (keep[1] + from_core[1].astype(F32)).astype(LOW)
-    from_y = swap(away, "tensor", 1)
-    total = keep[0] + from_core[0].astype(F32) + from_y.astype(F32)
-    total = total[0] + swap(total[1].astype(LOW), "dp", 0).astype(F32)
-    place = lax.axis_index("dp")
-    for bit in range(1, bits_of("dp")):
-        mine, other = halves(total, (place >> bit) & 1, total.ndim - 2)
-        total = mine + swap(other.astype(LOW), "dp", bit).astype(F32)
-    total = total.astype(LOW)
-    for bit in reversed(range(1, bits_of("dp"))):
-        total = join(total, swap(total, "dp", bit), (place >> bit) & 1, total.ndim - 2)
-    side = place & 1
-    other = swap(total, "dp", 0)
-    return jnp.where(side == 0, total, other).astype(F32), jnp.where(side == 0, other, total).astype(F32)
-
-
-def reduce_all(values):
-    for bit in range(bits_of("tensor")):
-        values = values + swap(values, "tensor", bit)
-    for bit in range(bits_of("dp")):
-        values = values + swap(values, "dp", bit)
-    return values
+        name="finish",
+    )(x, *weights, *grads, osend, okeep, dh, ffn_keep, ffn_core, ffn_x, ffn_y, small)
+
+
+def widen_kernel(side_ref, result, qkv_ref, out_ref, in_ref, back_ref):
+    half = result.shape[3]
+    rows = out_ref.shape[0]
+    piece = qkv_ref.shape[2]
+    side = side_ref[0]
+    for n in range(2):
+        natural = (side + n) % 2
+        at = pl.ds(pl.multiple_of(natural * half, half), half)
+        in_ref[:, at] = result[0, n].astype(F32)
+        for c in range(2):
+            back_ref[at, c * half : (c + 1) * half] = result[1, n, c * half : (c + 1) * half, :].astype(F32)
+        for i in range(3):
+            qkv_ref[i, at, :] = result[2, n, i * piece : (i + 1) * piece, :].astype(F32).T
+        out_ref[:, at] = result[2, n, 3 * piece :, :].astype(F32)
+
+
+def widen(side, result, piece, rows):
+    width, half = result.shape[2:]
+    return pl.pallas_call(
+        widen_kernel,
+        out_shape=(
+            shape((3, width, piece), F32),
+            shape((rows, width), F32),
+            shape((width, 2 * half), F32),
+            shape((2 * half, width), F32),
+        ),
+        in_specs=[SMEM, VMEM],
+        out_specs=(VMEM,) * 4,
+        compiler_params=pltpu.CompilerParams(vmem_limit_bytes=VMEM_LIMIT),
+        name="widen",
+    )(side, result)
 
 
 def per_device(
@@ -833,21 +1175,24 @@
     table = span_tables(segments, valid, seq)
 
     qa, ka, va, ctx_a, lse_a = attend_forward(table, x_low, near, core, code, seg)
+    first, second, far, first_far, lengths, ctx_a = lax.optimization_barrier(
+        (first, second, far, first_far, valid_lengths, ctx_a)
+    )
     core_far = swap(far, "tensor", 0)
+    second_far = swap(first_far[2 * piece :], "dp", 0)
     first_core = swap(first, "tensor", 0)
     second_core = swap(second, "tensor", 0)
-    token_count = jnp.sum(valid_lengths)
-    for bit in range(bits_of("dp")):
-        token_count = token_count + swap(token_count, "dp", bit)
-    token_count = token_count.astype(F32)
+    first_core_far = swap(first_far, "tensor", 0)
+    token_count = count_tokens(lengths)[0, 0].astype(F32)
     qb, kb, vb, ctx_b, lse_b = attend_forward(table, x_low, far, core_far, code, seg)
-    second_far = swap(first_far[2 * piece :], "dp", 0)
-    first_core_far = swap(first_far, "tensor", 0)
+    second_far, ctx_b = lax.optimization_barrier((second_far, ctx_b))
     second_core_far = swap(second_far, "tensor", 0)
     at = 3 * piece
     bias_in = jnp.concatenate(
         [
-            part[at : at + 1].astype(F32) + part[at + 1 : at + 2].astype(F32) + part[at + 2 : at + 3].astype(F32)
+            part[at : at + 1].astype(F32)
+            + part[at + 1 : at + 2].astype(F32)
+            + part[at + 2 : at + 3].astype(F32)
             for part in (near, core, far, core_far)
         ],
         axis=1,
@@ -866,49 +1211,44 @@
         (first, first_core, first_far, first_core_far),
         (second, second_core, second_far, second_core_far),
     )
-    low_ffn, high_ffn = reduce_pieces(ffn_send, ffn_keep)
+    ffn_core = swap(ffn_send, "tensor", 0)
+    grads_b = attend_backward(table, qb, kb, vb, cg_b, lse_b, code, seg)
+    ffn_core, ffn_keep, *grads_b = lax.optimization_barrier((ffn_core, ffn_keep, *grads_b))
+    to_x = (ffn_keep[:, 1, 0] + ffn_core[:, 1, 0].astype(F32)).astype(LOW)
+    to_y = (ffn_keep[1, :, 1] + ffn_core[1, :, 1].astype(F32)).astype(LOW)
+    to_x, to_y, cg_a = lax.optimization_barrier((to_x, to_y, cg_a))
+    ffn_x = swap(to_x, "dp", 0)
+    ffn_y = swap(to_y, "tensor", 1)
     grads_a = attend_backward(table, qa, ka, va, cg_a, lse_a, code, seg)
-    grads_b = attend_backward(table, qb, kb, vb, cg_b, lse_b, code, seg)
-    grad_inputs, send, keep, bias_qv = projections(
-        side_row, x_low, (near, core, far, core_far), grads_a + grads_b, out_send, out_keep, dh_one
+    small = jnp.concatenate([sums, bias_sums.reshape(4, units), jnp.zeros((4, width), F32)], axis=0)
+    grad_inputs, slabs, small = finish(
+        x_low,
+        (near, core, far, core_far),
+        (*grads_a, *grads_b),
+        out_send,
+        out_keep,
+        dh_one,
+        ffn_keep,
+        ffn_core,
+        ffn_x,
+        ffn_y,
+        small,
     )
-    low_qkv, high_qkv = reduce_pieces(send, keep)
-
-    grad_w_in = jnp.concatenate([low_ffn[0], high_ffn[0]], axis=1)
-    grad_w_back = jnp.concatenate(
-        [
-            jnp.concatenate([part[1, :half], part[1, half:]], axis=1)
-            for part in (low_ffn, high_ffn)
-        ],
-        axis=0,
-    )
-    rows = jnp.concatenate([low_qkv, high_qkv], axis=1)
-    grad_w_qkv = rows[: 3 * piece].reshape(3, piece, width).transpose(0, 2, 1)
-    grad_w_out = rows[3 * piece :]
-
-    bias_in_sums = bias_sums.reshape(4, 2, units // 2)
-    bias_in_sums = jnp.where(side == 0, bias_in_sums, bias_in_sums[:, ::-1]).reshape(4, units)
-    bias_qv_sums = bias_qv[:, (0, 2), :].reshape(2, 2, 2, piece).transpose(0, 2, 1, 3).reshape(4, 2 * piece)
-    by_shard = jnp.concatenate([bias_qv_sums, bias_in_sums], axis=1)
-    flipped = jnp.where((index & 1) == 0, by_shard, by_shard[jnp.array([1, 0, 3, 2])])
-    natural = jnp.where((index & 2) == 0, flipped, flipped[jnp.array([2, 3, 0, 1])])
-    wide = by_shard.shape[1]
-    small = reduce_all(jnp.concatenate([natural.reshape(-1), sums[:7].reshape(-1)]))
-    own = lax.dynamic_slice_in_dim(small, index * wide, wide)
-    rest = small[4 * wide :].reshape(7, width)
-    loss = jnp.sum(rest[6]) / (2.0 * width * token_count)
+    grad_w_qkv, grad_w_out, grad_w_in, grad_w_back = widen(side_row, slabs, piece, w_out.shape[0])
+    own = lax.dynamic_slice_in_dim(small, 4 * index, 4)
+    loss = jnp.sum(small[22]) / (2.0 * width * token_count)
     return (
         output.reshape(own_seqs, seq, width),
         loss,
         grad_inputs.reshape(own_seqs, seq, width),
         grad_w_qkv,
-        own[: 2 * piece].reshape(2, piece),
+        own[1:3, :piece],
         grad_w_out,
         grad_w_in,
-        own[2 * piece :],
+        own[0],
         grad_w_back,
-        rest[:2],
-        rest[2:6],
+        small[16:18],
+        small[18:22],
     )
 
 

time: 533 us -> 413 us (0.77)
  the two profiles are of different devices: /device:TPU:0 before, /device:TPU:20 now
where the time goes in v3:
time: 413 us; the launch traced here: 406 us
  Pallas kernels  334 us (81%)
  local copies, waits for them, and re-layouts  29.5 us (7%)
  waiting for transfers between devices  16.6 us (4%)
  other arithmetic  16.2 us (4%)
  starting transfers between devices  6.03 us (1%)
    pallas_call x1, Pallas kernels, finish(): pl.pallas_call(functools.partial(finish_kernel, dp_bits), out_shape=(shap...  147 us
    pallas_call x1, Pallas kernels, middle(): pl.pallas_call(middle_kernel, out_shape=(shape((seq, width), F32), shape(...  65.5 us
    pallas_call x2, Pallas kernels, attend_forward(): pl.pallas_call(forward_kernel, out_shape=(shape((seq, 2 * piece), LOW),)...  49.2 us
    pallas_call x2, Pallas kernels, attend_backward(): pl.pallas_call(backward_kernel, out_shape=(shape((seq, width), LOW),) * 3...  46.5 us
    ppermute x12, waiting for transfers between devices, swap(): return lax.ppermute(values, axis, [(i, i ^ 1 << bit) for i in range(size)])  16.6 us
    pallas_call x1, Pallas kernels, count_tokens(): pl.pallas_call(functools.partial(count_kernel, dp_bits), out_shape=shape(...  12.1 us
    unnamed x23, local copies, waits for them, and re-layouts  9.64 us
  transfers between devices with their start and end apart: 12, of which 2 were waited for; matrix products, arithmetic and copies ran while one was open for 5% of the time, Pallas kernels for 27%

profile of v3, /device:TPU:20, one launch (start us, length us, event | category | flops | bytes accessed | tf_op | source)
XLA Modules:
  0.0 406.1 jit_solution(8596207429089739219)
XLA Ops:
  0.7 5.6 %round_rest.1 = (bf16[1920,384]{1,0:T(8,128)(2,1)}, bf16[1536,384]{1,0:T(8,128)(2,1)}, bf16[1024,768]{1,0:T(8,128)(2,1)}) custom-call(s32[1]{0:T(128)} %bitcast.side_ref, f32[192,768]{1,0:T(8,128)} %wo_ref.1, f32[768,768]{1,0:T(8,128)} %wi_ref.1, f32[768,768]{1,0:T(8,128)} %wb_ref.1, f32[1024,768]{1,0:T(8,128)} %bitcast.31), custom_call_target="tpu_custom_call" | custom-call | tf_op jit(solution)/shard_map/round_rest/pallas_call | solution.py:100
  6.8 2.9 copy.36.w_ref
  10.3 3.0 round_qkv.1.w0_ref.w0
  13.3 1.5 collective-permute-start
  17.4 1.5 fusion.4.code_ref
  18.9 1.0 copy-done.3
  19.9 24.5 %attend_forward.2 = (bf16[1024,384]{1,0:T(8,128)(2,1)}, bf16[1024,384]{1,0:T(8,128)(2,1)}, bf16[1024,384]{1,0:T(8,128)(2,1)}, bf16[1024,384]{1,0:T(8,128)(2,1)}, f32[3,8,1024]{2,1,0:T(8,128)}) custom-call(s32[2,4]{1,0:T(2,128)} %pad_add_fusion.table_ref, bf16[1024,768]{1,0:T(8,128)(2,1)} %get-tuple-element.65.x_ref, bf16[592,768]{1,0:T(8,128)(2,1)} %round_qkv.1.w0_ref.w0, ...), custom_call_target="tpu_custom_call" | custom-call | flops 5033164800 | bytes 3145728 | tf_op jit(solution)/shard_map/attend_forward/pallas_call | solution.py:287
  44.4 15.7 %collective-permute-done.w0_ref.w2 = bf16[592,768]{1,0:T(8,128)(2,1)} collective-permute-done((bf16[592,768]{1,0:T(8,128)(2,1)}, bf16[592,768]{1,0:T(8,128)(2,1)}, u32[]{:S(2)}, u32[]{:S(2)}) %collective-permute-start) | collective-permute-done | bytes 909344 | tf_op jit(solution)/shard_map/ppermute | solution.py:692
  60.1 2.4 slice.78
  62.5 1.5 collective-permute-start.3
  64.8 0.9 copy-done.4
  65.7 24.7 %attend_forward.3 = (bf16[1024,384]{1,0:T(8,128)(2,1)}, bf16[1024,384]{1,0:T(8,128)(2,1)}, bf16[1024,384]{1,0:T(8,128)(2,1)}, bf16[1024,384]{1,0:T(8,128)(2,1)}, f32[3,8,1024]{2,1,0:T(8,128)}) custom-call(s32[2,4]{1,0:T(2,128)} %pad_add_fusion.table_ref, bf16[1024,768]{1,0:T(8,128)(2,1)} %get-tuple-element.65.x_ref, ...), custom_call_target="tpu_custom_call" | custom-call | flops 5033164800 | bytes 3145728 | tf_op jit(solution)/shard_map/attend_forward/pallas_call | solution.py:287
  90.4 0.8 collective-permute-done.3.r1c
  92.1 0.8 fusion.7
  92.9 12.1 %count_tokens.1 = s32[8,128]{1,0:T(8,128)} custom-call(s32[4]{0:T(128)} %lengths_ref), custom_call_target="tpu_custom_call" | custom-call | tf_op jit(solution)/shard_map/count_tokens/pallas_call | solution.py:737
  105.0 1.2 slice.77
  109.2 65.5 %middle.1 = (f32[1024,768]{1,0:T(8,128)}, f32[1024,768]{1,0:T(8,128)}, bf16[1024,384]{1,0:T(8,128)(2,1)}, bf16[1024,384]{1,0:T(8,128)(2,1)}, bf16[2,2,2,768,384]...) custom-call(s32[1]{0:T(128)} %dynamic_slice.11.valid_ref, ...), custom_call_target="tpu_custom_call" | custom-call | flops 32614907904 | bytes 31457280 | tf_op jit(solution)/shard_map/middle/pallas_call | solution.py:643
  174.7 5.0 %copy.38 = bf16[2,2,2,768,384]{4,3,1,2,0:T(8,128)(2,1)} copy(bf16[2,2,2,768,384]{4,3,2,1,0:T(8,128)(2,1)} %get-tuple-element.80) | data formatting | bytes 9437184 | tf_op jit(solution)/shard_map/middle/pallas_call | solution.py:643
  179.7 23.2 %attend_backward.2 = (bf16[1024,384]{1,0:T(8,128)(2,1)}, bf16[1024,384]{1,0:T(8,128)(2,1)}, bf16[1024,384]{1,0:T(8,128)(2,1)}) custom-call(s32[2,4]{1,0:T(2,128)} %pad_add_fusion.table_ref, bf16[1024,384]{1,0:T(8,128)(2,1)} %get-tuple-element.82.q_ref, bf16[1024,384]{1,0:T(8,128)(2,1)} %get-tuple-element.83.k_ref, ...), custom_call_target="tpu_custom_call" | custom-call | flops 6442450944 | bytes 6291456 | tf_op jit(solution)/shard_map/attend_backward/pallas_call | solution.py:329
  203.0 3.3 fusion.3
  206.3 3.3 fusion.2
  209.6 1.8 collective-permute-start.11
  213.3 5.1 %copy.41.ffn_core = bf16[2,2,2,768,384]{4,3,2,1,0:T(8,128)(2,1)} copy(bf16[2,2,2,768,384]{4,3,1,2,0:T(8,128)(2,1)} %collective-permute-done.9) | data formatting | bytes 9437184 | tf_op jit(solution)/shard_map/optimization_barrier | solution.py:1216
  218.4 23.3 %attend_backward.3 = (bf16[1024,384]{1,0:T(8,128)(2,1)}, bf16[1024,384]{1,0:T(8,128)(2,1)}, bf16[1024,384]{1,0:T(8,128)(2,1)}) custom-call(s32[2,4]{1,0:T(2,128)} %pad_add_fusion.table_ref, bf16[1024,384]{1,0:T(8,128)(2,1)} %get-tuple-element.77.q_ref, bf16[1024,384]{1,0:T(8,128)(2,1)} %get-tuple-element.78.k_ref, ...), custom_call_target="tpu_custom_call" | custom-call | flops 6442450944 | bytes 6291456 | tf_op jit(solution)/shard_map/attend_backward/pallas_call | solution.py:329
  241.7 146.5 %finish.1 = (f32[1024,768]{1,0:T(8,128)}, bf16[3,2,768,384]{3,2,1,0:T(8,128)(2,1)}, f32[24,768]{1,0:T(8,128)}) custom-call(bf16[1024,768]{1,0:T(8,128)(2,1)} %get-tuple-element.65.x_ref, bf16[592,768]{1,0:T(8,128)(2,1)} %round_qkv.1.w0_ref.w0, bf16[592,768]{1,0:T(8,128)(2,1)} %copy-done.3, bf16[592,768]{1,0:T(8,128)(2,1)} %collective-permute-done.w0_ref.w2, ...), custom_call_target="tpu_custom_call" | custom-call | flops 7247757312 | bytes 52428800 | tf_op jit(solution)/shard_map/finish/pallas_call | solution.py:1063
  388.2 1.3 slice.99
  389.6 1.4 dynamic-slice_reduce_fusion
  391.0 1.3 slice.98
  392.3 5.5 %widen.1 = (f32[3,768,192]{2,1,0:T(8,128)}, f32[192,768]{1,0:T(8,128)}, f32[768,768]{1,0:T(8,128)}, f32[768,768]{1,0:T(8,128)}) custom-call(s32[1]{0:T(128)} %bitcast.side_ref, bf16[3,2,768,384]{3,2,1,0:T(8,128)(2,1)} %get-tuple-element.110.result), custom_call_target="tpu_custom_call" | custom-call | tf_op jit(solution)/shard_map/widen/pallas_call | solution.py:1124
  397.8 3.1 copy.42
  400.9 1.3 constant_dynamic-slice_fusion
  402.9 1.7 copy.48
  (57 shorter events, 9.4 us)
Async XLA Ops:
  0.6 14.2 %copy-start = (s32[4,1024]{1,0:T(4,128)S(1)}, s32[4,1024]{1,0:T(4,128)}, u32[]{:S(2)}) copy-start(s32[4,1024]{1,0:T(4,128)} %param.21) | copy-start | bytes 49156
  6.3 3.5 copy-start.8
  6.3 53.8 %collective-permute-start.1 = (bf16[1920,384]{1,0:T(8,128)(2,1)}, bf16[1920,384]{1,0:T(8,128)(2,1)}, u32[]{:S(2)}, u32[]{:S(2)}) collective-permute-start(bf16[1920,384]{1,0:T(8,128)(2,1)} %get-tuple-element.73.r0a), channel_id=1, source_target_pairs={{0,2},{1,3},{2,0},{3,1},{4,6},{5,7},{6,4},{7,5},{8,10},{9,11},{10,... | collective-permute-start | bytes 4423688 | tf_op jit(solution)/shard_map/ppermute | solution.py:692
  9.8 5.3 %copy-start.9 = (s32[4]{0:T(128)S(1)}, s32[4]{0:T(128)}, u32[]{:S(2)}) copy-start(s32[4]{0:T(128)} %lengths_ref) | copy-start | bytes 52
  13.3 5.5 %collective-permute-start.2 = (bf16[592,768]{1,0:T(8,128)(2,1)}, bf16[592,768]{1,0:T(8,128)(2,1)S(1)}, u32[]{:S(2)}, u32[]{:S(2)}) collective-permute-start(bf16[592,768]{1,0:T(8,128)(2,1)} %round_qkv.1.w0_ref.w0), channel_id=1, source_target_pairs={{0,1},{1,0},{2,3},{3,2},{4,5},{5,4},{6,7},{7,6},{8,9},{9,8},{10,11... | collective-permute-start | bytes 2727944 | tf_op jit(solution)/shard_map/ppermute | solution.py:692
  13.3 46.8 %collective-permute-start = (bf16[592,768]{1,0:T(8,128)(2,1)}, bf16[592,768]{1,0:T(8,128)(2,1)}, u32[]{:S(2)}, u32[]{:S(2)}) collective-permute-start(bf16[592,768]{1,0:T(8,128)(2,1)} %round_qkv.1.w0_ref.w0), channel_id=1, source_target_pairs={{0,2},{1,3},{2,0},{3,1},{4,6},{5,7},{6,4},{7,5},{8,10},{9,11},{10,... | collective-permute-start | bytes 2727944 | tf_op jit(solution)/shard_map/ppermute | solution.py:692
  14.9 4.0 copy-start.6
  18.9 1.0 copy-start.3
  60.1 4.6 %collective-permute-start.4 = (bf16[592,768]{1,0:T(8,128)(2,1)}, bf16[592,768]{1,0:T(8,128)(2,1)S(1)}, u32[]{:S(2)}, u32[]{:S(2)}) collective-permute-start(bf16[592,768]{1,0:T(8,128)(2,1)} %collective-permute-done.w0_ref.w2), channel_id=1, source_target_pairs={{0,1},{1,0},{2,3},{3,2},{4,5},{5,4},{6,7},{7,6},{8,9},{9,8},{10,11... | collective-permute-start | bytes 2727944 | tf_op jit(solution)/shard_map/ppermute | solution.py:692
  62.5 28.7 %collective-permute-start.3 = (bf16[1536,384]{1,0:T(8,128)(2,1)}, bf16[1536,384]{1,0:T(8,128)(2,1)}, u32[]{:S(2)}, u32[]{:S(2)}) collective-permute-start(bf16[1536,384]{1,0:T(8,128)(2,1)} %slice.78), channel_id=1, source_target_pairs={{0,4},{4,0},{8,12},{12,8},{16,20},{20,16},{24,28},{28,24},{1,5},{5... | collective-permute-start | bytes 3538952 | tf_op jit(solution)/shard_map/ppermute | solution.py:692
  64.0 45.1 %collective-permute-start.6 = (bf16[1920,384]{1,0:T(8,128)(2,1)}, bf16[1920,384]{1,0:T(8,128)(2,1)}, u32[]{:S(2)}, u32[]{:S(2)}) collective-permute-start(bf16[1920,384]{1,0:T(8,128)(2,1)} %collective-permute-done.1.r0c), channel_id=1, source_target_pairs={{0,1},{1,0},{2,3},{3,2},{4,5},{5,4},{6,7},{7,6},{8,9},{9,8},{10,11... | collective-permute-start | bytes 4423688 | tf_op jit(solution)/shard_map/ppermute | solution.py:692
  64.3 44.9 %collective-permute-start.5 = (bf16[1920,384]{1,0:T(8,128)(2,1)}, bf16[1920,384]{1,0:T(8,128)(2,1)}, u32[]{:S(2)}, u32[]{:S(2)}) collective-permute-start(bf16[1920,384]{1,0:T(8,128)(2,1)} %get-tuple-element.73.r0a), channel_id=1, source_target_pairs={{0,1},{1,0},{2,3},{3,2},{4,5},{5,4},{6,7},{7,6},{8,9},{9,8},{10,11... | collective-permute-start | bytes 4423688 | tf_op jit(solution)/shard_map/ppermute | solution.py:692
  64.5 44.6 %collective-permute-start.7 = (bf16[1536,384]{1,0:T(8,128)(2,1)}, bf16[1536,384]{1,0:T(8,128)(2,1)}, u32[]{:S(2)}, u32[]{:S(2)}) collective-permute-start(bf16[1536,384]{1,0:T(8,128)(2,1)} %get-tuple-element.74.r1a), channel_id=1, source_target_pairs={{0,1},{1,0},{2,3},{3,2},{4,5},{5,4},{6,7},{7,6},{8,9},{9,8},{10,11... | collective-permute-start | bytes 3538952 | tf_op jit(solution)/shard_map/ppermute | solution.py:692
  64.8 0.9 copy-start.4
  91.2 17.9 %collective-permute-start.8 = (bf16[1536,384]{1,0:T(8,128)(2,1)}, bf16[1536,384]{1,0:T(8,128)(2,1)}, u32[]{:S(2)}, u32[]{:S(2)}) collective-permute-start(bf16[1536,384]{1,0:T(8,128)(2,1)} %collective-permute-done.3.r1c), channel_id=1, source_target_pairs={{0,1},{1,0},{2,3},{3,2},{4,5},{5,4},{6,7},{7,6},{8,9},{9,8},{10,11... | collective-permute-start | bytes 3538952 | tf_op jit(solution)/shard_map/ppermute | solution.py:692
  179.7 23.2 %collective-permute-start.9 = (bf16[2,2,2,768,384]{4,3,1,2,0:T(8,128)(2,1)}, bf16[2,2,2,768,384]{4,3,1,2,0:T(8,128)(2,1)}, u32[]{:S(2)}, u32[]{:S(2)}) collective-permute-start(bf16[2,2,2,768,384]{4,3,1,2,0:T(8,128)(2,1)} %copy.38), channel_id=1, source_target_pairs={{0,1},{1,0},{2,3},{3,2},{4,5},{5,4},{6,7},{7,6},{8,9},{9,8},{10,11... | collective-permute-start | bytes 14155784 | tf_op jit(solution)/shard_map/ppermute | solution.py:692
  206.3 5.7 %copy-start.7 = (f32[1,3072]{1,0:T(1,128)S(1)}, f32[1,3072]{1,0:T(1,128)}, u32[]{:S(2)}) copy-start(f32[1,3072]{1,0:T(1,128)} %get-tuple-element.107) | copy-start | bytes 36868
  206.3 6.4 %copy-start.5 = (f32[8,768]{1,0:T(8,128)S(1)}, f32[8,768]{1,0:T(8,128)}, u32[]{:S(2)}) copy-start(f32[8,768]{1,0:T(8,128)} %get-tuple-element.106) | copy-start | bytes 73732
  209.6 32.1 %collective-permute-start.10 = (bf16[2,768,384]{2,1,0:T(8,128)(2,1)}, bf16[2,768,384]{2,1,0:T(8,128)(2,1)}, u32[]{:S(2)}, u32[]{:S(2)}) collective-permute-start(bf16[2,768,384]{2,1,0:T(8,128)(2,1)} %fusion.2), channel_id=1, source_target_pairs={{0,4},{4,0},{8,12},{12,8},{16,20},{20,16},{24,28},{28,24},{1,5},{5... | collective-permute-start | bytes 3538952 | tf_op jit(solution)/shard_map/ppermute | solution.py:692
  209.6 32.1 %collective-permute-start.11 = (bf16[2,768,384]{2,1,0:T(8,128)(2,1)}, bf16[2,768,384]{2,1,0:T(8,128)(2,1)}, u32[]{:S(2)}, u32[]{:S(2)}) collective-permute-start(bf16[2,768,384]{2,1,0:T(8,128)(2,1)} %fusion.3), channel_id=1, source_target_pairs={{0,2},{1,3},{2,0},{3,1},{4,6},{5,7},{6,4},{7,5},{8,10},{9,11},{10,... | collective-permute-start | bytes 3538952 | tf_op jit(solution)/shard_map/ppermute | solution.py:692
  397.8 5.0 %copy-start.2 = (f32[1024,768]{1,0:T(8,128)S(1)}, f32[1024,768]{1,0:T(8,128)}, u32[]{:S(2)}) copy-start(f32[1024,768]{1,0:T(8,128)} %get-tuple-element.109) | copy-start | bytes 9437188
  402.8 1.7 copy-start.1
